TPU v7x, 32 devices: a whole 2x2x4 slice. The times are simulated.
32 devices in a mesh: dp: 8 (over y, x, core), shard: 4 (over z).
Axes of the slice: x: 2, y: 2, z: 4, core: 2. Of those that a mesh axis runs over, the one named last changes fastest.
Arguments:
- hidden_in: float32 [16384, 1536], P(('dp', 'shard')), may hold values from -6 to 6
- cotangent: float32 [16384, 1536], P(('dp', 'shard')), may hold values from -6 to 6
- segment_ids: int32 [16384], P(('dp', 'shard')), may hold values from 0 to 31, as said below
- param_prenorm: float32 [1536], replicated, may hold values from 0.5 to 1.5
- param_inputs: float32 [1536, 6448], P(('dp', 'shard')), may hold values from -0.15625 to 0.15625
- param_kernel: float32 [4, 3328], replicated, may hold values from -3 to 3
- param_offsets: float32 [3328], replicated, may hold values from -0.5 to 0.5
- param_timestep: float32 [48], replicated, may hold values from -7 to -3
- param_decays: float32 [48], replicated, may hold values from 0 to 2.5
- param_direct: float32 [48], replicated, may hold values from 0.5 to 1.5
- param_gating: float32 [3072], replicated, may hold values from 0.5 to 1.5
- param_outputs: float32 [3072, 1536], P(('dp', 'shard')), may hold values from -0.15625 to 0.15625
- moment_prenorm: float32 [1536], replicated, may hold values from -3 to 3
- moment_inputs: float32 [1536, 6448], P(('dp', 'shard')), may hold values from -3 to 3
- moment_kernel: float32 [4, 3328], replicated, may hold values from -3 to 3
- moment_offsets: float32 [3328], replicated, may hold values from -3 to 3
- moment_timestep: float32 [48], replicated, may hold values from -3 to 3
- moment_decays: float32 [48], replicated, may hold values from -3 to 3
- moment_direct: float32 [48], replicated, may hold values from -3 to 3
- moment_gating: float32 [3072], replicated, may hold values from -3 to 3
- moment_outputs: float32 [3072, 1536], P(('dp', 'shard')), may hold values from -3 to 3
- square_prenorm: float32 [1536], replicated, may hold values from 0.01 to 1
- square_inputs: float32 [1536, 6448], P(('dp', 'shard')), may hold values from 0.01 to 1
- square_kernel: float32 [4, 3328], replicated, may hold values from 0.01 to 1
- square_offsets: float32 [3328], replicated, may hold values from 0.01 to 1
- square_timestep: float32 [48], replicated, may hold values from 0.01 to 1
- square_decays: float32 [48], replicated, may hold values from 0.01 to 1
- square_direct: float32 [48], replicated, may hold values from 128 to 8192
- square_gating: float32 [3072], replicated, may hold values from 0.01 to 1
- square_outputs: float32 [3072, 1536], P(('dp', 'shard')), may hold values from 0.01 to 1
Outputs:
- block_out: float32 [16384, 1536], P(('dp', 'shard'))
- hidden_grad: float32 [16384, 1536], P(('dp', 'shard'))
- grad_prenorm: float32 [1536], replicated
- grad_inputs: float32 [1536, 6448], P(('dp', 'shard'))
- grad_kernel: float32 [4, 3328], replicated
- grad_offsets: float32 [3328], replicated
- grad_timestep: float32 [48], replicated
- grad_decays: float32 [48], replicated
- grad_direct: float32 [48], replicated
- grad_gating: float32 [3072], replicated
- grad_outputs: float32 [3072, 1536], P(('dp', 'shard'))
- newparam_prenorm: float32 [1536], replicated
- newparam_inputs: float32 [1536, 6448], P(('dp', 'shard'))
- newparam_kernel: float32 [4, 3328], replicated
- newparam_offsets: float32 [3328], replicated
- newparam_timestep: float32 [48], replicated
- newparam_decays: float32 [48], replicated
- newparam_direct: float32 [48], replicated
- newparam_gating: float32 [3072], replicated
- newparam_outputs: float32 [3072, 1536], P(('dp', 'shard'))
- newmoment_prenorm: float32 [1536], replicated
- newmoment_inputs: float32 [1536, 6448], P(('dp', 'shard'))
- newmoment_kernel: float32 [4, 3328], replicated
- newmoment_offsets: float32 [3328], replicated
- newmoment_timestep: float32 [48], replicated
- newmoment_decays: float32 [48], replicated
- newmoment_direct: float32 [48], replicated
- newmoment_gating: float32 [3072], replicated
- newmoment_outputs: float32 [3072, 1536], P(('dp', 'shard'))
- newsquare_prenorm: float32 [1536], replicated
- newsquare_inputs: float32 [1536, 6448], P(('dp', 'shard'))
- newsquare_kernel: float32 [4, 3328], replicated
- newsquare_offsets: float32 [3328], replicated
- newsquare_timestep: float32 [48], replicated
- newsquare_decays: float32 [48], replicated
- newsquare_direct: float32 [48], replicated
- newsquare_gating: float32 [3072], replicated
- newsquare_outputs: float32 [3072, 1536], P(('dp', 'shard'))
Inputs may be any that keep to these rules, and one draw needn't show every extreme that they name: `segment_ids`: segment ids never fall along the tokens, begin at 0, and each packed sequence of 2048 tokens holds exactly 4 documents of its own, each of at least 204 tokens, so that no document crosses from one packed sequence into the next.
All inputs are finite; a program needn't handle non-finite values.
Results may differ from a plain program's by a relative error of at most 0.0055.
The roundings to bfloat16 on the way count: a program that leaves them out, or rounds other values in their place, can miss the bound.
Values may be sent and summed in bfloat16 or wider, within the bound.
No kernel may reach another device: no remote copies, remote signals or barrier semaphores. Data moves between devices by JAX's collectives and lax.ppermute only.
A program may use at most 320 MiB of HBM per device.

v0:
```python
import jax
import jax.numpy as jnp
from jax import lax
from jax.sharding import PartitionSpec as P

HEADS = 48
HEAD_DIM = 64
STATE = 128
KW = 4
BLOCK = 256
ADAM_STEP = 10
DI = 3072
CH = 3328


norm_eps = 1e-05
beta_one = 0.9
beta_two = 0.95
adam_eps = 1e-08
highest = lax.Precision.HIGHEST
rate_table = (0.2, 0.01, 0.2, 0.2, 0.2, 0.2, 0.2, 0.2, 0.01)
shrink_table = (0.0, 0.1, 0.1, 0.0, 0.0, 0.0, 0.0, 0.0, 0.1)


def shifted(value, axis, by):
    count = lax.axis_size(axis)
    pairs = [(i, i + by) for i in range(count) if 0 <= i + by < count]
    return lax.ppermute(value, axis, pairs)


def prefix(value, axis, combine, identity, reverse):
    count, here = (lax.axis_size(axis), lax.axis_index(axis))
    everything = jax.tree.map(lambda part: lax.all_gather(part, axis), value)
    start = jax.tree.map(
        lambda part, zero: jnp.broadcast_to(jnp.asarray(zero, part.dtype), part.shape),
        value,
        identity,
    )

    def turn(k, before):
        at = count - 1 - k if reverse else k
        reached = at > here if reverse else at < here
        new = combine(before, jax.tree.map(lambda part: part[at], everything))
        return jax.tree.map(lambda a, b: jnp.where(reached, a, b), new, before)

    return lax.fori_loop(0, count, turn, start)


def pre_norm(hidden, norm_gain):
    inv_rms = lax.rsqrt(jnp.mean(hidden * hidden, axis=1, keepdims=True) + norm_eps)
    return hidden * inv_rms * norm_gain


def gated_norm(output, gate_in, gating):
    gated_rows = output * jax.nn.silu(gate_in)
    inv_rms = lax.rsqrt(jnp.mean(gated_rows * gated_rows, axis=1, keepdims=True) + norm_eps)
    return gated_rows * inv_rms * gating


def conv_mix(conv_in, rim_rows, seg_float, rim_segs, kernel, offsets):
    rim_count = rim_rows.shape[0]
    length = conv_in.shape[0]
    padded = jnp.concatenate([rim_rows, conv_in], axis=0)
    all_segs = jnp.concatenate([rim_segs, seg_float], axis=0)
    summed = jnp.zeros_like(conv_in) + offsets[None, :]
    for tap_index in range(rim_count + 1):
        matches = (all_segs[tap_index : tap_index + length] == seg_float).astype(jnp.float32)
        summed = (
            summed
            + kernel[tap_index][None, :] * padded[tap_index : tap_index + length] * matches[:, None]
        )
    return jax.nn.silu(summed)


def block_step(carried, pieces):
    values, keys_mat, query_mat, deltas, log_decay, seg_float, starts = pieces
    cumulative = jnp.cumsum(log_decay, axis=0)
    count_rows = values.shape[0]
    position = jnp.arange(count_rows)
    allowed = (seg_float[:, None] == seg_float[None, :]) & (position[:, None] >= position[None, :])
    allowed_cube = allowed[:, :, None]
    log_gaps = jnp.where(allowed_cube, cumulative[:, None, :] - cumulative[None, :, :], 0.0)
    decay_mat = jnp.where(allowed_cube, jnp.exp(log_gaps), 0.0)
    scores = jnp.dot(query_mat, keys_mat.T, precision=highest)
    mixing = scores[:, :, None] * decay_mat * deltas[None, :, :]
    local_out = jnp.einsum("tsh,shp->thp", mixing, values, precision=highest)
    alive_mask = (seg_float == seg_float[0]).astype(jnp.float32) * (1.0 - starts[0])
    inflow = jnp.exp(cumulative) * alive_mask[:, None]
    carry_out = (
        jnp.einsum("tn,hpn->thp", query_mat, carried, precision=highest) * inflow[:, :, None]
    )
    ending = (seg_float == seg_float[count_rows - 1]).astype(jnp.float32)
    tail_weight = (
        jnp.exp(cumulative[count_rows - 1][None, :] - cumulative) * ending[:, None] * deltas
    )
    weighted = values * tail_weight[:, :, None]
    fresh_state = jnp.einsum("shp,sn->hpn", weighted, keys_mat, precision=highest)
    keep_factor = jnp.exp(cumulative[count_rows - 1]) * alive_mask[count_rows - 1]
    carried_new = carried * keep_factor[:, None, None] + fresh_state
    return (carried_new, local_out + carry_out)


def scan_blocks(values, keys_mat, query_mat, deltas, log_decay, seg_float, starts, initial):
    block_count = values.shape[0] // BLOCK

    def shaped(array):
        return array.reshape((block_count, BLOCK) + array.shape[1:])

    pieces = (
        shaped(values),
        shaped(keys_mat),
        shaped(query_mat),
        shaped(deltas),
        shaped(log_decay),
        shaped(seg_float),
        shaped(starts),
    )
    final_state, block_outs = lax.scan(jax.checkpoint(block_step), initial, pieces)
    return (final_state, block_outs.reshape(values.shape))


def compose(earlier, later_pair):
    return (later_pair[0] * earlier[0], later_pair[0][:, None, None] * earlier[1] + later_pair[1])


def adamw(param, grad, moment, square, rate, shrink):
    moment_new = beta_one * moment + (1.0 - beta_one) * grad
    square_new = beta_two * square + (1.0 - beta_two) * grad * grad
    first_corr = 1.0 - beta_one**ADAM_STEP
    second_corr = 1.0 - beta_two**ADAM_STEP
    update = moment_new / first_corr / (jnp.sqrt(square_new / second_corr) + adam_eps)
    return (param - rate * (update + shrink * param), moment_new, square_new)


def shards(
    hidden_in,
    cotangent,
    segment_ids,
    param_prenorm,
    param_inputs,
    param_kernel,
    param_offsets,
    param_timestep,
    param_decays,
    param_direct,
    param_gating,
    param_outputs,
    moment_prenorm,
    moment_inputs,
    moment_kernel,
    moment_offsets,
    moment_timestep,
    moment_decays,
    moment_direct,
    moment_gating,
    moment_outputs,
    square_prenorm,
    square_inputs,
    square_kernel,
    square_offsets,
    square_timestep,
    square_decays,
    square_direct,
    square_gating,
    square_outputs,
):
    own_inputs = param_inputs.astype(jnp.bfloat16)
    own_outputs = param_outputs.astype(jnp.bfloat16)
    grouped_in, grouped_out = (
        lax.all_gather(own_inputs, "shard", axis=0, tiled=True),
        lax.all_gather(own_outputs, "shard", axis=0, tiled=True),
    )
    input_half, output_half = (
        lax.all_gather(grouped_in, "dp", axis=0, tiled=True),
        lax.all_gather(grouped_out, "dp", axis=0, tiled=True),
    )
    length = hidden_in.shape[0]
    rim_count = KW - 1
    normed, norm_back = jax.vjp(pre_norm, hidden_in, param_prenorm)
    normed_half = normed.astype(jnp.bfloat16)
    projected = jnp.dot(normed_half, input_half, preferred_element_type=jnp.float32)
    seg_float = segment_ids.astype(jnp.float32)
    rim_rows, rim_received = shifted(
        (projected[length - rim_count :, DI : DI + CH], seg_float[length - rim_count :]), "shard", 1
    )
    rim_segs = jnp.where(lax.axis_index("shard") == 0, -1.0, rim_received)
    previous = jnp.concatenate([rim_segs[rim_count - 1 :], seg_float[:-1]])
    starts = (seg_float != previous).astype(jnp.float32)
    gate_in = projected[:, :DI]
    rest_cols = projected[:, DI:]

    def first_piece(rest_in, rim_in, small_params):
        kernel, offsets, timestep, decays = small_params
        mixed = conv_mix(rest_in[:, :CH], rim_in, seg_float, rim_segs, kernel, offsets)
        values = mixed[:, :DI].reshape(length, HEADS, HEAD_DIM)
        keys_mat = mixed[:, DI : DI + STATE]
        query_mat = mixed[:, DI + STATE :]
        deltas = jax.nn.softplus(rest_in[:, CH:] + timestep)
        log_decay = -deltas * jnp.exp(decays)
        initial = jnp.zeros((HEADS, HEAD_DIM, STATE), jnp.float32)
        local_state, local_out = scan_blocks(
            values, keys_mat, query_mat, deltas, log_decay, seg_float, starts, initial
        )
        alive_mask = (seg_float == seg_float[0]).astype(jnp.float32) * (1.0 - starts[0])
        inflow = jnp.exp(jnp.cumsum(log_decay, axis=0)) * alive_mask[:, None]
        return (local_out, local_state, inflow[length - 1], inflow, values, query_mat)

    first_results, first_back = jax.vjp(
        first_piece,
        rest_cols,
        rim_rows,
        (param_kernel, param_offsets, param_timestep, param_decays),
    )
    local_out, local_state, factor, inflow, values, query_mat = first_results
    identity_pair = (jnp.ones_like(factor), jnp.zeros_like(local_state))
    scanned_factor, incoming = prefix((factor, local_state), "shard", compose, identity_pair, False)

    def second_piece(
        local_in, incoming_in, inflow_in, values_in, query_in, gate_cols, direct, gating
    ):
        carry_out = (
            jnp.einsum("tn,hpn->thp", query_in, incoming_in, precision=highest)
            * inflow_in[:, :, None]
        )
        mixer_out = local_in + carry_out + direct[None, :, None] * values_in
        return gated_norm(mixer_out.reshape(length, DI), gate_cols, gating)

    gated_full, second_back = jax.vjp(
        second_piece,
        local_out,
        incoming,
        inflow,
        values,
        query_mat,
        gate_in,
        param_direct,
        param_gating,
    )
    gated_half = gated_full.astype(jnp.bfloat16)
    block_out = hidden_in + jnp.dot(gated_half, output_half, preferred_element_type=jnp.float32)
    upstream_half = cotangent.astype(jnp.bfloat16)
    back_gated = jnp.dot(upstream_half, output_half.T, preferred_element_type=jnp.float32)
    grad_out_local = jnp.dot(gated_half.T, upstream_half, preferred_element_type=jnp.float32)
    (
        back_local,
        back_incoming,
        back_inflow,
        back_values,
        back_query,
        back_gate,
        grad_direct_local,
        grad_gating_local,
    ) = second_back(back_gated)
    identity_back = (jnp.ones_like(factor), jnp.zeros_like(back_incoming))
    reversed_factor, back_outgoing = prefix(
        (factor, back_incoming), "shard", compose, identity_back, True
    )
    back_factor = jnp.sum(back_outgoing * incoming, axis=(1, 2))
    back_rest, back_rim, back_small = first_back(
        (back_local, back_outgoing, back_factor, back_inflow, back_values, back_query)
    )
    rim_grad = shifted(back_rim, "shard", -1)
    back_rest = back_rest.at[length - rim_count :, :CH].add(rim_grad)
    back_projected = jnp.concatenate([back_gate, back_rest], axis=1)
    back_half = back_projected.astype(jnp.bfloat16)
    back_normed = jnp.dot(back_half, input_half.T, preferred_element_type=jnp.float32)
    grad_in_local = jnp.dot(normed_half.T, back_half, preferred_element_type=jnp.float32)
    back_hidden, grad_prenorm_local = norm_back(back_normed)
    hidden_grad = cotangent + back_hidden
    part_in, part_out = (
        lax.psum_scatter(grad_in_local, "dp", scatter_dimension=0, tiled=True),
        lax.psum_scatter(grad_out_local, "dp", scatter_dimension=0, tiled=True),
    )
    grad_inputs, grad_outputs = (
        lax.psum_scatter(part_in, "shard", scatter_dimension=0, tiled=True),
        lax.psum_scatter(part_out, "shard", scatter_dimension=0, tiled=True),
    )
    (
        grad_prenorm,
        grad_kernel,
        grad_offsets,
        grad_timestep,
        grad_decays,
        grad_direct,
        grad_gating,
    ) = lax.psum(
        (
            grad_prenorm_local,
            back_small[0],
            back_small[1],
            back_small[2],
            back_small[3],
            grad_direct_local,
            grad_gating_local,
        ),
        ("dp", "shard"),
    )
    params = (
        param_prenorm,
        param_inputs,
        param_kernel,
        param_offsets,
        param_timestep,
        param_decays,
        param_direct,
        param_gating,
        param_outputs,
    )
    moments = (
        moment_prenorm,
        moment_inputs,
        moment_kernel,
        moment_offsets,
        moment_timestep,
        moment_decays,
        moment_direct,
        moment_gating,
        moment_outputs,
    )
    squares = (
        square_prenorm,
        square_inputs,
        square_kernel,
        square_offsets,
        square_timestep,
        square_decays,
        square_direct,
        square_gating,
        square_outputs,
    )
    grads = (
        grad_prenorm,
        grad_inputs,
        grad_kernel,
        grad_offsets,
        grad_timestep,
        grad_decays,
        grad_direct,
        grad_gating,
        grad_outputs,
    )
    updated = [
        adamw(
            params[member_index],
            grads[member_index],
            moments[member_index],
            squares[member_index],
            rate_table[member_index],
            shrink_table[member_index],
        )
        for member_index in range(9)
    ]
    return (
        block_out,
        hidden_grad,
        grads[0],
        grads[1],
        grads[2],
        grads[3],
        grads[4],
        grads[5],
        grads[6],
        grads[7],
        grads[8],
        updated[0][0],
        updated[1][0],
        updated[2][0],
        updated[3][0],
        updated[4][0],
        updated[5][0],
        updated[6][0],
        updated[7][0],
        updated[8][0],
        updated[0][1],
        updated[1][1],
        updated[2][1],
        updated[3][1],
        updated[4][1],
        updated[5][1],
        updated[6][1],
        updated[7][1],
        updated[8][1],
        updated[0][2],
        updated[1][2],
        updated[2][2],
        updated[3][2],
        updated[4][2],
        updated[5][2],
        updated[6][2],
        updated[7][2],
        updated[8][2],
    )


def solution(mesh):
    placed = (
        P(("dp", "shard"), None),
        P(("dp", "shard"), None),
        P(("dp", "shard")),
        P(),
        P(("dp", "shard"), None),
        P(),
        P(),
        P(),
        P(),
        P(),
        P(),
        P(("dp", "shard"), None),
        P(),
        P(("dp", "shard"), None),
        P(),
        P(),
        P(),
        P(),
        P(),
        P(),
        P(("dp", "shard"), None),
        P(),
        P(("dp", "shard"), None),
        P(),
        P(),
        P(),
        P(),
        P(),
        P(),
        P(("dp", "shard"), None),
    )
    return jax.shard_map(
        shards,
        mesh=mesh,
        in_specs=placed,
        out_specs=(
            P(("dp", "shard"), None),
            P(("dp", "shard"), None),
            P(),
            P(("dp", "shard"), None),
            P(),
            P(),
            P(),
            P(),
            P(),
            P(),
            P(("dp", "shard"), None),
            P(),
            P(("dp", "shard"), None),
            P(),
            P(),
            P(),
            P(),
            P(),
            P(),
            P(("dp", "shard"), None),
            P(),
            P(("dp", "shard"), None),
            P(),
            P(),
            P(),
            P(),
            P(),
            P(),
            P(("dp", "shard"), None),
            P(),
            P(("dp", "shard"), None),
            P(),
            P(),
            P(),
            P(),
            P(),
            P(),
            P(("dp", "shard"), None),
        ),
        check_vma=False,
    )
```

profile of v0, /device:TPU:0, one launch (start us, length us, event | category | flops | bytes accessed | tf_op | source)
XLA Modules:
  0.0 2065.3 jit_solution(9091797902545524931)
XLA Ops:
  9.6 56.2 %all-gather.10.cloned.1.call-done = bf16[192,6448]{1,0:T(8,128)(2,1)} async-done(((bf16[48,6448]{1,0:T(8,128)(2,1)}), bf16[192,6448]{1,0:T(8,128)(2,1)}) %all-gather.10.cloned.1.call-update) | async-done | bytes 2476048 | tf_op jit(solution)/shard_map/all_gather | solution.py:170
  74.6 95.4 %all-gather.12.cloned.1.call-done = bf16[1536,6448]{1,0:T(8,128)(2,1)} async-done(((bf16[192,6448]{1,0:T(8,128)(2,1)}), bf16[1536,6448]{1,0:T(8,128)(2,1)}) %all-gather.12.cloned.1.call-update) | async-done | bytes 19808272 | tf_op jit(solution)/shard_map/all_gather | solution.py:174
  170.0 18.7 fusion.156
  205.9 20.1 fusion.100
  252.5 211.2 %while.73 = (s32[]{:T(128)}, f32[48,64,128]{2,1,0:T(8,128)S(1)}, f32[2,256,48,64]{1,0,3,2:T(2,128)}, f32[2,48,64,128]{3,2,1,0:T(8,128)}, f32[2,256,48]{1,2,0:T(8...) while((s32[]{:T(128)}, f32[48,64,128]{2,1,0:T(8,128)S(1)}, ...), condition=%wide.region_4.5_spmd.clone, body=%wide.region_1.4_spmd.clone.sunk | while | flops 4954387456 | bytes 38305860 | solution.py:118
  294.7 63.5 %dynamic_update_slice.80 = f32[2,256,48,64]{1,0,3,2:T(2,128)} dynamic-update-slice(f32[2,256,48,64]{1,0,3,2:T(2,128)} %get-tuple-element.1501, f32[1,256,48,64]{1,0,3,2:T(1,128)} %copy.485, s32[]{:T(128)S(6)} %copy.497, s32[]{:T(128)} %constant.325.clone.1..sunk.1, s32[]{:T(128)} %constant.325.clone.1..sunk.1, s32[]{:T(128)} %constant.325.clone.1..sunk.1) | dynamic-update-slice | bytes 6291460 | tf_op jit(solution)/shard_map/jvp()/while/body/jit(dynamic_update_index_in_dim)/dynamic_update_slice | solution.py:118
  400.1 63.5 %dynamic_update_slice.80 = f32[2,256,48,64]{1,0,3,2:T(2,128)} dynamic-update-slice(f32[2,256,48,64]{1,0,3,2:T(2,128)} %get-tuple-element.1501, f32[1,256,48,64]{1,0,3,2:T(1,128)} %copy.485, s32[]{:T(128)S(6)} %copy.497, s32[]{:T(128)} %constant.325.clone.1..sunk.1, s32[]{:T(128)} %constant.325.clone.1..sunk.1, s32[]{:T(128)} %constant.325.clone.1..sunk.1) | dynamic-update-slice | bytes 6291460 | tf_op jit(solution)/shard_map/jvp()/while/body/jit(dynamic_update_index_in_dim)/dynamic_update_slice | solution.py:118
  488.1 90.8 %all-gather.18.cloned.1.call-done = f32[192,64,128]{2,1,0:T(8,128)} async-done(((f32[48,64,128]{2,1,0:T(8,128)}), f32[192,64,128]{2,1,0:T(8,128)}) %all-gather.18.cloned.1.call-update) | async-done | bytes 6291472 | tf_op jit(solution)/shard_map/all_gather | solution.py:33
  624.5 124.7 %reduce-scatter.9.cloned.1.call-done = f32[384,1536]{1,0:T(8,128)} async-done(((f32[3072,1536]{1,0:T(8,128)}), f32[384,1536]{1,0:T(8,128)}) %reduce-scatter.9.cloned.1.call-update) | async-done | bytes 2359312 | tf_op jit(solution)/shard_map/reduce_scatter | solution.py:272
  749.3 50.4 %reduce-scatter.11.cloned.1.call-done = f32[96,1536]{1,0:T(8,128)} async-done(((f32[384,1536]{1,0:T(8,128)}), f32[96,1536]{1,0:T(8,128)}) %reduce-scatter.11.cloned.1.call-update) | async-done | bytes 589840 | tf_op jit(solution)/shard_map/reduce_scatter | solution.py:276
  802.4 29.7 %all-gather.14.cloned.1.call-done = bf16[384,1536]{1,0:T(8,128)(2,1)} async-done(((bf16[96,1536]{1,0:T(8,128)(2,1)}), bf16[384,1536]{1,0:T(8,128)(2,1)}) %all-gather.14.cloned.1.call-update) | async-done | bytes 1179664 | tf_op jit(solution)/shard_map/all_gather | solution.py:171
  832.2 59.8 %all-gather.16.cloned.1.call-done = bf16[3072,1536]{1,0:T(8,128)(2,1)} async-done(((bf16[384,1536]{1,0:T(8,128)(2,1)}), bf16[3072,1536]{1,0:T(8,128)(2,1)}) %all-gather.16.cloned.1.call-update) | async-done | bytes 9437200 | tf_op jit(solution)/shard_map/all_gather | solution.py:175
  943.3 98.7 %all-gather.20.cloned.1.call-done = f32[192,64,128]{2,1,0:T(8,128)} async-done(((f32[48,64,128]{2,1,0:T(8,128)}), f32[192,64,128]{2,1,0:T(8,128)}) %all-gather.20.cloned.1.call-update) | async-done | bytes 6291472 | tf_op jit(solution)/shard_map/all_gather | solution.py:33
  1065.6 394.9 %while.72 = (s32[]{:T(128)}, f32[48,64,128]{2,1,0:T(8,128)}, f32[2,256,48,64]{1,0,3,2:T(2,128)}, f32[2,256,128]{2,1,0:T(8,128)}, f32[2,256,128]{2,1,0:T(8,128)},...) while((s32[]{:T(128)}, f32[48,64,128]{2,1,0:T(8,128)}, ...), condition=%wide.region_26.27_spmd, body=%wide.region_13.26_spmd.sunk | while | flops 11248780288 | bytes 130828264 | solution.py:118
  1092.0 22.6 %fusion.259 = (f32[256,48]{0,1:T(8,128)}, f32[256,48]{0,1:T(8,128)}, f32[256,48]{0,1:T(8,128)}, f32[256,256]{1,0:T(8,128)}) fusion(f32[256,48]{0,1:T(8,128)} %copy.468, f32[256,48]{0,1:T(8,128)} %copy.470, f32[256,256]{1,0:T(8,128)S(1)} %fusion.257, pred[256,256]{1,0:T(8,128)(4,1)S(1)} %fusion.258, f32[256,48,64]{0,2,1:T(8,128)} %get-tuple-element.1442, ...), kind=kOutput, calls=%fused_computation.18.clone.1 | convolution fusion | flops 2463002624 | bytes 7127040 | tf_op jit(solution)/shard_map/transpose(jvp())/while/body/eval_jaxpr/checkpoint/tsh,shp->thp/dot_general | solution.py:86
  1177.5 63.5 %dynamic_update_slice.77 = f32[2,256,48,64]{1,0,3,2:T(2,128)} dynamic-update-slice(f32[2,256,48,64]{1,0,3,2:T(2,128)} %get-tuple-element.1599, f32[1,256,48,64]{1,0,3,2:T(1,128)} %copy.477, s32[]{:T(128)S(6)} %sub.334, s32[]{:T(128)} %constant.325.clone.1..sunk, s32[]{:T(128)} %constant.325.clone.1..sunk, s32[]{:T(128)} %constant.325.clone.1..sunk) | dynamic-update-slice | bytes 6291460 | tf_op jit(solution)/shard_map/transpose(jvp())/while/body/jit(dynamic_update_index_in_dim)/dynamic_update_slice | solution.py:118
  1285.9 22.8 %fusion.259 = (f32[256,48]{0,1:T(8,128)}, f32[256,48]{0,1:T(8,128)}, f32[256,48]{0,1:T(8,128)}, f32[256,256]{1,0:T(8,128)}) fusion(f32[256,48]{0,1:T(8,128)} %copy.468, f32[256,48]{0,1:T(8,128)} %copy.470, f32[256,256]{1,0:T(8,128)S(1)} %fusion.257, pred[256,256]{1,0:T(8,128)(4,1)S(1)} %fusion.258, f32[256,48,64]{0,2,1:T(8,128)} %get-tuple-element.1442, ...), kind=kOutput, calls=%fused_computation.18.clone.1 | convolution fusion | flops 2463002624 | bytes 7127040 | tf_op jit(solution)/shard_map/transpose(jvp())/while/body/eval_jaxpr/checkpoint/tsh,shp->thp/dot_general | solution.py:86
  1371.4 63.5 %dynamic_update_slice.77 = f32[2,256,48,64]{1,0,3,2:T(2,128)} dynamic-update-slice(f32[2,256,48,64]{1,0,3,2:T(2,128)} %get-tuple-element.1599, f32[1,256,48,64]{1,0,3,2:T(1,128)} %copy.477, s32[]{:T(128)S(6)} %sub.334, s32[]{:T(128)} %constant.325.clone.1..sunk, s32[]{:T(128)} %constant.325.clone.1..sunk, s32[]{:T(128)} %constant.325.clone.1..sunk) | dynamic-update-slice | bytes 6291460 | tf_op jit(solution)/shard_map/transpose(jvp())/while/body/jit(dynamic_update_index_in_dim)/dynamic_update_slice | solution.py:118
  1482.7 19.7 fusion.157
  1564.8 20.4 fusion.109
  1587.9 19.5 multiply_reduce_fusion.13
  1607.5 214.3 %reduce-scatter.5.cloned.1.call-done = f32[192,6448]{1,0:T(8,128)} async-done(((f32[1536,6448]{1,0:T(8,128)}), f32[192,6448]{1,0:T(8,128)}) %reduce-scatter.5.cloned.1.call-update) | async-done | bytes 4952080 | tf_op jit(solution)/shard_map/reduce_scatter | solution.py:271
  1836.2 119.3 %all-reduce.19.cloned.1.call-done = (f32[1536]{0:T(1024)}, f32[4,3328]{1,0:T(4,128)}, f32[3328]{0:T(1024)}, f32[48]{0:T(128)}, f32[48]{0:T(128)}, /*index=5*/f32[48]{0:T(128)}, f32[3072]{0:T(1024)}) async-done(((f32[1536]{0:T(1024)}, f32[4,3328]{1,0:T(4,128)}, f32[3328]{0:T(1024)}, f32[48]{0:T(128)}, f32[48]{0:T(128)}, /*index=5*/f32[48]{0:T(128)}, f32[3072]{0:T(1024)}), (f32[1536]{0:T(1024)}, ...) | async-done | bytes 85584 | tf_op jit(solution)/shard_map/psum | solution.py:286
  1963.6 85.8 %reduce-scatter.7.cloned.1.call-done = f32[48,6448]{1,0:T(8,128)} async-done(((f32[192,6448]{1,0:T(8,128)}), f32[48,6448]{1,0:T(8,128)}) %reduce-scatter.7.cloned.1.call-update) | async-done | bytes 1238032 | tf_op jit(solution)/shard_map/reduce_scatter | solution.py:275
  (560 shorter events, 635.7 us)
Async XLA Ops:
  7.2 162.7 %copy-start.69 = (f32[1536]{0:T(1024)S(1)}, f32[1536]{0:T(1024)}, u32[]{:S(2)}) copy-start(f32[1536]{0:T(1024)} %param.43) | copy-start | bytes 18436
  7.2 58.6 %all-gather.10.cloned.1.call-start = ((), (), s32[]{:S(2)}) async-start(), calls=%async_computation.4 | async-start | bytes 3133440 | tf_op jit(solution)/shard_map/all_gather | solution.py:170
  9.5 160.5 %all-gather.12.cloned.1.call-start = ((), (), s32[]{:S(2)}) async-start(), calls=%async_computation.5 | async-start | bytes 22560768 | tf_op jit(solution)/shard_map/all_gather | solution.py:174
  65.8 513.1 %all-gather.18.cloned.1.call-start = ((), (), s32[]{:S(2)}) async-start(), calls=%async_computation.12 | async-start | bytes 7864320 | tf_op jit(solution)/shard_map/all_gather | solution.py:33
  66.6 5.4 collective-permute-start
  191.2 13.3 collective-permute-start.1
  252.5 215.5 %copy-start.79 = (s32[512]{0:T(512)S(1)}, s32[512]{0:T(512)}, u32[]{:S(2)}) copy-start(s32[512]{0:T(512)} %param.42) | copy-start | bytes 6148
  464.9 284.3 %reduce-scatter.9.cloned.1.call-start = ((), (), s32[]{:S(2)}) async-start(), calls=%async_computation.10 | async-start | bytes 21233664 | tf_op jit(solution)/shard_map/reduce_scatter | solution.py:272
  470.3 446.4 %copy-start.19 = (f32[512,48]{0,1:T(8,128)}, f32[512,48]{0,1:T(8,128)S(1)}, u32[]{:S(2)}) copy-start(f32[512,48]{0,1:T(8,128)S(1)} %fusion.137) | copy-start | bytes 294916
  586.1 468.6 %copy-start.4 = (f32[48,64,128]{2,1,0:T(8,128)}, f32[48,64,128]{2,1,0:T(8,128)S(1)}, u32[]{:S(2)}) copy-start(f32[48,64,128]{2,1,0:T(8,128)S(1)} %get-tuple-element.741) | copy-start | bytes 4718596
  612.3 291.9 %copy-start.51 = (f32[512]{0:T(512)}, f32[512]{0:T(512)S(1)}, u32[]{:S(2)}) copy-start(f32[512]{0:T(512)S(1)} %fusion.148) | copy-start | bytes 6148
  624.4 175.2 %copy-start.32 = (f32[96,1536]{1,0:T(8,128)S(1)}, f32[96,1536]{1,0:T(8,128)}, u32[]{:S(2)}) copy-start(f32[96,1536]{1,0:T(8,128)} %param.51) | copy-start | bytes 1769476
  624.4 175.2 %copy-start.33 = (f32[96,1536]{1,0:T(8,128)S(1)}, f32[96,1536]{1,0:T(8,128)}, u32[]{:S(2)}) copy-start(f32[96,1536]{1,0:T(8,128)} %param.60) | copy-start | bytes 1769476
  624.4 175.2 %copy-start.34 = (f32[96,1536]{1,0:T(8,128)S(1)}, f32[96,1536]{1,0:T(8,128)}, u32[]{:S(2)}) copy-start(f32[96,1536]{1,0:T(8,128)} %param.69) | copy-start | bytes 1769476
  624.4 175.2 %reduce-scatter.11.cloned.1.call-start = ((), (), s32[]{:S(2)}) async-start(), calls=%async_computation.11 | async-start | bytes 2949120 | tf_op jit(solution)/shard_map/reduce_scatter | solution.py:276
  749.2 82.9 %all-gather.14.cloned.1.call-start = ((), (), s32[]{:S(2)}) async-start(), calls=%async_computation.6 | async-start | bytes 1474560 | tf_op jit(solution)/shard_map/all_gather | solution.py:171
  802.3 89.6 %all-gather.16.cloned.1.call-start = ((), (), s32[]{:S(2)}) async-start(), calls=%async_computation.7 | async-start | bytes 10616832 | tf_op jit(solution)/shard_map/all_gather | solution.py:175
  832.2 209.9 %all-gather.20.cloned.1.call-start = ((), (), s32[]{:S(2)}) async-start(), calls=%async_computation.13 | async-start | bytes 7864320 | tf_op jit(solution)/shard_map/all_gather | solution.py:33
  926.6 895.2 %reduce-scatter.5.cloned.1.call-start = ((), (), s32[]{:S(2)}) async-start(), calls=%async_computation.8 | async-start | bytes 45121536 | tf_op jit(solution)/shard_map/reduce_scatter | solution.py:271
  1541.0 8.1 collective-permute-start.2
  1585.2 370.3 %all-reduce.19.cloned.1.call-start = ((), (), s32[]{:S(2)}) async-start(), calls=%async_computation.14 | async-start | bytes 183296 | tf_op jit(solution)/shard_map/psum | solution.py:286
  1587.9 233.9 %copy-start.36 = (f32[3072]{0:T(1024)S(1)}, f32[3072]{0:T(1024)}, u32[]{:S(2)}) copy-start(f32[3072]{0:T(1024)} %param.50) | copy-start | bytes 36868
  1587.9 233.9 %copy-start.52 = (f32[512]{0:T(512)S(1)}, f32[512]{0:T(512)}, u32[]{:S(2)}) copy-start(f32[512]{0:T(512)} %copy-done.51) | copy-start | bytes 6148
  1607.4 442.0 %reduce-scatter.7.cloned.1.call-start = ((), (), s32[]{:S(2)}) async-start(), calls=%async_computation.9 | async-start | bytes 6266880 | tf_op jit(solution)/shard_map/reduce_scatter | solution.py:275
  (114 other events, 5280.3 us)
Sparse Core Ops, SparseCore 0:
  10.2 55.5 all-gather.9
  67.7 102.2 all-gather.11
  465.1 113.8 all-gather.17
  624.6 124.5 reduce-scatter.8
  751.9 47.6 reduce-scatter.10
  802.5 29.6 all-gather.13
  834.0 57.9 all-gather.15
  926.7 115.3 all-gather.19
  1585.4 236.3 reduce-scatter.4
  1829.8 125.6 all-reduce.18
  1958.4 90.9 reduce-scatter.6
where the time goes:
time: 2090 us; the launch traced here: 2070 us
  waiting for transfers between devices  1030 us (49%)
  local copies, waits for them, and re-layouts  463 us (22%)
  matrix products  314 us (15%)
  other arithmetic  221 us (11%)
    dynamic_update_slice x12, local copies, waits for them, and re-layouts, scan_blocks(): lax.scan(jax.checkpoint(block_step), initial, pieces)  278 us
    reduce_scatter x1, waiting for transfers between devices, shards(): lax.psum_scatter(grad_in_local, 'dp', scatter_dimension=0, tiled=True)  214 us
    all_gather x2, waiting for transfers between devices, prefix(): everything = jax.tree.map(lambda part: lax.all_gather(part, axis), value)  190 us
    reduce_scatter x1, waiting for transfers between devices, shards(): lax.psum_scatter(grad_out_local, 'dp', scatter_dimension=0, tiled=True)  125 us
    psum x1, waiting for transfers between devices, shards(): lax.psum((grad_prenorm_local, back_small[0], back_small[1], back_small[2]...  119 us
    dot_general x6, matrix products, block_step(): local_out = jnp.einsum('tsh,shp->thp', mixing, values, precision=highest)  102 us
    all_gather x1, waiting for transfers between devices, shards(): lax.all_gather(grouped_in, 'dp', axis=0, tiled=True)  95.4 us
    reduce_scatter x1, waiting for transfers between devices, shards(): lax.psum_scatter(part_in, 'shard', scatter_dimension=0, tiled=True)  85.8 us
  transfers between devices with their start and end apart: 14, of which 11 were waited for; matrix products, arithmetic and copies ran while one was open for 5% of the time, Pallas kernels for 0%

commit v1 on v0

v1 whole, which is shorter than its diff:
```python
import functools

import jax
import jax.numpy as jnp
from jax import lax
from jax.experimental import pallas as pl
from jax.experimental.pallas import tpu as pltpu
from jax.sharding import PartitionSpec as P


HEADS = 48
HEAD_DIM = 64
STATE = 128
KW = 4
ADAM_STEP = 10
DI = 3072
CH = 3328

Q = 128
GH = 8
GW = GH * HEAD_DIM
NG = HEADS // GH
HALO = 8
TILE = 256

bf16 = jnp.bfloat16
f32 = jnp.float32
highest = lax.Precision.HIGHEST

norm_eps = 1e-05
beta_one = 0.9
beta_two = 0.95
adam_eps = 1e-08
rate_table = (0.2, 0.01, 0.2, 0.2, 0.2, 0.2, 0.2, 0.2, 0.01)
shrink_table = (0.0, 0.1, 0.1, 0.0, 0.0, 0.0, 0.0, 0.0, 0.1)

NN = (((1,), (0,)), ((), ()))
NT = (((1,), (1,)), ((), ()))


def halves(x):
    hi = x.astype(bf16)
    return hi, (x - hi.astype(f32)).astype(bf16)


def dot1(a, b, dims=NN):
    return lax.dot_general(a.astype(bf16), b.astype(bf16), dims, preferred_element_type=f32)


def dot3(a, b, dims=NN):
    ah, al = halves(a)
    bh, bl = halves(b)
    return dot1(ah, bh, dims) + (dot1(ah, bl, dims) + dot1(al, bh, dims))


def dotf(a, b, dims=NN):
    return lax.dot_general(a, b, dims, precision=highest, preferred_element_type=f32)


def iota(shape, dim):
    return lax.broadcasted_iota(jnp.int32, shape, dim)


def sigmoid(x):
    return 1.0 / (1.0 + jnp.exp(-x))


def softplus(x):
    u = jnp.exp(-jnp.abs(x))
    series = u * (1.0 - u * (0.5 - u * (1.0 / 3.0 - u * (0.25 - u * 0.2))))
    return jnp.maximum(x, 0.0) + jnp.where(u < 0.03, series, jnp.log(1.0 + u))


def pair_lanes(cols, j):
    rows = cols.shape[0]
    low = iota((rows, 128), 1) < HEAD_DIM
    return jnp.where(low, cols[:, 2 * j : 2 * j + 1], cols[:, 2 * j + 1 : 2 * j + 2])


def group_lanes(cols):
    return jnp.concatenate([pair_lanes(cols, j) for j in range(cols.shape[1] // 2)], axis=1)


def head_onehot():
    return (iota((HEADS, DI), 1) // HEAD_DIM == iota((HEADS, DI), 0)).astype(f32)


def params(limit=60000, **kw):
    return pltpu.CompilerParams(vmem_limit_bytes=limit * 1024, **kw)


def prep_kernel(
    step_ref, par_ref, mask_ref, delta_ref, cum_ref, cumt_ref, infc_ref, tailc_ref, tailn_ref,
    taild_ref, infd_ref, keep_ref, factor_ref,
):
    length = step_ref.shape[0]
    count = length // Q
    tri = (iota((Q, Q), 0) >= iota((Q, Q), 1)).astype(f32)
    eye = (iota((HEADS, HEADS), 0) == iota((HEADS, HEADS), 1)).astype(f32)
    rate = jnp.exp(par_ref[1:2, :])
    base = jnp.zeros((1, HEADS), f32)
    held = []
    keeps = []
    for c in range(count):
        rows = slice(c * Q, (c + 1) * Q)
        delta = softplus(step_ref[rows, :] + par_ref[0:1, :])
        cum = dotf(tri, -delta * rate)
        cumt_ref[:, rows] = dotf(eye, cum, NT)
        last = cum[Q - 1 : Q, :]
        alive, ending = mask_ref[rows, 0:1], mask_ref[rows, 1:2]
        infc = jnp.exp(cum) * alive
        tailn = jnp.exp(last - cum) * ending
        tailc = tailn * delta
        for g in range(NG):
            part = slice(g * GH, (g + 1) * GH)
            delta_ref[g, rows, :] = delta[:, part]
            cum_ref[g, rows, :] = cum[:, part]
            infc_ref[g, rows, :] = infc[:, part]
            tailn_ref[g, rows, :] = tailn[:, part]
            tailc_ref[g, rows, :] = tailc[:, part]
        keeps.append(infc[Q - 1 : Q, :])
        whole = cum + base
        infd_ref[rows, :] = jnp.exp(whole) * mask_ref[rows, 2:3]
        held.append((whole, delta))
        base = base + last
    for c in range(count):
        rows = slice(c * Q, (c + 1) * Q)
        whole, delta = held[c]
        taild = jnp.exp(base - whole) * mask_ref[rows, 3:4] * delta
        for g in range(NG):
            taild_ref[g, rows, :] = taild[:, g * GH : (g + 1) * GH]
    factor = jnp.exp(base) * mask_ref[length - 1 : length, 2:3]
    spread = head_onehot()
    line = iota((8, HEADS), 0)
    table = jnp.zeros((8, HEADS), f32)
    for c in range(count):
        table = jnp.where(line == c, keeps[c], table)
    keep_ref[...] = dotf(table, spread)
    factor_ref[...] = dotf(jnp.where(line == 0, factor, 0.0), spread)


def prep(step_raw, pars, mask):
    length = step_raw.shape[0]
    cols = jax.ShapeDtypeStruct((NG, length, GH), f32)
    wide = jax.ShapeDtypeStruct((8, DI), f32)
    return pl.pallas_call(
        prep_kernel,
        out_shape=(
            cols, cols, jax.ShapeDtypeStruct((HEADS, length), f32), cols, cols, cols, cols,
            jax.ShapeDtypeStruct((length, HEADS), f32), wide, wide,
        ),
        compiler_params=params(),
        cost_estimate=pl.CostEstimate(flops=10**7, bytes_accessed=10**7, transcendentals=10**5),
        name="prep",
    )(step_raw, pars, mask)


def conv_sum(x_ref, tap_ref, match_ref, start, rows, cols):
    total = tap_ref[KW : KW + 1, cols] + tap_ref[KW - 1 : KW, cols] * x_ref[
        pl.ds(HALO + start, rows), cols
    ]
    for k in range(KW - 1):
        taken = x_ref[pl.ds(HALO - (KW - 1) + k + start, rows), cols]
        total = total + tap_ref[k : k + 1, cols] * (taken * match_ref[k, pl.ds(start, rows), :])
    return total


def conv_kernel(
    xv_ref, xk_ref, tv_ref, tk_ref, match_ref, taild_ref, v_ref, kq_ref, state_ref, kt_hi, kt_lo
):
    length = v_ref.shape[0]
    count = length // Q

    @pl.when(pl.program_id(0) == 0)
    def _():
        for c in range(count):
            for j in range(2):
                cols = slice(128 * j, 128 * (j + 1))
                s = conv_sum(xk_ref, tk_ref, match_ref, c * Q, Q, cols)
                m = s * sigmoid(s)
                kq_ref[c * Q : (c + 1) * Q, cols] = m
                if j == 0:
                    hi, lo = halves(m.T)
                    kt_hi[:, c * Q : (c + 1) * Q] = hi
                    kt_lo[:, c * Q : (c + 1) * Q] = lo

    total = jnp.zeros((STATE, GW), f32)
    for c in range(count):
        rows = slice(c * Q, (c + 1) * Q)
        tail = taild_ref[0, rows, :]
        parts = []
        for j in range(GW // 128):
            cols = slice(128 * j, 128 * (j + 1))
            s = conv_sum(xv_ref, tv_ref, match_ref, c * Q, Q, cols)
            m = s * sigmoid(s)
            v_ref[rows, cols] = m
            parts.append(m * pair_lanes(tail, j))
        hi, lo = halves(jnp.concatenate(parts, axis=1))
        kh, kl = kt_hi[:, rows], kt_lo[:, rows]
        total = total + (dot1(kh, hi) + (dot1(kh, lo) + dot1(kl, hi)))
    state_ref[...] = total


def conv_state(rest, taps, match, taild):
    length = match.shape[1]
    high = length + HALO
    kq_at = DI // (2 * STATE)
    return pl.pallas_call(
        conv_kernel,
        grid=(NG,),
        in_specs=[
            pl.BlockSpec((high, GW), lambda g: (0, g)),
            pl.BlockSpec((high, 2 * STATE), lambda g: (0, kq_at)),
            pl.BlockSpec((8, GW), lambda g: (0, g)),
            pl.BlockSpec((8, 2 * STATE), lambda g: (0, kq_at)),
            pl.BlockSpec((KW - 1, length, 128), lambda g: (0, 0, 0)),
            pl.BlockSpec((1, length, GH), lambda g: (g, 0, 0)),
        ],
        out_specs=(
            pl.BlockSpec((length, GW), lambda g: (0, g)),
            pl.BlockSpec((length, 2 * STATE), lambda g: (0, 0)),
            pl.BlockSpec((STATE, GW), lambda g: (0, g)),
        ),
        out_shape=(
            jax.ShapeDtypeStruct((length, DI), f32),
            jax.ShapeDtypeStruct((length, 2 * STATE), f32),
            jax.ShapeDtypeStruct((STATE, DI), f32),
        ),
        scratch_shapes=[pltpu.VMEM((STATE, length), bf16), pltpu.VMEM((STATE, length), bf16)],
        compiler_params=params(),
        cost_estimate=pl.CostEstimate(flops=2 * 10**9, bytes_accessed=2 * 10**7, transcendentals=2 * 10**6),
        name="conv_state",
    )(rest, rest, taps, taps, match, taild)


def masks_of(segc_ref, segr_ref, rows):
    same = segc_ref[rows, 0:1] == segr_ref[0:1, rows]
    later = iota((Q, Q), 0) >= iota((Q, Q), 1)
    earlier = iota((Q, Q), 0) <= iota((Q, Q), 1)
    return jnp.where(same & later, 0.0, -1e30), jnp.where(same & earlier, 0.0, -1e30)


def local_kernel(
    v_ref, kq_ref, delta_ref, cum_ref, cumt_ref, infc_ref, tailc_ref, keep_ref, segc_ref, segr_ref,
    y_ref, gram, bias, kt,
):
    length = v_ref.shape[0]
    count = length // Q

    @pl.when(pl.program_id(0) == 0)
    def _():
        for c in range(count):
            rows = slice(c * Q, (c + 1) * Q)
            k, q = kq_ref[rows, :STATE], kq_ref[rows, STATE:]
            bias[rows, :] = masks_of(segc_ref, segr_ref, rows)[0]
            gram[rows, :] = dot3(q, k, NT)
            kt[:, rows] = k.T

    low = iota((Q, 128), 1) < HEAD_DIM
    state = None
    for c in range(count):
        rows = slice(c * Q, (c + 1) * Q)
        delta, cum, tail, inflow = (r[0, rows, :] for r in (delta_ref, cum_ref, tailc_ref, infc_ref))
        g, b = gram[rows, :], bias[rows, :]
        if c:
            carried = dot3(kq_ref[rows, STATE:], state)
        tails = []
        for j in range(GW // 128):
            cols = slice(128 * j, 128 * (j + 1))
            v = v_ref[rows, cols]
            w = v * pair_lanes(delta, j)
            both = []
            for i in (2 * j, 2 * j + 1):
                both.append((g * jnp.exp(cum[:, i : i + 1] - cumt_ref[i : i + 1, rows] + b)))
            stacked = jnp.concatenate([jnp.where(low, w, 0.0), jnp.where(low, 0.0, w)], axis=0)
            y = dot3(jnp.concatenate(both, axis=1), stacked)
            if c:
                y = y + carried[:, cols] * pair_lanes(inflow, j)
            y_ref[rows, cols] = y
            if c < count - 1:
                tails.append(v * pair_lanes(tail, j))
        if c < count - 1:
            fresh = dot3(kt[:, rows], jnp.concatenate(tails, axis=1))
            state = fresh if state is None else state * keep_ref[c : c + 1, :] + fresh


def local_out(v, kq, delta, cum, cumt, infc, tailc, keep, segc, segr):
    length = v.shape[0]
    cols = pl.BlockSpec((1, length, GH), lambda g: (g, 0, 0))
    return pl.pallas_call(
        local_kernel,
        grid=(NG,),
        in_specs=[
            pl.BlockSpec((length, GW), lambda g: (0, g)),
            pl.BlockSpec((length, 2 * STATE), lambda g: (0, 0)),
            cols, cols,
            pl.BlockSpec((GH, length), lambda g: (g, 0)),
            cols, cols,
            pl.BlockSpec((8, GW), lambda g: (0, g)),
            pl.BlockSpec((length, 8), lambda g: (0, 0)),
            pl.BlockSpec((8, length), lambda g: (0, 0)),
        ],
        out_specs=pl.BlockSpec((length, GW), lambda g: (0, g)),
        out_shape=jax.ShapeDtypeStruct((length, DI), f32),
        scratch_shapes=[
            pltpu.VMEM((length, Q), f32), pltpu.VMEM((length, Q), f32),
            pltpu.VMEM((STATE, length), f32),
        ],
        compiler_params=params(),
        cost_estimate=pl.CostEstimate(flops=2 * 10**9, bytes_accessed=2 * 10**7, transcendentals=4 * 10**6),
        name="local_out",
    )(v, kq, delta, cum, cumt, infc, tailc, keep, segc, segr)


def gate_kernel(
    y_ref, v_ref, z_ref, g_ref, kq_ref, inc_ref, infd_ref, dir_ref, gam_ref,
    out_ref, dy_ref, dz_ref, dinc_ref, small_ref, ybuf, rbuf,
):
    first = pl.program_id(0) == 0
    rows = y_ref.shape[0]
    q = kq_ref[:, STATE:]
    inflow = infd_ref[...]
    square = jnp.zeros((rows, 128), f32)
    cross = jnp.zeros((rows, 128), f32)
    for j in range(DI // 128):
        cols = slice(128 * j, 128 * (j + 1))
        carry = dot3(q, inc_ref[:, cols]) * pair_lanes(inflow, j)
        y = y_ref[:, cols] + carry + dir_ref[0:1, cols] * v_ref[:, cols]
        z = z_ref[:, cols]
        gated = y * (z * sigmoid(z))
        ybuf[:, cols] = y
        rbuf[:, cols] = gated
        square = square + gated * gated
        cross = cross + gated * (g_ref[:, cols] * gam_ref[0:1, cols])
    inv = lax.rsqrt(jnp.sum(square, axis=1, keepdims=True) * (1.0 / DI) + norm_eps)
    slope = inv * inv * inv * (jnp.sum(cross, axis=1, keepdims=True) * (1.0 / DI))
    qt = q.T

    @pl.when(first)
    def _():
        dinc_ref[...] = jnp.zeros_like(dinc_ref)
        small_ref[...] = jnp.zeros_like(small_ref)

    for j in range(DI // 128):
        cols = slice(128 * j, 128 * (j + 1))
        gated = rbuf[:, cols]
        scaled = gated * inv
        gam = gam_ref[0:1, cols]
        out_ref[:, cols] = (scaled * gam).astype(bf16)
        g = g_ref[:, cols]
        dgated = inv * (g * gam) - gated * slope
        z = z_ref[:, cols]
        s = sigmoid(z)
        dy = dgated * (z * s)
        dy_ref[:, cols] = dy
        dz = dgated * ybuf[:, cols] * (s * (1.0 + z * (1.0 - s)))
        dz_ref[:, cols] = dz.astype(bf16)
        small_ref[2:3, cols] = jnp.maximum(
            small_ref[2:3, cols], jnp.max(jnp.abs(dz), axis=0, keepdims=True)
        )
        small_ref[0:1, cols] += jnp.sum(g * scaled, axis=0, keepdims=True)
        small_ref[1:2, cols] += jnp.sum(dy * v_ref[:, cols], axis=0, keepdims=True)
        dinc_ref[:, cols] += dot3(qt, dy * pair_lanes(inflow, j))


def gate(y, v, z, g, kq, inc, infd, dirx, gam):
    length = y.shape[0]
    tile = Q
    big = pl.BlockSpec((tile, DI), lambda i: (i, 0))
    return pl.pallas_call(
        gate_kernel,
        grid=(length // tile,),
        in_specs=[
            big, big, big, big,
            pl.BlockSpec((tile, 2 * STATE), lambda i: (i, 0)),
            pl.BlockSpec((STATE, DI), lambda i: (0, 0)),
            pl.BlockSpec((tile, HEADS), lambda i: (i, 0)),
            pl.BlockSpec((8, DI), lambda i: (0, 0)),
            pl.BlockSpec((8, DI), lambda i: (0, 0)),
        ],
        out_specs=(
            big, big, big,
            pl.BlockSpec((STATE, DI), lambda i: (0, 0)),
            pl.BlockSpec((8, DI), lambda i: (0, 0)),
        ),
        out_shape=(
            jax.ShapeDtypeStruct((length, DI), bf16),
            jax.ShapeDtypeStruct((length, DI), f32),
            jax.ShapeDtypeStruct((length, DI), bf16),
            jax.ShapeDtypeStruct((STATE, DI), f32),
            jax.ShapeDtypeStruct((8, DI), f32),
        ),
        scratch_shapes=[pltpu.VMEM((tile, DI), f32), pltpu.VMEM((tile, DI), f32)],
        compiler_params=params(),
        cost_estimate=pl.CostEstimate(flops=10**9, bytes_accessed=4 * 10**7, transcendentals=4 * 10**6),
        name="gate",
    )(y, v, z, g, kq, inc, infd, dirx, gam)


def back_kernel(
    final, v_ref, dy_ref, kq_ref, delta_ref, cum_ref, cumt_ref, infc_ref, tailc_ref, tailn_ref,
    keep_ref, inc_ref, dout_ref, dir_ref, segc_ref, segr_ref, dkq_in, dgram_in,
    dv_ref, dkq_ref, dgram, ddelta_ref, dcum_ref, drow_ref, flow_ref,
    gram, gramt, bias, biast, kt, qt, states,
):
    length = v_ref.shape[0]
    count = length // Q
    step = pl.program_id(0)

    @pl.when(step == 0)
    def _():
        for c in range(count):
            rows = slice(c * Q, (c + 1) * Q)
            k, q = kq_ref[rows, :STATE], kq_ref[rows, STATE:]
            b, bt = masks_of(segc_ref, segr_ref, rows)
            bias[rows, :] = b
            biast[rows, :] = bt
            scores = dot3(q, k, NT)
            gram[rows, :] = scores
            gramt[rows, :] = scores.T
            kt[:, rows] = k.T
            qt[:, rows] = q.T
        dgram[...] = dgram_in[...]
        dkq_ref[...] = dkq_in[...]

    low = iota((Q, 128), 1) < HEAD_DIM
    lane = iota((Q, GH), 1)
    line = iota((8, GW), 0)

    states[0] = inc_ref[...].astype(f32)
    for c in range(count):
        rows = slice(c * Q, (c + 1) * Q)
        weighted = v_ref[rows, :] * group_lanes(tailc_ref[0, rows, :])
        states[c + 1] = states[c] * keep_ref[c : c + 1, :] + dot3(kt[:, rows], weighted)

    back = dout_ref[...].astype(f32)
    flows = jnp.zeros((8, GW), f32)
    for c in reversed(range(count)):
        rows = slice(c * Q, (c + 1) * Q)
        flows = jnp.where(line == c, jnp.sum(back * states[c + 1], axis=0, keepdims=True), flows)
        delta, cum = delta_ref[0, rows, :], cum_ref[0, rows, :]
        inflow, tailc, tailn = infc_ref[0, rows, :], tailc_ref[0, rows, :], tailn_ref[0, rows, :]
        k, q = kq_ref[rows, :STATE], kq_ref[rows, STATE:]
        before = states[c]
        after = back
        y_in = dot3(q, before)
        w_in = dot3(k, after)
        g, gt, b, bt = gram[rows, :], gramt[rows, :], bias[rows, :], biast[rows, :]
        dg = dgram[rows, :]
        ddelta = jnp.zeros((Q, GH), f32)
        dcum = jnp.zeros((Q, GH), f32)
        dys, ws = [], []
        for j in range(GW // 128):
            cols = slice(128 * j, 128 * (j + 1))
            dy, v = dy_ref[rows, cols], v_ref[rows, cols]
            spread = pair_lanes(delta, j)
            w = v * spread
            stacked = jnp.concatenate(
                [jnp.where(low, dy, 0.0), jnp.where(low, 0.0, dy)], axis=0
            )
            inner = dot3(stacked, w, NT)
            turned = []
            for i in (0, 1):
                h = 2 * j + i
                col, row = cum[:, h : h + 1], cumt_ref[h : h + 1, rows]
                turned.append(gt * jnp.exp(row - col + bt))
                weighed = inner[Q * i : Q * (i + 1), :] * jnp.exp(col - row + b)
                dg = dg + weighed
                full = weighed * g
                dcum = dcum + jnp.where(lane == h, jnp.sum(full, axis=1, keepdims=True), 0.0)
                drow_ref[h : h + 1, rows] = jnp.sum(full, axis=0, keepdims=True)
            dw_in = w_in[:, cols] * pair_lanes(tailn, j)
            dw = dot3(jnp.concatenate(turned, axis=1), stacked) + dw_in
            dv_ref[rows, cols] = spread * dw + dir_ref[0:1, cols] * dy
            dflow = dy * pair_lanes(inflow, j)
            one = dflow * y_in[:, cols] - w * dw_in
            two = v * dw
            for i in (0, 1):
                h = 2 * j + i
                keep = low if i == 0 else jnp.logical_not(low)
                dcum = dcum + jnp.where(
                    lane == h, jnp.sum(jnp.where(keep, one, 0.0), axis=1, keepdims=True), 0.0
                )
                ddelta = ddelta + jnp.where(
                    lane == h, jnp.sum(jnp.where(keep, two, 0.0), axis=1, keepdims=True), 0.0
                )
            dys.append(dflow)
            ws.append(v * pair_lanes(tailc, j))
        dgram[rows, :] = dg
        ddelta_ref[0, rows, :] = ddelta
        dcum_ref[0, rows, :] = dcum
        flowing = jnp.concatenate(dys, axis=1)
        dkq_ref[rows, STATE:] += dot3(flowing, before, NT)
        dkq_ref[rows, :STATE] += dot3(jnp.concatenate(ws, axis=1), after, NT)
        if c:
            back = back * keep_ref[c : c + 1, :] + dot3(qt[:, rows], flowing)
    flow_ref[...] = flows

    @pl.when(jnp.logical_and(step == pl.num_programs(0) - 1, final))
    def _():
        for c in range(count):
            rows = slice(c * Q, (c + 1) * Q)
            k, q = kq_ref[rows, :STATE], kq_ref[rows, STATE:]
            dg = dgram[rows, :]
            dkq_ref[rows, STATE:] += dot3(dg, k)
            dkq_ref[rows, :STATE] += dot3(dg.T, q)


def back_local(
    first, last, held, v, dy, kq, delta, cum, cumt, infc, tailc, tailn, keep, inc, dout, dirx, segc, segr
):
    length = v.shape[0]
    count = length // Q
    groups = last - first
    if held is None:
        held = (jnp.zeros((length, 2 * STATE), f32), jnp.zeros((length, Q), f32))
    cols = pl.BlockSpec((1, length, GH), lambda g: (g + first, 0, 0))
    wide = pl.BlockSpec((length, GW), lambda g: (0, g + first))
    state = pl.BlockSpec((STATE, GW), lambda g: (0, g + first))
    lines = pl.BlockSpec((8, GW), lambda g: (0, g + first))
    turned = pl.BlockSpec((GH, length), lambda g: (g + first, 0))
    whole = pl.BlockSpec((length, 2 * STATE), lambda g: (0, 0))
    table = pl.BlockSpec((length, Q), lambda g: (0, 0))
    square = pltpu.VMEM((length, Q), f32)
    out_cols = pl.BlockSpec((1, length, GH), lambda g: (g, 0, 0))
    return pl.pallas_call(
        functools.partial(back_kernel, last == NG),
        grid=(groups,),
        in_specs=[
            wide, wide, whole, cols, cols, turned, cols, cols, cols, lines, state, state, lines,
            pl.BlockSpec((length, 8), lambda g: (0, 0)),
            pl.BlockSpec((8, length), lambda g: (0, 0)),
            whole, table,
        ],
        out_specs=(
            pl.BlockSpec((length, GW), lambda g: (0, g)), whole, table, out_cols, out_cols,
            pl.BlockSpec((GH, length), lambda g: (g, 0)),
            pl.BlockSpec((8, GW), lambda g: (0, g)),
        ),
        out_shape=(
            jax.ShapeDtypeStruct((length, groups * GW), f32),
            jax.ShapeDtypeStruct((length, 2 * STATE), f32),
            jax.ShapeDtypeStruct((length, Q), f32),
            jax.ShapeDtypeStruct((groups, length, GH), f32),
            jax.ShapeDtypeStruct((groups, length, GH), f32),
            jax.ShapeDtypeStruct((groups * GH, length), f32),
            jax.ShapeDtypeStruct((8, groups * GW), f32),
        ),
        scratch_shapes=[
            square, square, square, square,
            pltpu.VMEM((STATE, length), f32), pltpu.VMEM((STATE, length), f32),
            pltpu.VMEM((count + 1, STATE, GW), f32),
        ],
        compiler_params=params(),
        cost_estimate=pl.CostEstimate(
            flops=groups * 5 * 10**9, bytes_accessed=groups * 5 * 10**6, transcendentals=groups * 10**6
        ),
        name="back_local",
    )(v, dy, kq, delta, cum, cumt, infc, tailc, tailn, keep, inc, dout, dirx, segc, segr, *held)


def step_kernel(step_ref, par_ref, ddelta_ref, dcum_ref, drow_ref, flow_ref, dstep_ref, small_ref):
    length = step_ref.shape[0]
    upper = (iota((Q, Q), 0) <= iota((Q, Q), 1)).astype(f32)
    eye = (iota((Q, Q), 0) == iota((Q, Q), 1)).astype(f32)
    last = iota((Q, 1), 0) == Q - 1
    rate = jnp.exp(par_ref[1:2, :])
    flows = dotf(flow_ref[...], head_onehot(), NT)
    times = jnp.zeros((1, HEADS), f32)
    decays = jnp.zeros((1, HEADS), f32)
    most = jnp.zeros((1, HEADS), f32)
    for c in range(length // Q):
        rows = slice(c * Q, (c + 1) * Q)
        ddelta = jnp.zeros((Q, HEADS), f32)
        dcum = -dotf(eye, drow_ref[:, rows], NT)
        for g in range(NG):
            place = (iota((GH, HEADS), 0) + g * GH == iota((GH, HEADS), 1)).astype(f32)
            ddelta = ddelta + dotf(ddelta_ref[g, rows, :], place)
            dcum = dcum + dotf(dcum_ref[g, rows, :], place)
        dcum = dcum + jnp.where(last, flows[c : c + 1, :], 0.0)
        x = step_ref[rows, :] + par_ref[0:1, :]
        dlog = dotf(upper, dcum) * rate
        decays = decays - jnp.sum(dlog * softplus(x), axis=0, keepdims=True)
        dstep = (ddelta - dlog) * sigmoid(x)
        times = times + jnp.sum(dstep, axis=0, keepdims=True)
        most = jnp.maximum(most, jnp.max(jnp.abs(dstep), axis=0, keepdims=True))
        dstep_ref[rows, :] = dstep.astype(bf16)
    small_ref[...] = jnp.zeros_like(small_ref)
    small_ref[0:1, :] = times
    small_ref[1:2, :] = decays
    small_ref[2:3, :] = most


def step_back(step_raw, pars, ddelta, dcum, drow, flow):
    return pl.pallas_call(
        step_kernel,
        out_shape=(
            jax.ShapeDtypeStruct(step_raw.shape, bf16),
            jax.ShapeDtypeStruct((8, HEADS), f32),
        ),
        compiler_params=params(),
        cost_estimate=pl.CostEstimate(flops=10**7, bytes_accessed=10**7, transcendentals=10**5),
        name="step_back",
    )(step_raw, pars, ddelta, dcum, drow, flow)


def unconv_kernel(x_ref, tap_ref, match_ref, da_ref, db_ref, dkq_ref, dx_ref, edge_ref, dtap_ref, *held):
    length = dx_ref.shape[0]
    count = length // Q
    step = pl.program_id(0)
    half = DI // TILE // 2
    for buf in held:
        buf[0:HALO, :] = jnp.zeros((HALO, TILE), f32)
        buf[HALO + length :, :] = jnp.zeros((HALO, TILE), f32)
    for j in range(TILE // 128):
        cols = slice(128 * j, 128 * (j + 1))
        sums = [jnp.zeros((1, 128), f32) for _ in range(KW + 1)]
        for c in range(count):
            rows = slice(c * Q, (c + 1) * Q)
            s = conv_sum(x_ref, tap_ref, match_ref, c * Q, Q, cols)
            sig = sigmoid(s)
            dm = jnp.where(
                step < half, da_ref[rows, cols], jnp.where(step < 2 * half, db_ref[rows, cols], dkq_ref[rows, cols])
            )
            ds = dm * (sig * (1.0 + s * (1.0 - sig)))
            sums[KW] = sums[KW] + jnp.sum(ds, axis=0, keepdims=True)
            for k in range(KW):
                e = ds if k == KW - 1 else ds * match_ref[k, rows, :]
                held[k][HALO + c * Q : HALO + (c + 1) * Q, cols] = e
                taken = x_ref[pl.ds(HALO - (KW - 1) + k + c * Q, Q), cols]
                sums[k] = sums[k] + jnp.sum(e * taken, axis=0, keepdims=True)
        for k in range(KW + 1):
            dtap_ref[k : k + 1, cols] = sums[k]

        def placed(start, rows):
            total = None
            for k in range(KW):
                term = tap_ref[k : k + 1, cols] * held[k][pl.ds(start + KW - 1 - k, rows), cols]
                total = term if total is None else total + term
            return total

        edge_ref[0:HALO, cols] = placed(0, HALO)
        most = jnp.zeros((1, 128), f32)
        for c in range(count):
            dx = placed(HALO + c * Q, Q)
            most = jnp.maximum(most, jnp.max(jnp.abs(dx), axis=0, keepdims=True))
            dx_ref[c * Q : (c + 1) * Q, cols] = dx.astype(bf16)
            if c == count - 1:
                edge_ref[HALO:, cols] = dx[Q - HALO :, :]
        dtap_ref[KW + 1 : KW + 2, cols] = most
    dtap_ref[KW + 2 :, :] = jnp.zeros((8 - KW - 2, TILE), f32)


def unconv(rest, taps, match, dva, dvb, dkq):
    length = match.shape[1]
    high = length + HALO
    half = DI // TILE // 2
    return pl.pallas_call(
        unconv_kernel,
        grid=(CH // TILE,),
        in_specs=[
            pl.BlockSpec((high, TILE), lambda j: (0, j)),
            pl.BlockSpec((8, TILE), lambda j: (0, j)),
            pl.BlockSpec((KW - 1, length, 128), lambda j: (0, 0, 0)),
            pl.BlockSpec((length, TILE), lambda j: (0, jnp.minimum(j, half - 1))),
            pl.BlockSpec((length, TILE), lambda j: (0, jnp.clip(j - half, 0, half - 1))),
            pl.BlockSpec((length, TILE), lambda j: (0, 0)),
        ],
        out_specs=(
            pl.BlockSpec((length, TILE), lambda j: (0, j)),
            pl.BlockSpec((2 * HALO, TILE), lambda j: (0, j)),
            pl.BlockSpec((8, TILE), lambda j: (0, j)),
        ),
        out_shape=(
            jax.ShapeDtypeStruct((length, CH), bf16),
            jax.ShapeDtypeStruct((2 * HALO, CH), f32),
            jax.ShapeDtypeStruct((8, CH), f32),
        ),
        scratch_shapes=[pltpu.VMEM((length + 2 * HALO, TILE), f32) for _ in range(KW)],
        compiler_params=params(),
        cost_estimate=pl.CostEstimate(flops=10**8, bytes_accessed=2 * 10**7, transcendentals=2 * 10**6),
        name="unconv",
    )(rest, taps, match, dva, dvb, dkq)


def adamw(param, grad, moment, square, rate, shrink):
    moment_new = beta_one * moment + (1.0 - beta_one) * grad
    square_new = beta_two * square + (1.0 - beta_two) * grad * grad
    first_corr = 1.0 - beta_one**ADAM_STEP
    second_corr = 1.0 - beta_two**ADAM_STEP
    update = moment_new / first_corr / (jnp.sqrt(square_new / second_corr) + adam_eps)
    return (param - rate * (update + shrink * param), moment_new, square_new)


def shifted(value, axis, by):
    count = lax.axis_size(axis)
    pairs = [(i, i + by) for i in range(count) if 0 <= i + by < count]
    return lax.ppermute(value, axis, pairs)


TOKENS = (((0,), (0,)), ((), ()))


def gathered(value):
    return lax.all_gather(value, ("dp", "shard"), axis=0, tiled=True)


def shard_gathered(value):
    count, here = lax.axis_size("shard"), lax.axis_index("shard")
    rows, width = value.shape
    held = jnp.zeros((count * rows, width), value.dtype)
    for k in range(count):
        part = exchanged(value, "shard", k) if k else value
        held = lax.dynamic_update_slice(held, part, ((here ^ k) * rows, 0))
    return held


def exchanged(value, axis, by):
    return lax.ppermute(value, axis, [(i, i ^ by) for i in range(lax.axis_size(axis))])


PAD = 16


def relative(value, block, core):
    base = lax.axis_index("dp") // 2
    length = value.shape[0]
    return [
        lax.dynamic_slice(value, (0, (((j ^ base) * 2) + core) * block), (length, block))
        for j in range(lax.axis_size("dp") // 2)
    ]


def both_cores(value):
    return jnp.concatenate([value, exchanged(value, "dp", 1)], axis=0)


def sum_columns(value, block):
    core = lax.axis_index("dp") % 2
    theirs = jnp.concatenate(relative(value, block, 1 - core), axis=1)
    mine = jnp.concatenate(relative(value, block, core), axis=1)
    return jnp.concatenate([mine, exchanged(theirs, "dp", 1)], axis=0)


def exponent(bound):
    return jnp.ceil(jnp.log2(jnp.maximum(bound, 1e-30)))


def coded(total, power, rows):
    own = iota(total.shape, 0) < rows
    return jnp.where(own, total * jnp.exp2(15.0 - power), power).astype(jnp.float16)


def decoded(payload, rows):
    power = payload[rows, 0].astype(f32)
    return payload.astype(f32) * jnp.exp2(power - 15.0), power


def after(value, *earlier):
    return lax.optimization_barrier((value, earlier))[0]


class Sum:
    def __init__(self, lhs, order):
        spots = lax.axis_size("dp") // 2
        self.block = lhs.shape[1] // spots
        self.order = order
        self.kept, self.sends = [0], []
        for bit in reversed(order):
            send = [j ^ (1 << bit) for j in self.kept]
            self.sends.insert(0, send)
            self.kept = self.kept + send
        self.rows = spots * self.block
        half = len(self.kept) // 2
        self.sent = self.columns(lhs, self.sends[0])
        self.held = self.columns(lhs, self.kept[:half])
        self.total = None
        self.at = 0

    def columns(self, lhs, places):
        block = self.block
        return jnp.concatenate(
            [lhs[:, j * block : (j + 1) * block] for j in places] + [jnp.zeros((lhs.shape[0], PAD), bf16)],
            axis=1,
        )

    def prepare(self, rhs=None, bound=None):
        self.rows //= 2
        if self.total is None:
            self.rhs, self.power = rhs, exponent(bound)
            part = lax.dot_general(self.sent, rhs, TOKENS, preferred_element_type=f32)
        else:
            part = self.total[self.rows : 2 * self.rows + PAD]
        self.payload = coded(part, self.power, self.rows)

    def send(self):
        self.got = exchanged(self.payload, "dp", 2 << self.order[self.at])
        self.at += 1
        if self.total is None:
            self.total = lax.dot_general(self.held, self.rhs, TOKENS, preferred_element_type=f32)

    def take(self, *earlier):
        got, other = decoded(after(self.got, earlier), self.rows)
        self.total = self.total[: self.rows + PAD] + got
        self.power = jnp.maximum(self.power, other) + 1.0

    def more(self):
        return self.at < len(self.order)

    def shard_prepare(self):
        count, here = lax.axis_size("shard"), lax.axis_index("shard")
        self.rows //= count
        self.payloads = [
            coded(
                lax.dynamic_slice(self.total, ((here ^ k) * self.rows, 0), (self.rows + PAD, self.total.shape[1])),
                self.power, self.rows,
            )
            for k in range(1, count)
        ]

    def shard_send(self):
        self.parts = [exchanged(part, "shard", k + 1) for k, part in enumerate(self.payloads)]

    def shard_take(self, *earlier):
        here = lax.axis_index("shard")
        result = lax.dynamic_slice(self.total, (here * self.rows, 0), (self.rows, self.total.shape[1]))
        for part in self.parts:
            result = result + decoded(after(part, earlier), self.rows)[0][: self.rows]
        return result


def summed(value):
    for axis in ("dp", "shard"):
        count = lax.axis_size(axis)
        if count & (count - 1):
            value = lax.psum(value, axis)
            continue
        by = 1
        while by < count:
            value = value + lax.ppermute(value, axis, [(i, i ^ by) for i in range(count)])
            by *= 2
    return value


def carried(state, factor, by):
    incoming = shifted(state.astype(bf16), "shard", by)
    for _ in range(lax.axis_size("shard") - 2):
        incoming = shifted((state + factor * incoming.astype(f32)).astype(bf16), "shard", by)
    return incoming


def shards(
    hidden_in, cotangent, segment_ids,
    param_prenorm, param_inputs, param_kernel, param_offsets, param_timestep, param_decays,
    param_direct, param_gating, param_outputs,
    moment_prenorm, moment_inputs, moment_kernel, moment_offsets, moment_timestep, moment_decays,
    moment_direct, moment_gating, moment_outputs,
    square_prenorm, square_inputs, square_kernel, square_offsets, square_timestep, square_decays,
    square_direct, square_gating, square_outputs,
):
    length, width = hidden_in.shape
    own_inputs = param_inputs.astype(bf16)
    rest_w = gathered(own_inputs[:, DI:])
    gate_w = lax.all_gather(shard_gathered(own_inputs[:, :DI]), "dp", axis=0, tiled=True)
    out_w = lax.all_gather(shard_gathered(param_outputs.astype(bf16)), "dp", axis=0, tiled=True)

    seg = segment_ids.astype(f32)
    ends = jnp.pad(seg[length - HALO :], (0, width - HALO))[None, :]
    halo = shifted(
        jnp.concatenate([hidden_in[length - HALO :], jnp.broadcast_to(ends, (HALO, width))], axis=0),
        "shard", 1,
    )
    rim_seg = jnp.where(lax.axis_index("shard") == 0, -1.0, halo[HALO, :HALO])
    rim = rim_seg[HALO - 1]
    all_segs = jnp.concatenate([rim_seg, seg])
    match = jnp.stack(
        [
            (all_segs[HALO - (KW - 1) + k : HALO - (KW - 1) + k + length] == seg).astype(f32)
            for k in range(KW - 1)
        ]
    )
    match = jnp.broadcast_to(match[:, :, None], (KW - 1, length, 128))
    chunks = seg.reshape(-1, Q)
    before = jnp.concatenate([rim[None], chunks[:-1, Q - 1]])
    mask = jnp.stack(
        [
            (chunks == before[:, None]).reshape(-1),
            (chunks == chunks[:, Q - 1 :]).reshape(-1),
            seg == rim,
            seg == seg[length - 1],
        ]
        + [seg < -1.0] * 4,
        axis=1,
    ).astype(f32)
    segc = jnp.broadcast_to(seg[:, None], (length, 8))
    segr = jnp.broadcast_to(seg[None, :], (8, length))

    taps = jnp.concatenate([param_kernel, param_offsets[None, :], jnp.zeros((8 - KW - 1, CH), f32)], axis=0)
    pars = jnp.concatenate([param_timestep[None, :], param_decays[None, :], jnp.zeros((6, HEADS), f32)], axis=0)
    dirx = jnp.broadcast_to(jnp.repeat(param_direct, HEAD_DIM)[None, :], (8, DI))
    gam = jnp.broadcast_to(param_gating[None, :], (8, DI))

    hidden = jnp.concatenate([halo[:HALO], hidden_in], axis=0)
    inv = lax.rsqrt(jnp.mean(hidden * hidden, axis=1, keepdims=True) + norm_eps)
    normed = (hidden * inv * param_prenorm).astype(bf16)
    own_normed = normed[HALO:]
    upstream = cotangent.astype(bf16)

    groups = lax.axis_size("shard")
    spots = [bit for bit in range(20) if (2 << bit) < lax.axis_size("dp")]
    in_block, out_block = groups * param_inputs.shape[0], groups * param_outputs.shape[0]
    up_both = both_cores(upstream)
    normed_both = sum_columns(own_normed, in_block)
    norm_bound = 2.02 * length * width**0.5 * jnp.max(jnp.abs(param_prenorm))
    gate_bound = 2.02 * length * DI**0.5 * jnp.max(jnp.abs(param_gating))
    gate_bound = gate_bound * jnp.max(jnp.abs(up_both)).astype(f32)
    gate_sum = Sum(normed_both, spots[::-1])
    rest_sums = [Sum(normed_both, spots), Sum(normed_both, spots[::-1])]
    rest_w = after(
        rest_w, match, mask, segc, segr, taps, pars, dirx, gam, up_both, gate_bound, norm_bound,
        gate_sum.sent, gate_sum.held, rest_sums[0].sent, rest_sums[0].held,
    )

    rest = jnp.dot(normed, rest_w, preferred_element_type=f32)
    step_raw = rest[HALO:, CH:]
    delta, cum, cumt, infc, tailc, tailn, taild, infd, keep, factor = prep(step_raw, pars, mask)
    v, kq, state = conv_state(rest, taps, match, taild)
    incoming = carried(state, factor[0:1], 1)
    y = local_out(v, kq, delta, cum, cumt, infc, tailc, keep, segc, segr)
    gate_w = after(gate_w, y)
    out_w = after(out_w, y)
    z = jnp.dot(own_normed, gate_w, preferred_element_type=f32)
    back_gated = lax.dot_general(upstream, out_w, NT, preferred_element_type=f32)
    gated, dy, dz, dinc, small = gate(y, v, z, back_gated, kq, incoming, infd, dirx, gam)

    dz_most = jnp.max(small[2])
    dz_most = jnp.maximum(dz_most, exchanged(jnp.full((8, 128), dz_most), "dp", 1)[0, 0])
    outgoing = carried(dinc, factor[0:1], -1)
    out_sum = Sum(sum_columns(gated, out_block), spots)
    dz_both = both_cores(dz)
    block_out = hidden_in + jnp.dot(gated, out_w, preferred_element_type=f32)
    first_sums = [out_sum, gate_sum]
    out_sum.prepare(up_both, gate_bound)
    gate_sum.prepare(dz_both, norm_bound * dz_most)
    for one in first_sums:
        one.send()
    back_normed = lax.dot_general(dz, gate_w, NT, preferred_element_type=f32)
    outgoing = after(outgoing, out_sum.payload, gate_sum.payload, out_sum.total, gate_sum.total, back_normed, block_out)

    ssm = (kq, delta, cum, cumt, infc, tailc, tailn, keep, incoming)
    dv1, *held1 = back_local(0, NG // 2, None, v, dy, *ssm, outgoing, dirx, segc, segr)
    for one in first_sums:
        one.take(dv1)
        if one.more():
            one.prepare()
            one.send()
    dy = after(dy, *[one.payload for one in first_sums])
    dv2, *held2 = back_local(NG // 2, NG, held1[:2], v, dy, *ssm, outgoing, dirx, segc, segr)
    for one in first_sums:
        one.take(dv2)
        while one.more():
            one.prepare()
            one.send()
            one.take()
        one.shard_prepare()
        one.shard_send()
    dv2 = after(dv2, *[one.payloads for one in first_sums])
    dkq = held2[0]
    ddelta, dcum, drow = (jnp.concatenate([p, q], axis=0) for p, q in zip(held1[2:5], held2[2:5]))
    flow = jnp.concatenate([held1[5], held2[5]], axis=1)
    dstep, small_step = step_back(step_raw, pars, ddelta, dcum, drow, flow)
    dx, edge, dtap = unconv(rest, taps, match, dv1, dv2, dkq)
    rim_grad = shifted(edge[:HALO], "shard", -1)
    mended = edge[HALO:] + rim_grad
    dx = lax.dynamic_update_slice(dx, mended.astype(bf16), (length - HALO, 0))
    rest_most = jnp.maximum(jnp.maximum(jnp.max(dtap[KW + 1]), jnp.max(small_step[2])), jnp.max(jnp.abs(mended)))
    rest_most = jnp.maximum(rest_most, exchanged(jnp.full((8, 128), rest_most), "dp", 1)[0, 0])
    rest_bound = norm_bound * rest_most
    drest = jnp.concatenate([dx, dstep], axis=1)
    drest_both = both_cores(drest)
    middle = (drest.shape[1] // 256) * 128
    rest_sums[0].prepare(drest_both[:, :middle], rest_bound)
    rest_sums[1].prepare(drest_both[:, middle:], rest_bound)
    for one in rest_sums:
        one.send()
    drest = after(drest, *[one.payload for one in rest_sums])
    back_normed = back_normed + lax.dot_general(drest, rest_w, NT, preferred_element_type=f32)
    sent = [one.got for one in rest_sums]
    ready = [one.payload for one in rest_sums]
    grad_outputs = out_sum.shard_take(ready)
    grad_gate = gate_sum.shard_take(ready)
    for one in rest_sums:
        one.take(back_normed, grad_outputs, grad_gate)
        while one.more():
            one.prepare()
            one.send()
            one.take()
        one.shard_prepare()
        one.shard_send()
    sent = [one.payloads for one in rest_sums]
    grad_rest = [one.shard_take() for one in rest_sums]
    grad_inputs = jnp.concatenate([grad_gate] + grad_rest, axis=1)

    own_inv = inv[HALO:]
    scaled = hidden_in * own_inv
    gained = back_normed * param_prenorm
    hidden_grad = cotangent + own_inv * (
        gained - scaled * jnp.mean(gained * scaled, axis=1, keepdims=True)
    )
    grad_prenorm = jnp.sum(back_normed * scaled, axis=0)

    pieces = [
        grad_prenorm,
        dtap[:KW].reshape(-1),
        dtap[KW],
        small_step[0],
        small_step[1],
        jnp.sum(small[1].reshape(HEADS, HEAD_DIM), axis=1),
        small[0],
    ]
    flat = after(jnp.concatenate(pieces), sent)
    count = flat.shape[0]
    lines = -(-count // 1024) * 8
    total = summed(jnp.pad(flat, (0, lines * 128 - count)).reshape(lines, 128)).reshape(-1)
    found, at = [], 0
    for piece in pieces:
        found.append(total[at : at + piece.shape[0]])
        at += piece.shape[0]
    grad_prenorm, grad_kernel, grad_offsets, grad_timestep, grad_decays, grad_direct, grad_gating = found
    grad_kernel = grad_kernel.reshape(KW, CH)

    params = (
        param_prenorm, param_inputs, param_kernel, param_offsets, param_timestep, param_decays,
        param_direct, param_gating, param_outputs,
    )
    moments = (
        moment_prenorm, moment_inputs, moment_kernel, moment_offsets, moment_timestep, moment_decays,
        moment_direct, moment_gating, moment_outputs,
    )
    squares = (
        square_prenorm, square_inputs, square_kernel, square_offsets, square_timestep, square_decays,
        square_direct, square_gating, square_outputs,
    )
    grads = (
        grad_prenorm, grad_inputs, grad_kernel, grad_offsets, grad_timestep, grad_decays,
        grad_direct, grad_gating, grad_outputs,
    )
    updated = [
        adamw(params[i], grads[i], moments[i], squares[i], rate_table[i], shrink_table[i])
        for i in range(9)
    ]
    return (
        (block_out, hidden_grad)
        + grads
        + tuple(u[0] for u in updated)
        + tuple(u[1] for u in updated)
        + tuple(u[2] for u in updated)
    )


def solution(mesh):
    rows = P(("dp", "shard"), None)
    member = (P(), rows, P(), P(), P(), P(), P(), P(), rows)

    return jax.shard_map(
        shards,
        mesh=mesh,
        in_specs=(rows, rows, P(("dp", "shard"))) + member * 3,
        out_specs=(rows, rows) + member * 4,
        check_vma=False,
    )
```

time: 2090 us -> 797 us (0.38)
  waiting for transfers between devices: 1030 us -> 192 us
  local copies, waits for them, and re-layouts: 463 us -> 89.5 us
  matrix products: 314 us -> 99.9 us
  Pallas kernels: 0 us -> 186 us
  other arithmetic: 221 us -> 102 us
  starting transfers between devices: 7.27 us -> 80.9 us
    reduce_scatter x4 -> x0, waiting for transfers between devices: 475 us -> none  [the longest x1 214 us: shards(): lax.psum_scatter(grad_in_local, 'dp', scatter_dimension=0, tiled=True)]
    all_gather x6 -> x3, waiting for transfers between devices: 431 us -> 48.1 us  [the longest x1 35.9 us: shards(): lax.all_gather(shard_gathered(own_inputs[:, :DI]), 'dp', axis=0, tiled=True)]
    dynamic_update_slice x12 -> x6, local copies, waits for them, and re-layouts: 278 us -> 0.15 us  [shard_gathered(): held = lax.dynamic_update_slice(held, part, ((here ^ k) * rows, 0))]
    dot_general x37 -> x14, matrix products: 314 us -> 99.9 us  [the longest x4 22.3 us: send(): lax.dot_general(self.held, self.rhs, TOKENS, preferred_element_type=f32)]
    pallas_call x0 -> x8, Pallas kernels: none -> 186 us  [the longest x2 97 us: back_local(): pl.pallas_call(functools.partial(back_kernel, last == NG), grid=(groups,)...]
    ppermute x0 -> x38, waiting for transfers between devices: none -> 125 us  [the longest x33 123 us: exchanged(): lax.ppermute(value, axis, [(i, i ^ by) for i in range(lax.axis_size(axis))])]
    psum x1 -> x0, waiting for transfers between devices: 119 us -> none  [shards(): lax.psum((grad_prenorm_local, back_small[0], back_small[1], back_small[2]...]
    reduce_sum x12 -> x2, other arithmetic: 59.2 us -> 1.66 us  [the longest x1 1.36 us: shards(): jnp.sum(small[1].reshape(HEADS, HEAD_DIM), axis=1)]
  transfers between devices with their start and end apart: 14 -> 49, of which waited for: 11 -> 19; matrix products, arithmetic and copies ran while one was open for 5% -> 31% of each run, Pallas kernels for 0% -> 18%
where the time goes in v1:
time: 797 us; the launch traced here: 786 us
  waiting for transfers between devices  192 us (24%)
  Pallas kernels  186 us (23%)
  other arithmetic  102 us (13%)
  matrix products  99.9 us (13%)
  local copies, waits for them, and re-layouts  89.5 us (11%)
  starting transfers between devices  80.9 us (10%)
  between operations  36.2 us (5%)
    ppermute x33, waiting for transfers between devices, exchanged(): lax.ppermute(value, axis, [(i, i ^ by) for i in range(lax.axis_size(axis))])  123 us
    pallas_call x2, Pallas kernels, back_local(): pl.pallas_call(functools.partial(back_kernel, last == NG), grid=(groups,)...  97 us
    ppermute x33, starting transfers between devices, exchanged(): lax.ppermute(value, axis, [(i, i ^ by) for i in range(lax.axis_size(axis))])  48.7 us
    all_gather x1, waiting for transfers between devices, shards(): lax.all_gather(shard_gathered(own_inputs[:, :DI]), 'dp', axis=0, tiled=True)  35.9 us
    ppermute x8, starting transfers between devices, shifted(): return lax.ppermute(value, axis, pairs)  24.2 us
    dot_general x4, matrix products, send(): lax.dot_general(self.held, self.rhs, TOKENS, preferred_element_type=f32)  22.3 us
    pallas_call x1, Pallas kernels, unconv(): pl.pallas_call(unconv_kernel, grid=(CH // TILE,), in_specs=[pl.BlockSpec(...  21.6 us
    pallas_call x1, Pallas kernels, gate(): pl.pallas_call(gate_kernel, grid=(length // tile,), in_specs=[big, big, b...  20.4 us
  transfers between devices with their start and end apart: 49, of which 19 were waited for; matrix products, arithmetic and copies ran while one was open for 31% of the time, Pallas kernels for 18%

profile of v1, /device:TPU:0, one launch (start us, length us, event | category | flops | bytes accessed | tf_op | source)
XLA Modules:
  0.0 786.0 jit_solution(14004398209453246155)
XLA Ops:
  15.4 10.0 %collective-permute-done.6 = bf16[96,1536]{1,0:T(8,128)(2,1)S(1)} collective-permute-done((bf16[96,1536]{1,0:T(8,128)(2,1)S(1)}, bf16[96,1536]{1,0:T(8,128)(2,1)S(1)}, u32[]{:S(2)}, u32[]{:S(2)}) %collective-permute-start.6) | collective-permute-done | bytes 294944 | tf_op jit(solution)/shard_map/ppermute | solution.py:719
  25.4 14.4 %collective-permute-done.7 = bf16[96,1536]{1,0:T(8,128)(2,1)S(1)} collective-permute-done((bf16[96,1536]{1,0:T(8,128)(2,1)S(1)}, bf16[96,1536]{1,0:T(8,128)(2,1)S(1)}, u32[]{:S(2)}, u32[]{:S(2)}) %collective-permute-start.7) | collective-permute-done | bytes 294944 | tf_op jit(solution)/shard_map/ppermute | solution.py:719
  41.1 9.1 %collective-permute-start.3 = (bf16[48,3072]{1,0:T(8,128)(2,1)S(1)}, bf16[48,3072]{1,0:T(8,128)(2,1)S(1)}, u32[]{:S(2)}, u32[]{:S(2)}) collective-permute-start(bf16[48,3072]{1,0:T(8,128)(2,1)S(1)} %get-tuple-element.229), channel_id=1, source_target_pairs={{0,1},{1,0},{2,3},{3,2},{4,5},{5,4},{6,7},{7,6},{8,9},{9,8},{10,11... | collective-permute-start | bytes 884744 | tf_op jit(solution)/shard_map/ppermute | solution.py:719
  52.7 18.1 %collective-permute-done.3 = bf16[48,3072]{1,0:T(8,128)(2,1)S(1)} collective-permute-done((bf16[48,3072]{1,0:T(8,128)(2,1)S(1)}, bf16[48,3072]{1,0:T(8,128)(2,1)S(1)}, u32[]{:S(2)}, u32[]{:S(2)}) %collective-permute-start.3) | collective-permute-done | bytes 294944 | tf_op jit(solution)/shard_map/ppermute | solution.py:719
  70.8 16.0 %collective-permute-done.4 = bf16[48,3072]{1,0:T(8,128)(2,1)S(1)} collective-permute-done((bf16[48,3072]{1,0:T(8,128)(2,1)S(1)}, bf16[48,3072]{1,0:T(8,128)(2,1)S(1)}, u32[]{:S(2)}, u32[]{:S(2)}) %collective-permute-start.4) | collective-permute-done | bytes 294944 | tf_op jit(solution)/shard_map/ppermute | solution.py:719
  88.2 7.6 collective-permute-start
  116.7 12.1 %all-gather.4.cloned.1.call-done = bf16[1536,3376]{1,0:T(8,128)(2,1)} async-done(((bf16[48,3376]{1,0:T(8,128)(2,1)}), bf16[1536,3376]{1,0:T(8,128)(2,1)}) %all-gather.4.cloned.1.call-update) | async-done | bytes 10371088 | tf_op jit(solution)/shard_map/all_gather | solution.py:705
  132.7 9.4 %fusion.50.xv_ref.xk_ref.x_ref = f32[520,3376]{1,0:T(8,128)S(1)} fusion(bf16[520,1536]{1,0:T(8,128)(2,1)} %copy-done.11, bf16[1536,3376]{1,0:T(8,128)(2,1)} %all-gather.4.cloned.1.call-done), kind=kOutput, calls=%fused_computation.199 | convolution fusion | flops 5392957440 | bytes 18990592 | tf_op jit(solution)/shard_map/dot_general | solution.py:924
  152.9 13.2 %conv_state.1 = (f32[512,3072]{1,0:T(8,128)}, f32[512,256]{1,0:T(8,128)}, f32[128,3072]{1,0:T(8,128)}) custom-call(f32[520,3376]{1,0:T(8,128)} %copy-done, f32[520,3376]{1,0:T(8,128)} %copy-done, f32[8,3328]{1,0:T(8,128)} %maximum_maximum_fusion.tv_ref.tk_ref.tap_ref, f32[8,3328]{1,0:T(8,128)} %maximum_maximum_fusion.tv_ref.tk_ref.tap_ref, ...), custom_call_target="tpu_custom_call" | custom-call | flops 2000000000 | bytes 20000000 | tf_op jit(solution)/shard_map/conv_state/pallas_call | solution.py:208
  179.3 19.2 %local_out.1.y_ref = f32[512,3072]{1,0:T(8,128)} custom-call(f32[512,3072]{1,0:T(8,128)} %get-tuple-element.96.v_ref, f32[512,256]{1,0:T(8,128)} %get-tuple-element.97.kq_ref, f32[6,512,8]{2,1,0:T(8,128)} %get-tuple-element.98.delta_ref, f32[6,512,8]{2,1,0:T(8,128)} %get-tuple-element.99.cum_ref, f32[48,512]{1,0:T(8,128)} %get-tuple-element.100.cumt_ref, ...), custom_call_target="tpu_custom_call" | custom-call | flops 2000000000 | bytes 20000000 | tf_op jit(solution)/shard_map/local_out/pallas_call | solution.py:290
  204.5 9.8 %convolution_bitcast_fusion.g_ref = f32[512,3072]{1,0:T(8,128)} fusion(bf16[3072,1536]{1,0:T(8,128)(2,1)} %all-gather.8.cloned.1.call-done, bf16[512,1536]{1,0:T(8,128)(2,1)} %convert_element_type.281), kind=kOutput, calls=%fused_computation.2 | convolution fusion | flops 4831838208 | bytes 17301504 | tf_op jit(solution)/shard_map/dot_general | solution.py:933
  214.4 35.9 %all-gather.6.cloned.1.call-done = bf16[1536,3072]{1,0:T(8,128)(2,1)} async-done(((bf16[192,3072]{1,0:T(8,128)(2,1)}), bf16[1536,3072]{1,0:T(8,128)(2,1)}) %all-gather.6.cloned.1.call-update) | async-done | bytes 9437200 | tf_op jit(solution)/shard_map/all_gather | solution.py:864
  255.7 10.9 %fusion.35.z_ref = f32[512,3072]{1,0:T(8,128)} fusion(bf16[1536,3072]{1,0:T(8,128)(2,1)} %all-gather.6.cloned.1.call-done, bf16[520,1536]{1,0:T(8,128)(2,1)S(1)} %copy-done.12), kind=kOutput, calls=%fused_computation.193 | convolution fusion | flops 4831838208 | bytes 17301504 | tf_op jit(solution)/shard_map/dot_general | solution.py:932
  273.7 20.4 %gate.1 = (bf16[512,3072]{1,0:T(8,128)(2,1)}, f32[512,3072]{1,0:T(8,128)}, bf16[512,3072]{1,0:T(8,128)(2,1)}, f32[128,3072]{1,0:T(8,128)}, f32[8,3072]{1,0:T(8,128)}) custom-call(f32[512,3072]{1,0:T(8,128)} %local_out.1.y_ref, f32[512,3072]{1,0:T(8,128)} %get-tuple-element.96.v_ref, f32[512,3072]{1,0:T(8,128)} %fusion.35.z_ref, ...), custom_call_target="tpu_custom_call" | custom-call | flops 1000000000 | bytes 40000000 | tf_op jit(solution)/shard_map/gate/pallas_call | solution.py:370
  302.7 10.3 %convolution_add_fusion.1 = f32[512,1536]{1,0:T(8,128)} fusion(f32[512,1536]{1,0:T(8,128)S(1)} %copy-done.1, bf16[512,3072]{1,0:T(8,128)(2,1)S(1)} %copy-done.19, bf16[3072,1536]{1,0:T(8,128)(2,1)} %all-gather.8.cloned.1.call-done), kind=kOutput, calls=%fused_computation.10 | convolution fusion | flops 4832624640 | bytes 18874368 | tf_op jit(solution)/shard_map/dot_general | solution.py:941
  344.3 10.6 %pad_maximum_fusion.6 = bf16[1024,1536]{1,0:T(8,128)(2,1)S(1)} fusion(bf16[512,1536]{1,0:T(8,128)(2,1)} %collective-permute-done.15, bf16[512,384]{1,0:T(8,128)(2,1)S(1)} %copy-done.24, bf16[512,384]{1,0:T(8,128)(2,1)S(1)} %copy-done.25, bf16[512,384]{1,0:T(8,128)(2,1)S(1)} %copy-done.26, bf16[512,384]{1,0:T(8,128)(2,1)S(1)} %get-tuple-element.197), kind=kLoop, calls=%fused_computation.15 | loop fusion | flops 15728640 | bytes 6291456 | tf_op jit(solution)/shard_map/concatenate | solution.py:742
  383.8 48.4 %back_local.2 = (f32[512,1536]{1,0:T(8,128)}, f32[512,256]{1,0:T(8,128)}, f32[512,128]{1,0:T(8,128)}, f32[3,512,8]{2,1,0:T(8,128)}, f32[3,512,8]{2,1,0:T(8,128)}, /*index=5*/f32[24,512]{1,0:T(8,128)}, f32[8,1536]{1,0:T(8,128)}) custom-call(f32[512,3072]{1,0:T(8,128)} %get-tuple-element.96.v_ref, f32[512,3072]{1,0:T(8,128)} %get-tuple-element.119.dy_ref, ...), custom_call_target="tpu_custom_call" | custom-call | flops 15000000512 | bytes 15000000 | tf_op jit(solution)/shard_map/back_local/pallas_call | solution.py:526
  455.9 48.6 %back_local.3 = (f32[512,1536]{1,0:T(8,128)}, f32[512,256]{1,0:T(8,128)}, f32[512,128]{1,0:T(8,128)}, f32[3,512,8]{2,1,0:T(8,128)}, f32[3,512,8]{2,1,0:T(8,128)}, /*index=5*/f32[24,512]{1,0:T(8,128)}, f32[8,1536]{1,0:T(8,128)}) custom-call(f32[512,3072]{1,0:T(8,128)} %get-tuple-element.96.v_ref, f32[512,3072]{1,0:T(8,128)} %get-tuple-element.119.dy_ref, ...), custom_call_target="tpu_custom_call" | custom-call | flops 15000000512 | bytes 15000000 | tf_op jit(solution)/shard_map/back_local/pallas_call | solution.py:526
  525.8 21.6 %unconv.1 = (bf16[512,3328]{1,0:T(8,128)(2,1)}, f32[16,3328]{1,0:T(8,128)}, f32[8,3328]{1,0:T(8,128)}) custom-call(f32[520,3376]{1,0:T(8,128)} %copy-done, f32[8,3328]{1,0:T(8,128)} %maximum_maximum_fusion.tv_ref.tk_ref.tap_ref, f32[3,512,128]{2,1,0:T(8,128)} %broadcast_in_dim.140.match_ref, f32[512,1536]{1,0:T(8,128)} %get-tuple-element.116.da_ref, ...), custom_call_target="tpu_custom_call" | custom-call | flops 100000000 | bytes 20000000 | tf_op jit(solution)/shard_map/unconv/pallas_call | solution.py:658
  550.4 7.9 %step_back.1 = (bf16[512,48]{1,0:T(8,128)(2,1)}, f32[8,48]{1,0:T(8,128)}) custom-call(f32[512,48]{1,0:T(8,128)} %slice.390.step_ref, f32[8,48]{1,0:T(8,128)} %maximum_maximum_fusion.1.par_ref, f32[6,512,8]{2,1,0:T(8,128)} %copy.93.ddelta_ref, f32[6,512,8]{2,1,0:T(8,128)} %copy.94.dcum_ref, f32[48,512]{1,0:T(8,128)} %pad_maximum_fusion.20.drow_ref, ...), custom_call_target="tpu_custom_call" | custom-call | flops 10000000 | bytes 10000000 | tf_op jit(solution)/shard_map/step_back/pallas_call | solution.py:595
  621.1 23.6 %collective-permute-done.30 = f16[64,3072]{1,0:T(8,128)(2,1)} collective-permute-done((f16[64,3072]{1,0:T(8,128)(2,1)S(1)}, f16[64,3072]{1,0:T(8,128)(2,1)}, u32[]{:S(2)}, u32[]{:S(2)}) %collective-permute-start.30) | collective-permute-done | bytes 393248 | tf_op jit(solution)/shard_map/ppermute | solution.py:719
  646.2 11.4 %multiply_reduce_fusion.1 = (f32[1536]{0:T(1024)}, f32[512]{0:T(512)}, f32[512,1536]{1,0:T(8,128)}) fusion(f32[512,1536]{1,0:T(8,128)S(1)} %copy-done.1, f32[512]{0:T(512)S(1)} %copy-done.67, f32[1536]{0:T(1024)S(1)} %copy-done.50, f32[512,1536]{1,0:T(8,128)} %fusion.51, bf16[512,3376]{1,0:T(8,128)(2,1)S(1)} %copy-done.4, ...), kind=kOutput, calls=%fused_computation.16 | convolution fusion | flops 5315491840 | bytes 23281664 | tf_op jit(solution)/shard_map/dot_general | solution.py:987
  685.5 10.5 %collective-permute-done.33 = f16[400,1712]{1,0:T(8,128)(2,1)} collective-permute-done((f16[400,1712]{1,0:T(8,128)(2,1)}, f16[400,1712]{1,0:T(8,128)(2,1)}, u32[]{:S(2)}, u32[]{:S(2)}) %collective-permute-start.33) | collective-permute-done | bytes 1369632 | tf_op jit(solution)/shard_map/ppermute | solution.py:719
  749.4 11.9 %collective-permute-done.44 = f16[64,1712]{1,0:T(8,128)(2,1)S(1)} collective-permute-done((f16[64,1712]{1,0:T(8,128)(2,1)S(1)}, f16[64,1712]{1,0:T(8,128)(2,1)S(1)}, u32[]{:S(2)}, u32[]{:S(2)}) %collective-permute-start.44) | collective-permute-done | bytes 219168 | tf_op jit(solution)/shard_map/ppermute | solution.py:719
  (476 shorter events, 338.9 us)
Async XLA Ops:
  7.2 121.6 %all-gather.4.cloned.1.call-start = ((), (), s32[]{:S(2)}) async-start(), calls=%async_computation | async-start | bytes 10948608 | tf_op jit(solution)/shard_map/all_gather | solution.py:705
  9.5 189.0 %all-gather.8.cloned.1.call-start = ((), (), s32[]{:S(2)}) async-start(), calls=%async_computation.2 | async-start | bytes 10616832 | tf_op jit(solution)/shard_map/all_gather | solution.py:865
  12.8 27.0 %collective-permute-start.7 = (bf16[96,1536]{1,0:T(8,128)(2,1)S(1)}, bf16[96,1536]{1,0:T(8,128)(2,1)S(1)}, u32[]{:S(2)}, u32[]{:S(2)}) collective-permute-start(bf16[96,1536]{1,0:T(8,128)(2,1)S(1)} %get-tuple-element.192), channel_id=1, source_target_pairs={{0,2},{1,3},{2,0},{3,1},{4,6},{5,7},{6,4},{7,5},{8,10},{9,11},{10,... | collective-permute-start | bytes 884744 | tf_op jit(solution)/shard_map/ppermute | solution.py:719
  40.9 209.4 %all-gather.6.cloned.1.call-start = ((), (), s32[]{:S(2)}) async-start(), calls=%async_computation.1 | async-start | bytes 10616832 | tf_op jit(solution)/shard_map/all_gather | solution.py:864
  41.1 29.7 %collective-permute-start.3 = (bf16[48,3072]{1,0:T(8,128)(2,1)S(1)}, bf16[48,3072]{1,0:T(8,128)(2,1)S(1)}, u32[]{:S(2)}, u32[]{:S(2)}) collective-permute-start(bf16[48,3072]{1,0:T(8,128)(2,1)S(1)} %get-tuple-element.229), channel_id=1, source_target_pairs={{0,1},{1,0},{2,3},{3,2},{4,5},{5,4},{6,7},{7,6},{8,9},{9,8},{10,11... | collective-permute-start | bytes 884744 | tf_op jit(solution)/shard_map/ppermute | solution.py:719
  50.2 36.6 %collective-permute-start.4 = (bf16[48,3072]{1,0:T(8,128)(2,1)S(1)}, bf16[48,3072]{1,0:T(8,128)(2,1)S(1)}, u32[]{:S(2)}, u32[]{:S(2)}) collective-permute-start(bf16[48,3072]{1,0:T(8,128)(2,1)S(1)} %get-tuple-element.229), channel_id=1, source_target_pairs={{0,2},{1,3},{2,0},{3,1},{4,6},{5,7},{6,4},{7,5},{8,10},{9,11},{10,... | collective-permute-start | bytes 884744 | tf_op jit(solution)/shard_map/ppermute | solution.py:719
  51.3 35.5 %collective-permute-start.5 = (bf16[48,3072]{1,0:T(8,128)(2,1)S(1)}, bf16[48,3072]{1,0:T(8,128)(2,1)S(1)}, u32[]{:S(2)}, u32[]{:S(2)}) collective-permute-start(bf16[48,3072]{1,0:T(8,128)(2,1)S(1)} %get-tuple-element.229), channel_id=1, source_target_pairs={{0,3},{1,2},{2,1},{3,0},{4,7},{5,6},{6,5},{7,4},{8,11},{9,10},{10,... | collective-permute-start | bytes 884744 | tf_op jit(solution)/shard_map/ppermute | solution.py:719
  112.6 62.1 %collective-permute-start.2 = (bf16[512,768]{1,0:T(8,128)(2,1)}, bf16[512,768]{1,0:T(8,128)(2,1)}, u32[]{:S(2)}, u32[]{:S(2)}) collective-permute-start(bf16[512,768]{1,0:T(8,128)(2,1)} %pad_maximum_fusion.16), channel_id=1, source_target_pairs={{0,4},{4,0},{8,12},{12,8},{16,20},{20,16},{24,28},{28,24},{1,5},{5... | collective-permute-start | bytes 2359304 | tf_op jit(solution)/shard_map/ppermute | solution.py:719
  168.5 30.0 %collective-permute-start.9 = (bf16[128,3072]{1,0:T(8,128)(2,1)}, bf16[128,3072]{1,0:T(8,128)(2,1)}, u32[]{:S(2)}, u32[]{:S(2)}) collective-permute-start(bf16[128,3072]{1,0:T(8,128)(2,1)} %convert_element_type.284), channel_id=1, source_target_pairs={{0,1},{1,2},{2,3},{4,5},{5,6},{6,7},{8,9},{9,10},{10,11},{12,13},{... | collective-permute-start | bytes 2359304 | tf_op jit(solution)/shard_map/ppermute | solution.py:698
  201.5 48.8 %collective-permute-start.10 = (bf16[128,3072]{1,0:T(8,128)(2,1)}, bf16[128,3072]{1,0:T(8,128)(2,1)}, u32[]{:S(2)}, u32[]{:S(2)}) collective-permute-start(bf16[128,3072]{1,0:T(8,128)(2,1)} %add_convert_fusion.3), channel_id=1, source_target_pairs={{0,1},{1,2},{2,3},{4,5},{5,6},{6,7},{8,9},{9,10},{10,11},{12,13},{... | collective-permute-start | bytes 2359304 | tf_op jit(solution)/shard_map/ppermute | solution.py:698
  294.1 76.3 %collective-permute-start.16 = (bf16[512,3072]{1,0:T(8,128)(2,1)}, bf16[512,3072]{1,0:T(8,128)(2,1)}, u32[]{:S(2)}, u32[]{:S(2)}) collective-permute-start(bf16[512,3072]{1,0:T(8,128)(2,1)} %get-tuple-element.110), channel_id=1, source_target_pairs={{0,4},{4,0},{8,12},{12,8},{16,20},{20,16},{24,28},{28,24},{1,5},{5... | collective-permute-start | bytes 9437192 | tf_op jit(solution)/shard_map/ppermute | solution.py:719
  301.5 42.7 %collective-permute-start.15 = (bf16[512,1536]{1,0:T(8,128)(2,1)}, bf16[512,1536]{1,0:T(8,128)(2,1)}, u32[]{:S(2)}, u32[]{:S(2)}) collective-permute-start(bf16[512,1536]{1,0:T(8,128)(2,1)} %pad_maximum_fusion.12), channel_id=1, source_target_pairs={{0,4},{4,0},{8,12},{12,8},{16,20},{20,16},{24,28},{28,24},{1,5},{5... | collective-permute-start | bytes 4718600 | tf_op jit(solution)/shard_map/ppermute | solution.py:719
  342.7 39.5 %collective-permute-start.14 = (bf16[128,3072]{1,0:T(8,128)(2,1)S(1)}, bf16[128,3072]{1,0:T(8,128)(2,1)S(1)}, u32[]{:S(2)}, u32[]{:S(2)}) collective-permute-start(bf16[128,3072]{1,0:T(8,128)(2,1)S(1)} %add_convert_fusion), channel_id=1, source_target_pairs={{1,0},{2,1},{3,2},{5,4},{6,5},{7,6},{9,8},{10,9},{11,10},{13,12},{... | collective-permute-start | bytes 2359304 | tf_op jit(solution)/shard_map/ppermute | solution.py:698
  362.1 72.9 %collective-permute-start.18 = (f16[784,1536]{1,0:T(8,128)(2,1)}, f16[784,1536]{1,0:T(8,128)(2,1)}, u32[]{:S(2)}, u32[]{:S(2)}) collective-permute-start(f16[784,1536]{1,0:T(8,128)(2,1)} %select_convert_fusion.1), channel_id=1, source_target_pairs={{0,8},{4,12},{8,0},{12,4},{16,24},{20,28},{24,16},{28,20},{1,9},{5... | collective-permute-start | bytes 7225352 | tf_op jit(solution)/shard_map/ppermute | solution.py:719
  376.8 69.1 %collective-permute-start.19 = (f16[400,3072]{1,0:T(8,128)(2,1)}, f16[400,3072]{1,0:T(8,128)(2,1)}, u32[]{:S(2)}, u32[]{:S(2)}) collective-permute-start(f16[400,3072]{1,0:T(8,128)(2,1)} %select_convert_fusion), channel_id=1, source_target_pairs={{0,16},{4,20},{8,24},{12,28},{16,0},{20,4},{24,8},{28,12},{1,17},{... | collective-permute-start | bytes 7372808 | tf_op jit(solution)/shard_map/ppermute | solution.py:719
  444.4 63.0 %collective-permute-start.20 = (f16[400,1536]{1,0:T(8,128)(2,1)}, f16[400,1536]{1,0:T(8,128)(2,1)}, u32[]{:S(2)}, u32[]{:S(2)}) collective-permute-start(f16[400,1536]{1,0:T(8,128)(2,1)} %fusion.7), channel_id=1, source_target_pairs={{0,16},{4,20},{8,24},{12,28},{16,0},{20,4},{24,8},{28,12},{1,17},{... | collective-permute-start | bytes 3686408 | tf_op jit(solution)/shard_map/ppermute | solution.py:719
  455.4 63.5 %collective-permute-start.21 = (f16[208,3072]{1,0:T(8,128)(2,1)}, f16[208,3072]{1,0:T(8,128)(2,1)}, u32[]{:S(2)}, u32[]{:S(2)}) collective-permute-start(f16[208,3072]{1,0:T(8,128)(2,1)} %fusion.5), channel_id=1, source_target_pairs={{0,8},{4,12},{8,0},{12,4},{16,24},{20,28},{24,16},{28,20},{1,9},{5... | collective-permute-start | bytes 3833864 | tf_op jit(solution)/shard_map/ppermute | solution.py:719
  581.8 81.4 %collective-permute-start.26 = (f16[112,1536]{1,0:T(8,128)(2,1)}, f16[112,1536]{1,0:T(8,128)(2,1)}, u32[]{:S(2)}, u32[]{:S(2)}) collective-permute-start(f16[112,1536]{1,0:T(8,128)(2,1)} %get-tuple-element.210), channel_id=1, source_target_pairs={{0,1},{1,0},{2,3},{3,2},{4,5},{5,4},{6,7},{7,6},{8,9},{9,8},{10,11... | collective-permute-start | bytes 1032200 | tf_op jit(solution)/shard_map/ppermute | solution.py:719
  585.1 80.0 %collective-permute-start.27 = (f16[112,1536]{1,0:T(8,128)(2,1)}, f16[112,1536]{1,0:T(8,128)(2,1)}, u32[]{:S(2)}, u32[]{:S(2)}) collective-permute-start(f16[112,1536]{1,0:T(8,128)(2,1)} %get-tuple-element.209), channel_id=1, source_target_pairs={{0,2},{1,3},{2,0},{3,1},{4,6},{5,7},{6,4},{7,5},{8,10},{9,11},{10,... | collective-permute-start | bytes 1032200 | tf_op jit(solution)/shard_map/ppermute | solution.py:719
  588.0 79.0 %collective-permute-start.28 = (f16[112,1536]{1,0:T(8,128)(2,1)}, f16[112,1536]{1,0:T(8,128)(2,1)}, u32[]{:S(2)}, u32[]{:S(2)}) collective-permute-start(f16[112,1536]{1,0:T(8,128)(2,1)} %get-tuple-element.208), channel_id=1, source_target_pairs={{0,3},{1,2},{2,1},{3,0},{4,7},{5,6},{6,5},{7,4},{8,11},{9,10},{10,... | collective-permute-start | bytes 1032200 | tf_op jit(solution)/shard_map/ppermute | solution.py:719
  593.5 51.2 %collective-permute-start.30 = (f16[64,3072]{1,0:T(8,128)(2,1)S(1)}, f16[64,3072]{1,0:T(8,128)(2,1)}, u32[]{:S(2)}, u32[]{:S(2)}) collective-permute-start(f16[64,3072]{1,0:T(8,128)(2,1)S(1)} %copy-done.39), channel_id=1, source_target_pairs={{0,2},{1,3},{2,0},{3,1},{4,6},{5,7},{6,4},{7,5},{8,10},{9,11},{10,... | collective-permute-start | bytes 1179656 | tf_op jit(solution)/shard_map/ppermute | solution.py:719
  617.1 44.2 %collective-permute-start.31 = (f16[64,3072]{1,0:T(8,128)(2,1)S(1)}, f16[64,3072]{1,0:T(8,128)(2,1)S(1)}, u32[]{:S(2)}, u32[]{:S(2)}) collective-permute-start(f16[64,3072]{1,0:T(8,128)(2,1)S(1)} %copy-done.38), channel_id=1, source_target_pairs={{0,3},{1,2},{2,1},{3,0},{4,7},{5,6},{6,5},{7,4},{8,11},{9,10},{10,... | collective-permute-start | bytes 1179656 | tf_op jit(solution)/shard_map/ppermute | solution.py:719
  644.7 30.3 %collective-permute-start.25 = (f16[400,1664]{1,0:T(8,128)(2,1)}, f16[400,1664]{1,0:T(8,128)(2,1)}, u32[]{:S(2)}, u32[]{:S(2)}) collective-permute-start(f16[400,1664]{1,0:T(8,128)(2,1)} %fusion.2), channel_id=1, source_target_pairs={{0,8},{4,12},{8,0},{12,4},{16,24},{20,28},{24,16},{28,20},{1,9},{5... | collective-permute-start | bytes 3993608 | tf_op jit(solution)/shard_map/ppermute | solution.py:719
  661.3 34.7 %collective-permute-start.33 = (f16[400,1712]{1,0:T(8,128)(2,1)}, f16[400,1712]{1,0:T(8,128)(2,1)}, u32[]{:S(2)}, u32[]{:S(2)}) collective-permute-start(f16[400,1712]{1,0:T(8,128)(2,1)} %fusion.3), channel_id=1, source_target_pairs={{0,16},{4,20},{8,24},{12,28},{16,0},{20,4},{24,8},{28,12},{1,17},{... | collective-permute-start | bytes 4108808 | tf_op jit(solution)/shard_map/ppermute | solution.py:719
  (127 other events, 2101.8 us)
Sparse Core Ops, SparseCore 0:
  11.4 117.3 all-gather.3
  131.3 57.7 all-gather.7
  191.6 58.6 all-gather.5

commit v2 on v1

--- a/solution.py
+++ b/solution.py
@@ -21,6 +21,7 @@
 GW = GH * HEAD_DIM
 NG = HEADS // GH
 HALO = 8
+PAD = 16
 TILE = 256
 
 bf16 = jnp.bfloat16
@@ -93,7 +94,7 @@
     step_ref, par_ref, mask_ref, delta_ref, cum_ref, cumt_ref, infc_ref, tailc_ref, tailn_ref,
     taild_ref, infd_ref, keep_ref, factor_ref,
 ):
-    length = step_ref.shape[0]
+    length = mask_ref.shape[0]
     count = length // Q
     tri = (iota((Q, Q), 0) >= iota((Q, Q), 1)).astype(f32)
     eye = (iota((HEADS, HEADS), 0) == iota((HEADS, HEADS), 1)).astype(f32)
@@ -103,7 +104,7 @@
     keeps = []
     for c in range(count):
         rows = slice(c * Q, (c + 1) * Q)
-        delta = softplus(step_ref[rows, :] + par_ref[0:1, :])
+        delta = softplus(step_ref[pl.ds(HALO + c * Q, Q), :HEADS] + par_ref[0:1, :])
         cum = dotf(tri, -delta * rate)
         cumt_ref[:, rows] = dotf(eye, cum, NT)
         last = cum[Q - 1 : Q, :]
@@ -139,20 +140,32 @@
     factor_ref[...] = dotf(jnp.where(line == 0, factor, 0.0), spread)
 
 
-def prep(step_raw, pars, mask):
-    length = step_raw.shape[0]
+def whole(array):
+    return pl.BlockSpec(array.shape, lambda i: (0,) * array.ndim)
+
+
+def steps_of(rest):
+    return pl.BlockSpec((rest.shape[0], 128), lambda i: (0, CH // 128))
+
+
+def prep(rest, pars, mask):
+    length = mask.shape[0]
     cols = jax.ShapeDtypeStruct((NG, length, GH), f32)
     wide = jax.ShapeDtypeStruct((8, DI), f32)
+    shapes = (
+        cols, cols, jax.ShapeDtypeStruct((HEADS, length), f32), cols, cols, cols, cols,
+        jax.ShapeDtypeStruct((length, HEADS), f32), wide, wide,
+    )
     return pl.pallas_call(
         prep_kernel,
-        out_shape=(
-            cols, cols, jax.ShapeDtypeStruct((HEADS, length), f32), cols, cols, cols, cols,
-            jax.ShapeDtypeStruct((length, HEADS), f32), wide, wide,
-        ),
+        grid=(1,),
+        in_specs=[steps_of(rest), whole(pars), whole(mask)],
+        out_specs=tuple(whole(shape) for shape in shapes),
+        out_shape=shapes,
         compiler_params=params(),
         cost_estimate=pl.CostEstimate(flops=10**7, bytes_accessed=10**7, transcendentals=10**5),
         name="prep",
-    )(step_raw, pars, mask)
+    )(rest, pars, mask)
 
 
 def conv_sum(x_ref, tap_ref, match_ref, start, rows, cols):
@@ -386,7 +399,7 @@
         out_shape=(
             jax.ShapeDtypeStruct((length, DI), bf16),
             jax.ShapeDtypeStruct((length, DI), f32),
-            jax.ShapeDtypeStruct((length, DI), bf16),
+            jax.ShapeDtypeStruct((length + PAD, DI), bf16),
             jax.ShapeDtypeStruct((STATE, DI), f32),
             jax.ShapeDtypeStruct((8, DI), f32),
         ),
@@ -555,60 +568,79 @@
         cost_estimate=pl.CostEstimate(
             flops=groups * 5 * 10**9, bytes_accessed=groups * 5 * 10**6, transcendentals=groups * 10**6
         ),
-        name="back_local",
+        name="back_first" if first == 0 else "back_second",
     )(v, dy, kq, delta, cum, cumt, infc, tailc, tailn, keep, inc, dout, dirx, segc, segr, *held)
 
 
-def step_kernel(step_ref, par_ref, ddelta_ref, dcum_ref, drow_ref, flow_ref, dstep_ref, small_ref):
-    length = step_ref.shape[0]
+def step_kernel(
+    step_ref, par_ref, ddelta_a, ddelta_b, dcum_a, dcum_b, drow_a, drow_b, flow_a, flow_b,
+    dstep_ref, small_ref,
+):
+    length = ddelta_a.shape[1]
+    half = ddelta_a.shape[0]
     upper = (iota((Q, Q), 0) <= iota((Q, Q), 1)).astype(f32)
     eye = (iota((Q, Q), 0) == iota((Q, Q), 1)).astype(f32)
     last = iota((Q, 1), 0) == Q - 1
     rate = jnp.exp(par_ref[1:2, :])
-    flows = dotf(flow_ref[...], head_onehot(), NT)
+    spread = head_onehot()
+    wide = half * GW
+    flows = dotf(flow_a[...], spread[:, :wide], NT) + dotf(flow_b[...], spread[:, wide:], NT)
+    top = half * GH
+    rise = (iota((HEADS, top), 0) == iota((HEADS, top), 1)).astype(f32)
+    fall = (iota((HEADS, HEADS - top), 0) == iota((HEADS, HEADS - top), 1) + top).astype(f32)
     times = jnp.zeros((1, HEADS), f32)
     decays = jnp.zeros((1, HEADS), f32)
     most = jnp.zeros((1, HEADS), f32)
+    dstep_ref[...] = jnp.zeros_like(dstep_ref)
     for c in range(length // Q):
         rows = slice(c * Q, (c + 1) * Q)
         ddelta = jnp.zeros((Q, HEADS), f32)
-        dcum = -dotf(eye, drow_ref[:, rows], NT)
+        turned = dotf(rise, drow_a[:, rows]) + dotf(fall, drow_b[:, rows])
+        dcum = -dotf(eye, turned, NT)
         for g in range(NG):
             place = (iota((GH, HEADS), 0) + g * GH == iota((GH, HEADS), 1)).astype(f32)
-            ddelta = ddelta + dotf(ddelta_ref[g, rows, :], place)
-            dcum = dcum + dotf(dcum_ref[g, rows, :], place)
+            one, two = (ddelta_a[g, rows, :], dcum_a[g, rows, :]) if g < half else (
+                ddelta_b[g - half, rows, :], dcum_b[g - half, rows, :]
+            )
+            ddelta = ddelta + dotf(one, place)
+            dcum = dcum + dotf(two, place)
         dcum = dcum + jnp.where(last, flows[c : c + 1, :], 0.0)
-        x = step_ref[rows, :] + par_ref[0:1, :]
+        x = step_ref[pl.ds(HALO + c * Q, Q), :HEADS] + par_ref[0:1, :]
         dlog = dotf(upper, dcum) * rate
         decays = decays - jnp.sum(dlog * softplus(x), axis=0, keepdims=True)
         dstep = (ddelta - dlog) * sigmoid(x)
         times = times + jnp.sum(dstep, axis=0, keepdims=True)
         most = jnp.maximum(most, jnp.max(jnp.abs(dstep), axis=0, keepdims=True))
-        dstep_ref[rows, :] = dstep.astype(bf16)
+        dstep_ref[rows, :HEADS] = dstep.astype(bf16)
+    dstep_ref[pl.ds(length, PAD), :HEADS] = jnp.broadcast_to(most * 1.01, (PAD, HEADS)).astype(bf16)
     small_ref[...] = jnp.zeros_like(small_ref)
     small_ref[0:1, :] = times
     small_ref[1:2, :] = decays
-    small_ref[2:3, :] = most
-
-
-def step_back(step_raw, pars, ddelta, dcum, drow, flow):
+
+
+def step_back(rest, pars, first, second):
+    length = first[0].shape[1]
+    arrays = [part for both in zip(first, second) for part in both]
+    shapes = (
+        jax.ShapeDtypeStruct((length + PAD, 128), bf16),
+        jax.ShapeDtypeStruct((8, HEADS), f32),
+    )
     return pl.pallas_call(
         step_kernel,
-        out_shape=(
-            jax.ShapeDtypeStruct(step_raw.shape, bf16),
-            jax.ShapeDtypeStruct((8, HEADS), f32),
-        ),
+        grid=(1,),
+        in_specs=[steps_of(rest), whole(pars)] + [whole(array) for array in arrays],
+        out_specs=tuple(whole(shape) for shape in shapes),
+        out_shape=shapes,
         compiler_params=params(),
         cost_estimate=pl.CostEstimate(flops=10**7, bytes_accessed=10**7, transcendentals=10**5),
         name="step_back",
-    )(step_raw, pars, ddelta, dcum, drow, flow)
-
-
-def unconv_kernel(x_ref, tap_ref, match_ref, da_ref, db_ref, dkq_ref, dx_ref, edge_ref, dtap_ref, *held):
-    length = dx_ref.shape[0]
+    )(rest, pars, *arrays)
+
+
+def unconv_kernel(mixed, x_ref, tap_ref, match_ref, dv_ref, dkq_ref, dx_ref, edge_ref, dtap_ref, *held):
+    length = match_ref.shape[1]
     count = length // Q
-    step = pl.program_id(0)
-    half = DI // TILE // 2
+    wide = pl.program_id(0) < mixed
     for buf in held:
         buf[0:HALO, :] = jnp.zeros((HALO, TILE), f32)
         buf[HALO + length :, :] = jnp.zeros((HALO, TILE), f32)
@@ -619,9 +651,7 @@
             rows = slice(c * Q, (c + 1) * Q)
             s = conv_sum(x_ref, tap_ref, match_ref, c * Q, Q, cols)
             sig = sigmoid(s)
-            dm = jnp.where(
-                step < half, da_ref[rows, cols], jnp.where(step < 2 * half, db_ref[rows, cols], dkq_ref[rows, cols])
-            )
+            dm = jnp.where(wide, dv_ref[rows, cols], dkq_ref[rows, cols])
             ds = dm * (sig * (1.0 + s * (1.0 - sig)))
             sums[KW] = sums[KW] + jnp.sum(ds, axis=0, keepdims=True)
             for k in range(KW):
@@ -651,19 +681,20 @@
     dtap_ref[KW + 2 :, :] = jnp.zeros((8 - KW - 2, TILE), f32)
 
 
-def unconv(rest, taps, match, dva, dvb, dkq):
+def unconv(first, rest, taps, match, dv, dkq):
     length = match.shape[1]
     high = length + HALO
-    half = DI // TILE // 2
+    mixed = dv.shape[1] // TILE
+    tiles = mixed if dkq is None else mixed + 1
+    lone = dv if dkq is None else dkq
     return pl.pallas_call(
-        unconv_kernel,
-        grid=(CH // TILE,),
+        functools.partial(unconv_kernel, mixed),
+        grid=(tiles,),
         in_specs=[
-            pl.BlockSpec((high, TILE), lambda j: (0, j)),
-            pl.BlockSpec((8, TILE), lambda j: (0, j)),
+            pl.BlockSpec((high, TILE), lambda j: (0, j + first)),
+            pl.BlockSpec((8, TILE), lambda j: (0, j + first)),
             pl.BlockSpec((KW - 1, length, 128), lambda j: (0, 0, 0)),
-            pl.BlockSpec((length, TILE), lambda j: (0, jnp.minimum(j, half - 1))),
-            pl.BlockSpec((length, TILE), lambda j: (0, jnp.clip(j - half, 0, half - 1))),
+            pl.BlockSpec((length, TILE), lambda j: (0, jnp.minimum(j, mixed - 1))),
             pl.BlockSpec((length, TILE), lambda j: (0, 0)),
         ],
         out_specs=(
@@ -672,15 +703,14 @@
             pl.BlockSpec((8, TILE), lambda j: (0, j)),
         ),
         out_shape=(
-            jax.ShapeDtypeStruct((length, CH), bf16),
-            jax.ShapeDtypeStruct((2 * HALO, CH), f32),
-            jax.ShapeDtypeStruct((8, CH), f32),
+            jax.ShapeDtypeStruct((length + PAD, tiles * TILE), bf16),
+            jax.ShapeDtypeStruct((2 * HALO, tiles * TILE), f32),
+            jax.ShapeDtypeStruct((8, tiles * TILE), f32),
         ),
         scratch_shapes=[pltpu.VMEM((length + 2 * HALO, TILE), f32) for _ in range(KW)],
         compiler_params=params(),
-        cost_estimate=pl.CostEstimate(flops=10**8, bytes_accessed=2 * 10**7, transcendentals=2 * 10**6),
-        name="unconv",
-    )(rest, taps, match, dva, dvb, dkq)
+        cost_estimate=pl.CostEstimate(flops=10**8, bytes_accessed=10**7, transcendentals=10**6),
+    )(rest, taps, match, dv, lone)
 
 
 def adamw(param, grad, moment, square, rate, shrink):
@@ -702,7 +732,7 @@
 
 
 def gathered(value):
-    return lax.all_gather(value, ("dp", "shard"), axis=0, tiled=True)
+    return lax.all_gather(value, "dp", axis=0, tiled=True)
 
 
 def shard_gathered(value):
@@ -719,9 +749,6 @@
     return lax.ppermute(value, axis, [(i, i ^ by) for i in range(lax.axis_size(axis))])
 
 
-PAD = 16
-
-
 def relative(value, block, core):
     base = lax.axis_index("dp") // 2
     length = value.shape[0]
@@ -735,11 +762,9 @@
     return jnp.concatenate([value, exchanged(value, "dp", 1)], axis=0)
 
 
-def sum_columns(value, block):
+def own_and_partner(value, block):
     core = lax.axis_index("dp") % 2
-    theirs = jnp.concatenate(relative(value, block, 1 - core), axis=1)
-    mine = jnp.concatenate(relative(value, block, core), axis=1)
-    return jnp.concatenate([mine, exchanged(theirs, "dp", 1)], axis=0)
+    return relative(value, block, core), relative(value, block, 1 - core)
 
 
 def exponent(bound):
@@ -752,7 +777,7 @@
 
 
 def decoded(payload, rows):
-    power = payload[rows, 0].astype(f32)
+    power = payload[rows : rows + 1].astype(f32)
     return payload.astype(f32) * jnp.exp2(power - 15.0), power
 
 
@@ -760,35 +785,37 @@
     return lax.optimization_barrier((value, earlier))[0]
 
 
+def split_plan(order):
+    kept, sends = [0], []
+    for bit in reversed(order):
+        send = [j ^ (1 << bit) for j in kept]
+        sends.insert(0, send)
+        kept = kept + send
+    return kept, sends
+
+
+def columns_of(blocks, order):
+    kept, sends = split_plan(order)
+    zeros = jnp.zeros((blocks[0].shape[0], PAD), bf16)
+    return (
+        jnp.concatenate([blocks[j] for j in sends[0]] + [zeros], axis=1),
+        jnp.concatenate([blocks[j] for j in kept[: len(sends[0])]] + [zeros], axis=1),
+    )
+
+
 class Sum:
-    def __init__(self, lhs, order):
-        spots = lax.axis_size("dp") // 2
-        self.block = lhs.shape[1] // spots
+    def __init__(self, sent, held, rhs, bound, order):
+        self.sent, self.held, self.rhs = sent, held, rhs
+        self.power = exponent(bound)
         self.order = order
-        self.kept, self.sends = [0], []
-        for bit in reversed(order):
-            send = [j ^ (1 << bit) for j in self.kept]
-            self.sends.insert(0, send)
-            self.kept = self.kept + send
-        self.rows = spots * self.block
-        half = len(self.kept) // 2
-        self.sent = self.columns(lhs, self.sends[0])
-        self.held = self.columns(lhs, self.kept[:half])
+        self.rows = 2 * (sent.shape[1] - PAD)
         self.total = None
         self.at = 0
 
-    def columns(self, lhs, places):
-        block = self.block
-        return jnp.concatenate(
-            [lhs[:, j * block : (j + 1) * block] for j in places] + [jnp.zeros((lhs.shape[0], PAD), bf16)],
-            axis=1,
-        )
-
-    def prepare(self, rhs=None, bound=None):
+    def prepare(self):
         self.rows //= 2
         if self.total is None:
-            self.rhs, self.power = rhs, exponent(bound)
-            part = lax.dot_general(self.sent, rhs, TOKENS, preferred_element_type=f32)
+            part = lax.dot_general(self.sent, self.rhs, TOKENS, preferred_element_type=f32)
         else:
             part = self.total[self.rows : 2 * self.rows + PAD]
         self.payload = coded(part, self.power, self.rows)
@@ -807,21 +834,30 @@
     def more(self):
         return self.at < len(self.order)
 
-    def shard_prepare(self):
+    def finish(self):
+        while self.more():
+            self.prepare()
+            self.send()
+            self.take()
+
+
+class ShardSum:
+    def __init__(self, sums):
         count, here = lax.axis_size("shard"), lax.axis_index("shard")
-        self.rows //= count
+        self.rows = sums[0].rows // count
+        self.total = jnp.concatenate([one.total for one in sums], axis=1) if len(sums) > 1 else sums[0].total
+        power = jnp.concatenate([one.power for one in sums], axis=1) if len(sums) > 1 else sums[0].power
+        width = self.total.shape[1]
         self.payloads = [
             coded(
-                lax.dynamic_slice(self.total, ((here ^ k) * self.rows, 0), (self.rows + PAD, self.total.shape[1])),
-                self.power, self.rows,
+                lax.dynamic_slice(self.total, ((here ^ k) * self.rows, 0), (self.rows + PAD, width)),
+                power, self.rows,
             )
             for k in range(1, count)
         ]
-
-    def shard_send(self):
         self.parts = [exchanged(part, "shard", k + 1) for k, part in enumerate(self.payloads)]
 
-    def shard_take(self, *earlier):
+    def take(self, *earlier):
         here = lax.axis_index("shard")
         result = lax.dynamic_slice(self.total, (here * self.rows, 0), (self.rows, self.total.shape[1]))
         for part in self.parts:
@@ -849,6 +885,28 @@
     return incoming
 
 
+def both_with_most(rows):
+    length = rows.shape[0] - PAD
+    arrived = exchanged(rows, "dp", 1)
+    most = jnp.maximum(rows[length : length + 1], arrived[length : length + 1]).astype(f32)
+    return jnp.concatenate([rows[:length], arrived[:length]], axis=0), most
+
+
+def mended(dx, edge, dtap, length):
+    last = edge[HALO:] + shifted(edge[:HALO], "shard", -1)
+    most = jnp.maximum(dtap[KW + 1 : KW + 2], jnp.max(jnp.abs(last), axis=0, keepdims=True)) * 1.01
+    tail = jnp.concatenate([last, jnp.broadcast_to(most, (PAD, most.shape[1]))], axis=0).astype(bf16)
+    return lax.dynamic_update_slice(dx, tail, (length - HALO, 0)), dtap
+
+
+def rest_sums(both, bound, in_columns, orders):
+    middle = both.shape[1] // 256 * 128
+    return [
+        Sum(*in_columns[0], both[:, :middle], bound[:, :middle], orders[0]),
+        Sum(*in_columns[1], both[:, middle:], bound[:, middle:], orders[1]),
+    ]
+
+
 def shards(
     hidden_in, cotangent, segment_ids,
     param_prenorm, param_inputs, param_kernel, param_offsets, param_timestep, param_decays,
@@ -860,9 +918,12 @@
 ):
     length, width = hidden_in.shape
     own_inputs = param_inputs.astype(bf16)
-    rest_w = gathered(own_inputs[:, DI:])
-    gate_w = lax.all_gather(shard_gathered(own_inputs[:, :DI]), "dp", axis=0, tiled=True)
-    out_w = lax.all_gather(shard_gathered(param_outputs.astype(bf16)), "dp", axis=0, tiled=True)
+    spare = -(param_inputs.shape[1] - DI) % 128
+    rest_rows = shard_gathered(jnp.pad(own_inputs[:, DI:], ((0, 0), (0, spare))))
+    rest_w = gathered(rest_rows)
+    gate_rows = shard_gathered(after(own_inputs[:, :DI], rest_rows))
+    gate_w = gathered(gate_rows)
+    out_w = gathered(shard_gathered(after(param_outputs.astype(bf16), gate_rows)))
 
     seg = segment_ids.astype(f32)
     ends = jnp.pad(seg[length - HALO :], (0, width - HALO))[None, :]
@@ -908,98 +969,109 @@
 
     groups = lax.axis_size("shard")
     spots = [bit for bit in range(20) if (2 << bit) < lax.axis_size("dp")]
+    orders = (spots, spots[::-1])
     in_block, out_block = groups * param_inputs.shape[0], groups * param_outputs.shape[0]
     up_both = both_cores(upstream)
-    normed_both = sum_columns(own_normed, in_block)
+    own_blocks, partner_blocks = own_and_partner(own_normed, in_block)
+    arrived = exchanged(jnp.concatenate(partner_blocks, axis=1), "dp", 1)
+    both_blocks = [
+        jnp.concatenate([one, arrived[:, j * in_block : (j + 1) * in_block]], axis=0)
+        for j, one in enumerate(own_blocks)
+    ]
+    in_columns = [columns_of(both_blocks, order) for order in orders]
     norm_bound = 2.02 * length * width**0.5 * jnp.max(jnp.abs(param_prenorm))
-    gate_bound = 2.02 * length * DI**0.5 * jnp.max(jnp.abs(param_gating))
-    gate_bound = gate_bound * jnp.max(jnp.abs(up_both)).astype(f32)
-    gate_sum = Sum(normed_both, spots[::-1])
-    rest_sums = [Sum(normed_both, spots), Sum(normed_both, spots[::-1])]
+    out_bound = 2.02 * length * DI**0.5 * jnp.max(jnp.abs(param_gating))
+    out_bound = out_bound * jnp.max(jnp.abs(up_both), axis=0, keepdims=True).astype(f32)
     rest_w = after(
-        rest_w, match, mask, segc, segr, taps, pars, dirx, gam, up_both, gate_bound, norm_bound,
-        gate_sum.sent, gate_sum.held, rest_sums[0].sent, rest_sums[0].held,
+        rest_w, match, mask, segc, segr, taps, pars, dirx, gam, up_both, out_bound, norm_bound, in_columns
     )
 
     rest = jnp.dot(normed, rest_w, preferred_element_type=f32)
-    step_raw = rest[HALO:, CH:]
-    delta, cum, cumt, infc, tailc, tailn, taild, infd, keep, factor = prep(step_raw, pars, mask)
+    delta, cum, cumt, infc, tailc, tailn, taild, infd, keep, factor = prep(rest, pars, mask)
     v, kq, state = conv_state(rest, taps, match, taild)
     incoming = carried(state, factor[0:1], 1)
     y = local_out(v, kq, delta, cum, cumt, infc, tailc, keep, segc, segr)
     gate_w = after(gate_w, y)
-    out_w = after(out_w, y)
     z = jnp.dot(own_normed, gate_w, preferred_element_type=f32)
+    out_w = after(out_w, z)
     back_gated = lax.dot_general(upstream, out_w, NT, preferred_element_type=f32)
     gated, dy, dz, dinc, small = gate(y, v, z, back_gated, kq, incoming, infd, dirx, gam)
 
-    dz_most = jnp.max(small[2])
-    dz_most = jnp.maximum(dz_most, exchanged(jnp.full((8, 128), dz_most), "dp", 1)[0, 0])
     outgoing = carried(dinc, factor[0:1], -1)
-    out_sum = Sum(sum_columns(gated, out_block), spots)
-    dz_both = both_cores(dz)
+    own_blocks, partner_blocks = own_and_partner(gated, out_block)
+    out_columns = [
+        jnp.concatenate([mine, exchanged(theirs, "dp", 1)], axis=0)
+        for mine, theirs in zip(columns_of(own_blocks, spots), columns_of(partner_blocks, spots))
+    ]
+    dz_most = jnp.broadcast_to(small[2:3] * 1.01, (PAD, DI)).astype(bf16)
+    dz = lax.dynamic_update_slice(dz, dz_most, (length, 0))
+    dz_both, dz_bound = both_with_most(dz)
+    dz = dz[:length]
     block_out = hidden_in + jnp.dot(gated, out_w, preferred_element_type=f32)
+    out_sum = Sum(*out_columns, up_both, out_bound, spots)
+    gate_sum = Sum(*in_columns[1], dz_both, norm_bound * dz_bound, spots[::-1])
     first_sums = [out_sum, gate_sum]
-    out_sum.prepare(up_both, gate_bound)
-    gate_sum.prepare(dz_both, norm_bound * dz_most)
     for one in first_sums:
+        one.prepare()
         one.send()
     back_normed = lax.dot_general(dz, gate_w, NT, preferred_element_type=f32)
-    outgoing = after(outgoing, out_sum.payload, gate_sum.payload, out_sum.total, gate_sum.total, back_normed, block_out)
+    outgoing = after(
+        outgoing, out_sum.payload, gate_sum.payload, out_sum.total, gate_sum.total, back_normed, block_out
+    )
 
     ssm = (kq, delta, cum, cumt, infc, tailc, tailn, keep, incoming)
-    dv1, *held1 = back_local(0, NG // 2, None, v, dy, *ssm, outgoing, dirx, segc, segr)
+    half = NG // 2
+    dv1, *held1 = back_local(0, half, None, v, dy, *ssm, outgoing, dirx, segc, segr)
     for one in first_sums:
         one.take(dv1)
         if one.more():
             one.prepare()
             one.send()
-    dy = after(dy, *[one.payload for one in first_sums])
-    dv2, *held2 = back_local(NG // 2, NG, held1[:2], v, dy, *ssm, outgoing, dirx, segc, segr)
+    dv1 = after(dv1, *[one.payload for one in first_sums])
+    drest1, dtap1 = mended(*unconv(0, rest, taps, match, dv1, None), length)
+    both1, bound1 = both_with_most(drest1)
+    sums1 = rest_sums(both1, norm_bound * bound1, in_columns, orders)
+    for one in sums1:
+        one.prepare()
+        one.send()
+    dy = after(dy, *[one.payload for one in sums1], *[one.total for one in sums1])
+    dv2, *held2 = back_local(half, NG, held1[:2], v, dy, *ssm, outgoing, dirx, segc, segr)
     for one in first_sums:
         one.take(dv2)
-        while one.more():
+        one.finish()
+    shard_out, shard_gate = ShardSum([out_sum]), ShardSum([gate_sum])
+    for one in sums1:
+        one.take(dv2, shard_out.payloads, shard_gate.payloads)
+        if one.more():
             one.prepare()
             one.send()
-            one.take()
-        one.shard_prepare()
-        one.shard_send()
-    dv2 = after(dv2, *[one.payloads for one in first_sums])
-    dkq = held2[0]
-    ddelta, dcum, drow = (jnp.concatenate([p, q], axis=0) for p, q in zip(held1[2:5], held2[2:5]))
-    flow = jnp.concatenate([held1[5], held2[5]], axis=1)
-    dstep, small_step = step_back(step_raw, pars, ddelta, dcum, drow, flow)
-    dx, edge, dtap = unconv(rest, taps, match, dv1, dv2, dkq)
-    rim_grad = shifted(edge[:HALO], "shard", -1)
-    mended = edge[HALO:] + rim_grad
-    dx = lax.dynamic_update_slice(dx, mended.astype(bf16), (length - HALO, 0))
-    rest_most = jnp.maximum(jnp.maximum(jnp.max(dtap[KW + 1]), jnp.max(small_step[2])), jnp.max(jnp.abs(mended)))
-    rest_most = jnp.maximum(rest_most, exchanged(jnp.full((8, 128), rest_most), "dp", 1)[0, 0])
-    rest_bound = norm_bound * rest_most
-    drest = jnp.concatenate([dx, dstep], axis=1)
-    drest_both = both_cores(drest)
-    middle = (drest.shape[1] // 256) * 128
-    rest_sums[0].prepare(drest_both[:, :middle], rest_bound)
-    rest_sums[1].prepare(drest_both[:, middle:], rest_bound)
-    for one in rest_sums:
+    dv2 = after(dv2, *[one.payload for one in sums1])
+    dstep, small_step = step_back(rest, pars, held1[2:], held2[2:])
+    drest2, dtap2 = mended(*unconv(dv1.shape[1] // TILE, rest, taps, match, dv2, held2[0]), length)
+    drest2 = jnp.concatenate([drest2, dstep], axis=1)
+    both2, bound2 = both_with_most(drest2)
+    sums2 = rest_sums(both2, norm_bound * bound2, in_columns, orders)
+    for one in sums2:
+        one.prepare()
         one.send()
-    drest = after(drest, *[one.payload for one in rest_sums])
-    back_normed = back_normed + lax.dot_general(drest, rest_w, NT, preferred_element_type=f32)
-    sent = [one.got for one in rest_sums]
-    ready = [one.payload for one in rest_sums]
-    grad_outputs = out_sum.shard_take(ready)
-    grad_gate = gate_sum.shard_take(ready)
-    for one in rest_sums:
+    for one in sums1:
+        one.take([two.payload for two in sums2])
+        one.finish()
+    shard1 = ShardSum(sums1)
+    drest1, drest2 = after((drest1, drest2), shard1.payloads, [two.payload for two in sums2])
+    wide1 = drest1.shape[1]
+    back_normed = back_normed + lax.dot_general(drest1[:length], rest_w[:, :wide1], NT, preferred_element_type=f32)
+    back_normed = back_normed + lax.dot_general(drest2[:length], rest_w[:, wide1:], NT, preferred_element_type=f32)
+    grad_outputs = shard_out.take(back_normed)
+    grad_gate = shard_gate.take(back_normed)
+    for one in sums2:
         one.take(back_normed, grad_outputs, grad_gate)
-        while one.more():
-            one.prepare()
-            one.send()
-            one.take()
-        one.shard_prepare()
-        one.shard_send()
-    sent = [one.payloads for one in rest_sums]
-    grad_rest = [one.shard_take() for one in rest_sums]
-    grad_inputs = jnp.concatenate([grad_gate] + grad_rest, axis=1)
+        one.finish()
+    shard2 = ShardSum(sums2)
+    sent = shard2.payloads
+    grad_rest = jnp.concatenate([shard1.take(sent), shard2.take()], axis=1)
+    grad_inputs = jnp.concatenate([grad_gate, grad_rest[:, : param_inputs.shape[1] - DI]], axis=1)
+    dtap = jnp.concatenate([dtap1, dtap2], axis=1)
 
     own_inv = inv[HALO:]
     scaled = hidden_in * own_inv

time: 797 us -> 704 us (0.88)
  waiting for transfers between devices: 192 us -> 129 us
  local copies, waits for them, and re-layouts: 89.5 us -> 44.8 us
  starting transfers between devices: 80.9 us -> 114 us
  between operations: 36.2 us -> 17.7 us
    ppermute x33 -> x40, waiting for transfers between devices: 123 us -> 82.6 us  [exchanged(): lax.ppermute(value, axis, [(i, i ^ by) for i in range(lax.axis_size(axis))])]
    ppermute x33 -> x40, starting transfers between devices: 48.7 us -> 81.9 us  [exchanged(): lax.ppermute(value, axis, [(i, i ^ by) for i in range(lax.axis_size(axis))])]
    all_gather x3, waiting for transfers between devices: 48.1 us -> 16.4 us  [gathered(): return lax.all_gather(value, 'dp', axis=0, tiled=True)]
    slice x29 -> x11, local copies, waits for them, and re-layouts: 27.7 us -> 12 us  [the longest x4 6.88 us: both_with_most(): return (jnp.concatenate([rows[:length], arrived[:length]], axis=0), most)]
    exp2 x0 -> x26, other arithmetic: none -> 12.6 us  [the longest x15 7.68 us: coded(): jnp.exp2(15.0 - power)]
    unnamed x203 -> x225, local copies, waits for them, and re-layouts: 19.2 us -> 8.23 us
    ppermute x8 -> x9, waiting for transfers between devices: 18.1 us -> 25.1 us  [shifted(): return lax.ppermute(value, axis, pairs)]
    concatenate x9 -> x7, other arithmetic: 20.6 us -> 14.2 us  [the longest x2 8.45 us: columns_of(): jnp.concatenate([blocks[j] for j in kept[:len(sends[0])]] + [zeros], axis=1)]
  transfers between devices with their start and end apart: 49 -> 57, of which waited for: 19 -> 21; matrix products, arithmetic and copies ran while one was open for 31% -> 31% of each run, Pallas kernels for 18% -> 21%
where the time goes in v2:
time: 704 us; the launch traced here: 697 us
  Pallas kernels  190 us (27%)
  waiting for transfers between devices  129 us (18%)
  starting transfers between devices  114 us (16%)
  matrix products  104 us (15%)
  other arithmetic  97.9 us (14%)
  local copies, waits for them, and re-layouts  44.8 us (6%)
  between operations  17.7 us (3%)
    pallas_call x2, Pallas kernels, back_local(): pl.pallas_call(functools.partial(back_kernel, last == NG), grid=(groups,)...  97.6 us
    ppermute x40, waiting for transfers between devices, exchanged(): lax.ppermute(value, axis, [(i, i ^ by) for i in range(lax.axis_size(axis))])  82.6 us
    ppermute x40, starting transfers between devices, exchanged(): lax.ppermute(value, axis, [(i, i ^ by) for i in range(lax.axis_size(axis))])  81.9 us
    ppermute x9, waiting for transfers between devices, shifted(): return lax.ppermute(value, axis, pairs)  25.1 us
    pallas_call x2, Pallas kernels, unconv(): pl.pallas_call(functools.partial(unconv_kernel, mixed), grid=(tiles,), in...  23.6 us
    ppermute x9, starting transfers between devices, shifted(): return lax.ppermute(value, axis, pairs)  22.3 us
    pallas_call x1, Pallas kernels, gate(): pl.pallas_call(gate_kernel, grid=(length // tile,), in_specs=[big, big, b...  20.4 us
    pallas_call x1, Pallas kernels, local_out(): pl.pallas_call(local_kernel, grid=(NG,), in_specs=[pl.BlockSpec((length,...  20 us
  transfers between devices with their start and end apart: 57, of which 21 were waited for; matrix products, arithmetic and copies ran while one was open for 31% of the time, Pallas kernels for 21%

profile of v2, /device:TPU:0, one launch (start us, length us, event | category | flops | bytes accessed | tf_op | source)
XLA Modules:
  0.0 697.0 jit_solution(3541043454229974920)
XLA Ops:
  14.5 11.6 %collective-permute-done.1 = bf16[48,3456]{1,0:T(8,128)(2,1)S(1)} collective-permute-done((bf16[48,3456]{1,0:T(8,128)(2,1)S(1)}, bf16[48,3456]{1,0:T(8,128)(2,1)S(1)}, u32[]{:S(2)}, u32[]{:S(2)}) %collective-permute-start.1) | collective-permute-done | bytes 331808 | tf_op jit(solution)/shard_map/ppermute | solution.py:749
  26.2 11.6 %collective-permute-done.2 = bf16[48,3456]{1,0:T(8,128)(2,1)S(1)} collective-permute-done((bf16[48,3456]{1,0:T(8,128)(2,1)S(1)}, bf16[48,3456]{1,0:T(8,128)(2,1)S(1)}, u32[]{:S(2)}, u32[]{:S(2)}) %collective-permute-start.2) | collective-permute-done | bytes 331808 | tf_op jit(solution)/shard_map/ppermute | solution.py:749
  48.0 8.3 %collective-permute-done.6 = bf16[48,3072]{1,0:T(8,128)(2,1)S(1)} collective-permute-done((bf16[48,3072]{1,0:T(8,128)(2,1)S(1)}, bf16[48,3072]{1,0:T(8,128)(2,1)S(1)}, u32[]{:S(2)}, u32[]{:S(2)}) %collective-permute-start.6) | collective-permute-done | bytes 294944 | tf_op jit(solution)/shard_map/ppermute | solution.py:749
  56.3 12.4 %collective-permute-done.7 = bf16[48,3072]{1,0:T(8,128)(2,1)S(1)} collective-permute-done((bf16[48,3072]{1,0:T(8,128)(2,1)S(1)}, bf16[48,3072]{1,0:T(8,128)(2,1)S(1)}, u32[]{:S(2)}, u32[]{:S(2)}) %collective-permute-start.7) | collective-permute-done | bytes 294944 | tf_op jit(solution)/shard_map/ppermute | solution.py:749
  83.7 13.8 %collective-permute-done.10 = bf16[96,1536]{1,0:T(8,128)(2,1)S(1)} collective-permute-done((bf16[96,1536]{1,0:T(8,128)(2,1)S(1)}, bf16[96,1536]{1,0:T(8,128)(2,1)S(1)}, u32[]{:S(2)}, u32[]{:S(2)}) %collective-permute-start.10) | collective-permute-done | bytes 294944 | tf_op jit(solution)/shard_map/ppermute | solution.py:749
  135.7 12.6 %fusion.165.step_ref.xv_ref.xk_ref.x_ref = f32[520,3456]{1,0:T(8,128)} fusion(bf16[520,1536]{1,0:T(8,128)(2,1)} %copy-done.17, bf16[1536,3456]{1,0:T(8,128)(2,1)} %all-gather.4.cloned.1.call-done), kind=kOutput, calls=%fused_computation.394 | convolution fusion | flops 5520752640 | bytes 19402752 | tf_op jit(solution)/shard_map/dot_general | solution.py:989
  148.2 7.1 %prep.1 = (f32[6,512,8]{2,1,0:T(8,128)}, f32[6,512,8]{2,1,0:T(8,128)}, f32[48,512]{1,0:T(8,128)}, f32[6,512,8]{2,1,0:T(8,128)}, f32[6,512,8]{2,1,0:T(8,128)}, /*...) custom-call(f32[520,3456]{1,0:T(8,128)} %fusion.165.step_ref.xv_ref., ...), custom_call_target="tpu_custom_call" | custom-call | flops 10000000 | bytes 10000000 | tf_op jit(solution)/shard_map/prep/pallas_call | solution.py:159
  155.3 12.8 %conv_state.1 = (f32[512,3072]{1,0:T(8,128)}, f32[512,256]{1,0:T(8,128)}, f32[128,3072]{1,0:T(8,128)}) custom-call(f32[520,3456]{1,0:T(8,128)} %fusion.165.step_ref.xv_ref.xk_ref.x_ref, f32[520,3456]{1,0:T(8,128)} %fusion.165.step_ref.xv_ref.xk_ref.x_ref, f32[8,3328]{1,0:T(8,128)} %maximum_maximum_fusion.4.tv_ref.tk_ref.tap_ref, ...), custom_call_target="tpu_custom_call" | custom-call | flops 2000000000 | bytes 20000000 | tf_op jit(solution)/shard_map/conv_state/pallas_call | solution.py:221
  177.7 20.0 %local_out.1.y_ref = f32[512,3072]{1,0:T(8,128)} custom-call(f32[512,3072]{1,0:T(8,128)} %get-tuple-element.110.v_ref, f32[512,256]{1,0:T(8,128)} %get-tuple-element.111.kq_ref, f32[6,512,8]{2,1,0:T(8,128)} %get-tuple-element.112.delta_ref, f32[6,512,8]{2,1,0:T(8,128)} %get-tuple-element.113.cum_ref, f32[48,512]{1,0:T(8,128)} %get-tuple-element.114.cumt_ref, ...), custom_call_target="tpu_custom_call" | custom-call | flops 2000000000 | bytes 20000000 | tf_op jit(solution)/shard_map/local_out/pallas_call | solution.py:303
  202.8 10.8 %fusion.138.z_ref = f32[512,3072]{1,0:T(8,128)} fusion(bf16[1536,3072]{1,0:T(8,128)(2,1)} %all-gather.6.cloned.1.call-done, bf16[520,1536]{1,0:T(8,128)(2,1)S(1)} %copy-done.18), kind=kOutput, calls=%fused_computation.384 | convolution fusion | flops 4831838208 | bytes 17301504 | tf_op jit(solution)/shard_map/dot_general | solution.py:995
  213.6 16.4 %all-gather.8.cloned.1.call-done = bf16[3072,1536]{1,0:T(8,128)(2,1)} async-done(((bf16[384,1536]{1,0:T(8,128)(2,1)}), bf16[3072,1536]{1,0:T(8,128)(2,1)}) %all-gather.8.cloned.1.call-update) | async-done | bytes 9437200 | tf_op jit(solution)/shard_map/all_gather | solution.py:735
  235.3 9.8 %convolution_bitcast_fusion.g_ref = f32[512,3072]{1,0:T(8,128)} fusion(bf16[3072,1536]{1,0:T(8,128)(2,1)} %all-gather.8.cloned.1.call-done, bf16[512,1536]{1,0:T(8,128)(2,1)} %convert_element_type.313), kind=kOutput, calls=%fused_computation.5 | convolution fusion | flops 4831838208 | bytes 17301504 | tf_op jit(solution)/shard_map/dot_general | solution.py:997
  245.1 7.3 %collective-permute-done.14.inc_ref = bf16[128,3072]{1,0:T(8,128)(2,1)S(1)} collective-permute-done((bf16[128,3072]{1,0:T(8,128)(2,1)S(1)}, bf16[128,3072]{1,0:T(8,128)(2,1)S(1)}, u32[]{:S(2)}, u32[]{:S(2)}) %collective-permute-start.14) | collective-permute-done | bytes 786464 | tf_op jit(solution)/shard_map/ppermute | solution.py:728
  253.3 20.4 %gate.1 = (bf16[512,3072]{1,0:T(8,128)(2,1)}, f32[512,3072]{1,0:T(8,128)}, bf16[528,3072]{1,0:T(8,128)(2,1)}, f32[128,3072]{1,0:T(8,128)}, f32[8,3072]{1,0:T(8,128)}) custom-call(f32[512,3072]{1,0:T(8,128)} %local_out.1.y_ref, f32[512,3072]{1,0:T(8,128)} %get-tuple-element.110.v_ref, f32[512,3072]{1,0:T(8,128)} %fusion.138.z_ref, ...), custom_call_target="tpu_custom_call" | custom-call | flops 1000000000 | bytes 40000000 | tf_op jit(solution)/shard_map/gate/pallas_call | solution.py:383
  275.3 10.7 %convolution_add_fusion = f32[512,1536]{1,0:T(8,128)} fusion(f32[512,1536]{1,0:T(8,128)S(1)} %copy-done, bf16[512,3072]{1,0:T(8,128)(2,1)} %get-tuple-element.125, bf16[3072,1536]{1,0:T(8,128)(2,1)} %all-gather.8.cloned.1.call-done), kind=kOutput, calls=%fused_computation.16 | convolution fusion | flops 4832624640 | bytes 18874368 | tf_op jit(solution)/shard_map/dot_general | solution.py:1010
  295.3 10.7 %fusion.140 = f32[512,1536]{1,0:T(8,128)} fusion(bf16[1536,3072]{1,0:T(8,128)(2,1)} %all-gather.6.cloned.1.call-done, bf16[528,3072]{1,0:T(8,128)(2,1)} %broadcast_dynamic-update-slice_fusion), kind=kOutput, calls=%fused_computation.386 | convolution fusion | flops 4831838208 | bytes 15728640 | tf_op jit(solution)/shard_map/dot_general | solution.py:1017
  333.1 7.4 %fusion.20 = f32[784,1536]{1,0:T(8,128)} fusion(bf16[512,16]{1,0:T(8,128)(2,1)S(1)} %broadcast.327, bf16[512,784]{1,0:T(8,128)(2,1)} %copy.92, bf16[512,384]{1,0:T(8,128)(2,1)} %get-tuple-element.260, bf16[512,384]{1,0:T(8,128)(2,1)} %get-tuple-element.257, bf16[512,1536]{1,0:T(8,128)(2,1)} %collective-permute-done.4, ...), kind=kOutput, calls=%fused_computation.59 | convolution fusion | flops 2478964736 | bytes 9568256 | tf_op jit(solution)/shard_map/dot_general | solution.py:827
  364.9 48.9 %back_first.1 = (f32[512,1536]{1,0:T(8,128)}, f32[512,256]{1,0:T(8,128)}, f32[512,128]{1,0:T(8,128)}, f32[3,512,8]{2,1,0:T(8,128)}, f32[3,512,8]{2,1,0:T(8,128)}, /*index=5*/f32[24,512]{1,0:T(8,128)}, f32[8,1536]{1,0:T(8,128)}) custom-call(f32[512,3072]{1,0:T(8,128)} %get-tuple-element.110.v_ref, f32[512,3072]{1,0:T(8,128)} %get-tuple-element.139.dy_ref, ...), custom_call_target="tpu_custom_call" | custom-call | flops 15000000512 | bytes 15000000 | tf_op jit(solution)/shard_map/back_first/pallas_call | solution.py:539
  427.6 11.0 %shard_map.581 = (bf16[528,1536]{1,0:T(8,128)(2,1)}, f32[16,1536]{1,0:T(8,128)}, f32[8,1536]{1,0:T(8,128)}) custom-call(f32[520,3456]{1,0:T(8,128)} %fusion.165.step_ref.xv_ref.xk_ref.x_ref, f32[8,3328]{1,0:T(8,128)} %maximum_maximum_fusion.4.tv_ref.tk_ref.tap_ref, f32[3,512,128]{2,1,0:T(8,128)} %broadcast_in_dim.284.match_ref, ...), custom_call_target="tpu_custom_call" | custom-call | flops 100000000 | bytes 10000000 | tf_op jit(solution)/shard_map/pallas_call | solution.py:690
  462.3 48.7 %back_second.1 = (f32[512,1536]{1,0:T(8,128)}, f32[512,256]{1,0:T(8,128)}, f32[512,128]{1,0:T(8,128)}, f32[3,512,8]{2,1,0:T(8,128)}, f32[3,512,8]{2,1,0:T(8,128)}, /*index=5*/f32[24,512]{1,0:T(8,128)}, f32[8,1536]{1,0:T(8,128)}) custom-call(f32[512,3072]{1,0:T(8,128)} %get-tuple-element.110.v_ref, f32[512,3072]{1,0:T(8,128)} %get-tuple-element.139.dy_ref, ...), custom_call_target="tpu_custom_call" | custom-call | flops 15000000512 | bytes 15000000 | tf_op jit(solution)/shard_map/back_second/pallas_call | solution.py:539
  523.5 12.6 %shard_map.582 = (bf16[528,1792]{1,0:T(8,128)(2,1)}, f32[16,1792]{1,0:T(8,128)}, f32[8,1792]{1,0:T(8,128)}) custom-call(f32[520,3456]{1,0:T(8,128)} %fusion.165.step_ref.xv_ref.xk_ref.x_ref, f32[8,3328]{1,0:T(8,128)} %maximum_maximum_fusion.4.tv_ref.tk_ref.tap_ref, f32[3,512,128]{2,1,0:T(8,128)} %broadcast_in_dim.284.match_ref, ...), custom_call_target="tpu_custom_call" | custom-call | flops 100000000 | bytes 10000000 | tf_op jit(solution)/shard_map/pallas_call | solution.py:690
  538.2 8.7 %step_back.1 = (bf16[528,128]{1,0:T(8,128)(2,1)}, f32[8,48]{1,0:T(8,128)}) custom-call(f32[520,3456]{1,0:T(8,128)} %fusion.165.step_ref.xv_ref.xk_ref.x_ref, f32[8,48]{1,0:T(8,128)} %maximum_maximum_fusion.5.par_ref, f32[3,512,8]{2,1,0:T(8,128)} %get-tuple-element.152.ddelta_a, f32[3,512,8]{2,1,0:T(8,128)} %get-tuple-element.153.ddelta_b, ...), custom_call_target="tpu_custom_call" | custom-call | flops 10000000 | bytes 10000000 | tf_op jit(solution)/shard_map/step_back/pallas_call | solution.py:628
  591.6 17.7 %collective-permute-start.48 = (f16[64,1536]{1,0:T(8,128)(2,1)}, f16[64,1536]{1,0:T(8,128)(2,1)}, u32[]{:S(2)}, u32[]{:S(2)}) collective-permute-start(f16[64,1536]{1,0:T(8,128)(2,1)} %get-tuple-element.285), channel_id=1, source_target_pairs={{0,1},{1,0},{2,3},{3,2},{4,5},{5,4},{6,7},{7,6},{8,9},{9,8},{10,11... | collective-permute-start | bytes 589832 | tf_op jit(solution)/shard_map/ppermute | solution.py:749
  643.7 14.6 %collective-permute-start.52 = (f16[64,1920]{1,0:T(8,128)(2,1)S(1)}, f16[64,1920]{1,0:T(8,128)(2,1)S(1)}, u32[]{:S(2)}, u32[]{:S(2)}) collective-permute-start(f16[64,1920]{1,0:T(8,128)(2,1)S(1)} %get-tuple-element.275), channel_id=1, source_target_pairs={{0,2},{1,3},{2,0},{3,1},{4,6},{5,7},{6,4},{7,5},{8,10},{9,11},{10,... | collective-permute-start | bytes 737288 | tf_op jit(solution)/shard_map/ppermute | solution.py:749
  (546 shorter events, 313.5 us)
Async XLA Ops:
  7.2 124.6 %all-gather.4.cloned.1.call-start = ((), (), s32[]{:S(2)}) async-start(), calls=%async_computation | async-start | bytes 11943936 | tf_op jit(solution)/shard_map/all_gather | solution.py:735
  38.9 158.8 %all-gather.6.cloned.1.call-start = ((), (), s32[]{:S(2)}) async-start(), calls=%async_computation.1 | async-start | bytes 10616832 | tf_op jit(solution)/shard_map/all_gather | solution.py:735
  69.9 160.2 %all-gather.8.cloned.1.call-start = ((), (), s32[]{:S(2)}) async-start(), calls=%async_computation.2 | async-start | bytes 10616832 | tf_op jit(solution)/shard_map/all_gather | solution.py:735
  107.9 66.6 %collective-permute-start.4 = (bf16[512,1536]{1,0:T(8,128)(2,1)}, bf16[512,1536]{1,0:T(8,128)(2,1)}, u32[]{:S(2)}, u32[]{:S(2)}) collective-permute-start(bf16[512,1536]{1,0:T(8,128)(2,1)} %convert_element_type.313), channel_id=1, source_target_pairs={{0,4},{4,0},{8,12},{12,8},{16,20},{20,16},{24,28},{28,24},{1,5},{5... | collective-permute-start | bytes 4718600 | tf_op jit(solution)/shard_map/ppermute | solution.py:749
  170.5 27.3 %collective-permute-start.12 = (bf16[128,3072]{1,0:T(8,128)(2,1)}, bf16[128,3072]{1,0:T(8,128)(2,1)}, u32[]{:S(2)}, u32[]{:S(2)}) collective-permute-start(bf16[128,3072]{1,0:T(8,128)(2,1)} %convert_element_type.315), channel_id=1, source_target_pairs={{0,1},{1,2},{2,3},{4,5},{5,6},{6,7},{8,9},{9,10},{10,11},{12,13},{... | collective-permute-start | bytes 2359304 | tf_op jit(solution)/shard_map/ppermute | solution.py:728
  200.6 29.5 %collective-permute-start.13 = (bf16[128,3072]{1,0:T(8,128)(2,1)}, bf16[128,3072]{1,0:T(8,128)(2,1)}, u32[]{:S(2)}, u32[]{:S(2)}) collective-permute-start(bf16[128,3072]{1,0:T(8,128)(2,1)} %add_convert_fusion.3), channel_id=1, source_target_pairs={{0,1},{1,2},{2,3},{4,5},{5,6},{6,7},{8,9},{9,10},{10,11},{12,13},{... | collective-permute-start | bytes 2359304 | tf_op jit(solution)/shard_map/ppermute | solution.py:728
  275.3 68.1 %collective-permute-start.19 = (bf16[528,3072]{1,0:T(8,128)(2,1)}, bf16[528,3072]{1,0:T(8,128)(2,1)}, u32[]{:S(2)}, u32[]{:S(2)}) collective-permute-start(bf16[528,3072]{1,0:T(8,128)(2,1)} %broadcast_dynamic-update-slice_fusion), channel_id=1, source_target_pairs={{0,4},{4,0},{8,12},{12,8},{16,20},{20,16},{24,28},{28,24},{1,5},{5... | collective-permute-start | bytes 9732104 | tf_op jit(solution)/shard_map/ppermute | solution.py:749
  291.1 29.3 %collective-permute-start.18 = (bf16[512,784]{0,1:T(8,128)(2,1)}, bf16[512,784]{0,1:T(8,128)(2,1)}, u32[]{:S(2)}, u32[]{:S(2)}) collective-permute-start(bf16[512,784]{0,1:T(8,128)(2,1)} %copy.89), channel_id=1, source_target_pairs={{0,4},{4,0},{8,12},{12,8},{16,20},{20,16},{24,28},{28,24},{1,5},{5... | collective-permute-start | bytes 2408456 | tf_op jit(solution)/shard_map/ppermute | solution.py:749
  329.5 84.3 %collective-permute-start.21 = (f16[784,1536]{1,0:T(8,128)(2,1)}, f16[784,1536]{1,0:T(8,128)(2,1)}, u32[]{:S(2)}, u32[]{:S(2)}) collective-permute-start(f16[784,1536]{1,0:T(8,128)(2,1)} %select_convert_fusion.1), channel_id=1, source_target_pairs={{0,8},{4,12},{8,0},{12,4},{16,24},{20,28},{24,16},{28,20},{1,9},{5... | collective-permute-start | bytes 7225352 | tf_op jit(solution)/shard_map/ppermute | solution.py:749
  351.4 68.8 %collective-permute-start.22 = (f16[400,3072]{1,0:T(8,128)(2,1)}, f16[400,3072]{1,0:T(8,128)(2,1)}, u32[]{:S(2)}, u32[]{:S(2)}) collective-permute-start(f16[400,3072]{1,0:T(8,128)(2,1)} %select_convert_fusion), channel_id=1, source_target_pairs={{0,16},{4,20},{8,24},{12,28},{16,0},{20,4},{24,8},{28,12},{1,17},{... | collective-permute-start | bytes 7372808 | tf_op jit(solution)/shard_map/ppermute | solution.py:749
  447.7 66.8 %collective-permute-start.26 = (f16[400,1536]{1,0:T(8,128)(2,1)}, f16[400,1536]{1,0:T(8,128)(2,1)}, u32[]{:S(2)}, u32[]{:S(2)}) collective-permute-start(f16[400,1536]{1,0:T(8,128)(2,1)} %fusion.14), channel_id=1, source_target_pairs={{0,16},{4,20},{8,24},{12,28},{16,0},{20,4},{24,8},{28,12},{1,17},{... | collective-permute-start | bytes 3686408 | tf_op jit(solution)/shard_map/ppermute | solution.py:749
  448.4 62.8 %collective-permute-start.27 = (f16[208,3072]{1,0:T(8,128)(2,1)}, f16[208,3072]{1,0:T(8,128)(2,1)}, u32[]{:S(2)}, u32[]{:S(2)}) collective-permute-start(f16[208,3072]{1,0:T(8,128)(2,1)} %fusion.12), channel_id=1, source_target_pairs={{0,8},{4,12},{8,0},{12,4},{16,24},{20,28},{24,16},{28,20},{1,9},{5... | collective-permute-start | bytes 3833864 | tf_op jit(solution)/shard_map/ppermute | solution.py:749
  458.7 60.9 %collective-permute-start.25 = (f16[400,768]{1,0:T(8,128)(2,1)}, f16[400,768]{1,0:T(8,128)(2,1)}, u32[]{:S(2)}, u32[]{:S(2)}) collective-permute-start(f16[400,768]{1,0:T(8,128)(2,1)} %fusion.37), channel_id=1, source_target_pairs={{0,8},{4,12},{8,0},{12,4},{16,24},{20,28},{24,16},{28,20},{1,9},{5... | collective-permute-start | bytes 1843208 | tf_op jit(solution)/shard_map/ppermute | solution.py:749
  461.0 60.9 %collective-permute-start.28 = (f16[400,768]{1,0:T(8,128)(2,1)}, f16[400,768]{1,0:T(8,128)(2,1)S(1)}, u32[]{:S(2)}, u32[]{:S(2)}) collective-permute-start(f16[400,768]{1,0:T(8,128)(2,1)} %fusion.36), channel_id=1, source_target_pairs={{0,16},{4,20},{8,24},{12,28},{16,0},{20,4},{24,8},{28,12},{1,17},{... | collective-permute-start | bytes 1843208 | tf_op jit(solution)/shard_map/ppermute | solution.py:749
  551.1 37.3 %collective-permute-start.37 = (f16[64,3072]{1,0:T(8,128)(2,1)}, f16[64,3072]{1,0:T(8,128)(2,1)}, u32[]{:S(2)}, u32[]{:S(2)}) collective-permute-start(f16[64,3072]{1,0:T(8,128)(2,1)} %get-tuple-element.267), channel_id=1, source_target_pairs={{0,1},{1,0},{2,3},{3,2},{4,5},{5,4},{6,7},{7,6},{8,9},{9,8},{10,11... | collective-permute-start | bytes 1179656 | tf_op jit(solution)/shard_map/ppermute | solution.py:749
  553.8 34.9 %collective-permute-start.38 = (f16[64,3072]{1,0:T(8,128)(2,1)}, f16[64,3072]{1,0:T(8,128)(2,1)}, u32[]{:S(2)}, u32[]{:S(2)}) collective-permute-start(f16[64,3072]{1,0:T(8,128)(2,1)} %get-tuple-element.266), channel_id=1, source_target_pairs={{0,2},{1,3},{2,0},{3,1},{4,6},{5,7},{6,4},{7,5},{8,10},{9,11},{10,... | collective-permute-start | bytes 1179656 | tf_op jit(solution)/shard_map/ppermute | solution.py:749
  556.5 33.5 %collective-permute-start.39 = (f16[64,3072]{1,0:T(8,128)(2,1)}, f16[64,3072]{1,0:T(8,128)(2,1)}, u32[]{:S(2)}, u32[]{:S(2)}) collective-permute-start(f16[64,3072]{1,0:T(8,128)(2,1)} %get-tuple-element.265), channel_id=1, source_target_pairs={{0,3},{1,2},{2,1},{3,0},{4,7},{5,6},{6,5},{7,4},{8,11},{9,10},{10,... | collective-permute-start | bytes 1179656 | tf_op jit(solution)/shard_map/ppermute | solution.py:749
  569.6 44.8 %collective-permute-start.35 = (f16[112,1536]{1,0:T(8,128)(2,1)S(1)}, f16[112,1536]{1,0:T(8,128)(2,1)S(1)}, u32[]{:S(2)}, u32[]{:S(2)}) collective-permute-start(f16[112,1536]{1,0:T(8,128)(2,1)S(1)} %copy-done.56), channel_id=1, source_target_pairs={{0,2},{1,3},{2,0},{3,1},{4,6},{5,7},{6,4},{7,5},{8,10},{9,11},{10,... | collective-permute-start | bytes 1032200 | tf_op jit(solution)/shard_map/ppermute | solution.py:749
  588.7 37.2 %collective-permute-start.33 = (f16[400,896]{1,0:T(8,128)(2,1)}, f16[400,896]{1,0:T(8,128)(2,1)}, u32[]{:S(2)}, u32[]{:S(2)}) collective-permute-start(f16[400,896]{1,0:T(8,128)(2,1)} %fusion.35), channel_id=1, source_target_pairs={{0,8},{4,12},{8,0},{12,4},{16,24},{20,28},{24,16},{28,20},{1,9},{5... | collective-permute-start | bytes 2150408 | tf_op jit(solution)/shard_map/ppermute | solution.py:749
  590.1 40.2 %collective-permute-start.41 = (f16[400,1024]{1,0:T(8,128)(2,1)}, f16[400,1024]{1,0:T(8,128)(2,1)}, u32[]{:S(2)}, u32[]{:S(2)}) collective-permute-start(f16[400,1024]{1,0:T(8,128)(2,1)} %select_convert_fusion.2), channel_id=1, source_target_pairs={{0,16},{4,20},{8,24},{12,28},{16,0},{20,4},{24,8},{28,12},{1,17},{... | collective-permute-start | bytes 2457608 | tf_op jit(solution)/shard_map/ppermute | solution.py:749
  591.6 66.8 %collective-permute-start.48 = (f16[64,1536]{1,0:T(8,128)(2,1)}, f16[64,1536]{1,0:T(8,128)(2,1)}, u32[]{:S(2)}, u32[]{:S(2)}) collective-permute-start(f16[64,1536]{1,0:T(8,128)(2,1)} %get-tuple-element.285), channel_id=1, source_target_pairs={{0,1},{1,0},{2,3},{3,2},{4,5},{5,4},{6,7},{7,6},{8,9},{9,8},{10,11... | collective-permute-start | bytes 589832 | tf_op jit(solution)/shard_map/ppermute | solution.py:749
  614.4 46.3 %collective-permute-start.49 = (f16[64,1536]{1,0:T(8,128)(2,1)}, f16[64,1536]{1,0:T(8,128)(2,1)}, u32[]{:S(2)}, u32[]{:S(2)}) collective-permute-start(f16[64,1536]{1,0:T(8,128)(2,1)} %get-tuple-element.286), channel_id=1, source_target_pairs={{0,2},{1,3},{2,0},{3,1},{4,6},{5,7},{6,4},{7,5},{8,10},{9,11},{10,... | collective-permute-start | bytes 589832 | tf_op jit(solution)/shard_map/ppermute | solution.py:749
  615.2 47.0 %collective-permute-start.50 = (f16[64,1536]{1,0:T(8,128)(2,1)S(1)}, f16[64,1536]{1,0:T(8,128)(2,1)}, u32[]{:S(2)}, u32[]{:S(2)}) collective-permute-start(f16[64,1536]{1,0:T(8,128)(2,1)S(1)} %get-tuple-element.284), channel_id=1, source_target_pairs={{0,3},{1,2},{2,1},{3,0},{4,7},{5,6},{6,5},{7,4},{8,11},{9,10},{10,... | collective-permute-start | bytes 589832 | tf_op jit(solution)/shard_map/ppermute | solution.py:749
  643.7 28.0 %collective-permute-start.52 = (f16[64,1920]{1,0:T(8,128)(2,1)S(1)}, f16[64,1920]{1,0:T(8,128)(2,1)S(1)}, u32[]{:S(2)}, u32[]{:S(2)}) collective-permute-start(f16[64,1920]{1,0:T(8,128)(2,1)S(1)} %get-tuple-element.275), channel_id=1, source_target_pairs={{0,2},{1,3},{2,0},{3,1},{4,6},{5,7},{6,4},{7,5},{8,10},{9,11},{10,... | collective-permute-start | bytes 737288 | tf_op jit(solution)/shard_map/ppermute | solution.py:749
  (146 other events, 1991.6 us)
Sparse Core Ops, SparseCore 0:
  39.0 68.5 all-gather.3
  110.1 58.6 all-gather.5
  171.3 58.6 all-gather.7

commit v3 on v2

--- a/solution.py
+++ b/solution.py
@@ -880,8 +880,9 @@
 
 def carried(state, factor, by):
     incoming = shifted(state.astype(bf16), "shard", by)
-    for _ in range(lax.axis_size("shard") - 2):
-        incoming = shifted((state + factor * incoming.astype(f32)).astype(bf16), "shard", by)
+    for _ in range(1, lax.axis_size("shard") - 1):
+        passed = (state + factor * incoming.astype(f32)).astype(bf16)
+        incoming = shifted(passed, "shard", by)
     return incoming
 
 
@@ -921,9 +922,6 @@
     spare = -(param_inputs.shape[1] - DI) % 128
     rest_rows = shard_gathered(jnp.pad(own_inputs[:, DI:], ((0, 0), (0, spare))))
     rest_w = gathered(rest_rows)
-    gate_rows = shard_gathered(after(own_inputs[:, :DI], rest_rows))
-    gate_w = gathered(gate_rows)
-    out_w = gathered(shard_gathered(after(param_outputs.astype(bf16), gate_rows)))
 
     seg = segment_ids.astype(f32)
     ends = jnp.pad(seg[length - HALO :], (0, width - HALO))[None, :]
@@ -982,9 +980,11 @@
     norm_bound = 2.02 * length * width**0.5 * jnp.max(jnp.abs(param_prenorm))
     out_bound = 2.02 * length * DI**0.5 * jnp.max(jnp.abs(param_gating))
     out_bound = out_bound * jnp.max(jnp.abs(up_both), axis=0, keepdims=True).astype(f32)
-    rest_w = after(
-        rest_w, match, mask, segc, segr, taps, pars, dirx, gam, up_both, out_bound, norm_bound, in_columns
-    )
+    early = (match, mask, segc, segr, taps, pars, dirx, gam, up_both, out_bound, norm_bound, in_columns, normed)
+    gate_rows = shard_gathered(after(own_inputs[:, :DI], rest_rows, early))
+    gate_w = gathered(gate_rows)
+    out_w = gathered(shard_gathered(after(param_outputs.astype(bf16), gate_rows)))
+    rest_w = after(rest_w, early)
 
     rest = jnp.dot(normed, rest_w, preferred_element_type=f32)
     delta, cum, cumt, infc, tailc, tailn, taild, infd, keep, factor = prep(rest, pars, mask)
@@ -1031,17 +1031,19 @@
     drest1, dtap1 = mended(*unconv(0, rest, taps, match, dv1, None), length)
     both1, bound1 = both_with_most(drest1)
     sums1 = rest_sums(both1, norm_bound * bound1, in_columns, orders)
+    for one in first_sums:
+        one.take(dv1, both1)
+        one.finish()
+    shard_out, shard_gate = ShardSum([out_sum]), ShardSum([gate_sum])
     for one in sums1:
         one.prepare()
         one.send()
-    dy = after(dy, *[one.payload for one in sums1], *[one.total for one in sums1])
+    dy = after(
+        dy, [one.payload for one in sums1], [one.total for one in sums1], shard_out.payloads, shard_gate.payloads
+    )
     dv2, *held2 = back_local(half, NG, held1[:2], v, dy, *ssm, outgoing, dirx, segc, segr)
-    for one in first_sums:
+    for one in sums1:
         one.take(dv2)
-        one.finish()
-    shard_out, shard_gate = ShardSum([out_sum]), ShardSum([gate_sum])
-    for one in sums1:
-        one.take(dv2, shard_out.payloads, shard_gate.payloads)
         if one.more():
             one.prepare()
             one.send()
@@ -1055,20 +1057,25 @@
         one.prepare()
         one.send()
     for one in sums1:
-        one.take([two.payload for two in sums2])
+        one.take(dv2, dstep)
         one.finish()
     shard1 = ShardSum(sums1)
     drest1, drest2 = after((drest1, drest2), shard1.payloads, [two.payload for two in sums2])
     wide1 = drest1.shape[1]
     back_normed = back_normed + lax.dot_general(drest1[:length], rest_w[:, :wide1], NT, preferred_element_type=f32)
     back_normed = back_normed + lax.dot_general(drest2[:length], rest_w[:, wide1:], NT, preferred_element_type=f32)
-    grad_outputs = shard_out.take(back_normed)
-    grad_gate = shard_gate.take(back_normed)
+    grad_outputs = shard_out.take(drest2)
+    grad_gate = shard_gate.take(drest2)
     for one in sums2:
-        one.take(back_normed, grad_outputs, grad_gate)
+        one.take(back_normed)
+        if one.more():
+            one.prepare()
+            one.send()
+    sent = [one.payload for one in sums2]
+    for one in sums2:
+        one.take()
         one.finish()
     shard2 = ShardSum(sums2)
-    sent = shard2.payloads
     grad_rest = jnp.concatenate([shard1.take(sent), shard2.take()], axis=1)
     grad_inputs = jnp.concatenate([grad_gate, grad_rest[:, : param_inputs.shape[1] - DI]], axis=1)
     dtap = jnp.concatenate([dtap1, dtap2], axis=1)

time: 704 us -> 749 us (1.064)
  waiting for transfers between devices: 129 us -> 161 us
  starting transfers between devices: 114 us -> 91.1 us
  other arithmetic: 97.9 us -> 115 us
  local copies, waits for them, and re-layouts: 44.8 us -> 60.4 us
    ppermute x40, starting transfers between devices: 81.9 us -> 50.1 us  [exchanged(): lax.ppermute(value, axis, [(i, i ^ by) for i in range(lax.axis_size(axis))])]
    ppermute x40, waiting for transfers between devices: 82.6 us -> 110 us  [exchanged(): lax.ppermute(value, axis, [(i, i ^ by) for i in range(lax.axis_size(axis))])]
  transfers between devices with their start and end apart: 57 -> 57, of which waited for: 21 -> 20; matrix products, arithmetic and copies ran while one was open for 31% -> 34% of each run, Pallas kernels for 21% -> 21%
where the time goes in v3:
time: 749 us; the launch traced here: 739 us
  Pallas kernels  189 us (25%)
  waiting for transfers between devices  161 us (21%)
  other arithmetic  115 us (15%)
  matrix products  105 us (14%)
  starting transfers between devices  91.1 us (12%)
  local copies, waits for them, and re-layouts  60.4 us (8%)
  between operations  17.2 us (2%)
    ppermute x40, waiting for transfers between devices, exchanged(): lax.ppermute(value, axis, [(i, i ^ by) for i in range(lax.axis_size(axis))])  110 us
    pallas_call x2, Pallas kernels, back_local(): pl.pallas_call(functools.partial(back_kernel, last == NG), grid=(groups,)...  97.6 us
    ppermute x40, starting transfers between devices, exchanged(): lax.ppermute(value, axis, [(i, i ^ by) for i in range(lax.axis_size(axis))])  50.1 us
    ppermute x9, starting transfers between devices, shifted(): return lax.ppermute(value, axis, pairs)  27.6 us
    ppermute x9, waiting for transfers between devices, shifted(): return lax.ppermute(value, axis, pairs)  25.9 us
    pallas_call x2, Pallas kernels, unconv(): pl.pallas_call(functools.partial(unconv_kernel, mixed), grid=(tiles,), in...  23.7 us
    pallas_call x1, Pallas kernels, gate(): pl.pallas_call(gate_kernel, grid=(length // tile,), in_specs=[big, big, b...  20.4 us
    dot_general x6, matrix products, send(): lax.dot_general(self.held, self.rhs, TOKENS, preferred_element_type=f32)  19.2 us
  transfers between devices with their start and end apart: 57, of which 20 were waited for; matrix products, arithmetic and copies ran while one was open for 34% of the time, Pallas kernels for 21%

profile of v3, /device:TPU:0, one launch (start us, length us, event | category | flops | bytes accessed | tf_op | source)
XLA Modules:
  0.0 739.3 jit_solution(2372157019011595785)
XLA Ops:
  15.4 11.6 %collective-permute-done.1 = bf16[48,3456]{1,0:T(8,128)(2,1)S(1)} collective-permute-done((bf16[48,3456]{1,0:T(8,128)(2,1)S(1)}, bf16[48,3456]{1,0:T(8,128)(2,1)S(1)}, u32[]{:S(2)}, u32[]{:S(2)}) %collective-permute-start.1) | collective-permute-done | bytes 331808 | tf_op jit(solution)/shard_map/ppermute | solution.py:749
  27.0 11.6 %collective-permute-done.2 = bf16[48,3456]{1,0:T(8,128)(2,1)S(1)} collective-permute-done((bf16[48,3456]{1,0:T(8,128)(2,1)S(1)}, bf16[48,3456]{1,0:T(8,128)(2,1)S(1)}, u32[]{:S(2)}, u32[]{:S(2)}) %collective-permute-start.2) | collective-permute-done | bytes 331808 | tf_op jit(solution)/shard_map/ppermute | solution.py:749
  41.2 9.1 %collective-permute-start = (f32[16,1536]{1,0:T(8,128)}, f32[16,1536]{1,0:T(8,128)}, u32[]{:S(2)}, u32[]{:S(2)}) collective-permute-start(f32[16,1536]{1,0:T(8,128)} %pad_maximum_fusion.21), channel_id=1, source_target_pairs={{0,1},{1,2},{2,3},{4,5},{5,6},{6,7},{8,9},{9,10},{10,11},{12,13},{... | collective-permute-start | bytes 294920 | tf_op jit(solution)/shard_map/ppermute | solution.py:728
  78.5 7.5 %maximum_maximum_fusion.3 = (bf16[1024,400]{1,0:T(8,128)(2,1)}, bf16[1024,400]{1,0:T(8,128)(2,1)}, bf16[1024,400]{1,0:T(8,128)(2,1)}, bf16[1024,400]{1,0:T(8,128)(2,1)}) fusion(bf16[512,192]{1,0:T(8,128)(2,1)S(1)} %get-tuple-element.294, bf16[512,192]{1,0:T(8,128)(2,1)S(1)} %copy-done.47, bf16[512,192]{1,0:T(8,128)(2,1)S(1)} %get-tuple-element.291, ...), kind=kLoop, calls=%fused_computation.106 | loop fusion | flops 12697600 | bytes 4850464 | tf_op jit(solution)/shard_map/concatenate | solution.py:802
  106.4 10.3 %collective-permute-done.7 = bf16[48,3072]{1,0:T(8,128)(2,1)S(1)} collective-permute-done((bf16[48,3072]{1,0:T(8,128)(2,1)S(1)}, bf16[48,3072]{1,0:T(8,128)(2,1)S(1)}, u32[]{:S(2)}, u32[]{:S(2)}) %collective-permute-start.7) | collective-permute-done | bytes 294944 | tf_op jit(solution)/shard_map/ppermute | solution.py:749
  136.7 11.1 %collective-permute-done.10 = bf16[96,1536]{1,0:T(8,128)(2,1)S(1)} collective-permute-done((bf16[96,1536]{1,0:T(8,128)(2,1)S(1)}, bf16[96,1536]{1,0:T(8,128)(2,1)S(1)}, u32[]{:S(2)}, u32[]{:S(2)}) %collective-permute-start.10) | collective-permute-done | bytes 294944 | tf_op jit(solution)/shard_map/ppermute | solution.py:749
  149.3 13.8 %fusion.164.step_ref.xv_ref.xk_ref.x_ref = f32[520,3456]{1,0:T(8,128)} fusion(bf16[520,1536]{1,0:T(8,128)(2,1)} %copy-done.14, bf16[1536,3456]{1,0:T(8,128)(2,1)} %all-gather.4.cloned.1.call-done), kind=kOutput, calls=%fused_computation.395 | convolution fusion | flops 5520752640 | bytes 19402752 | tf_op jit(solution)/shard_map/dot_general | solution.py:989
  170.2 12.7 %conv_state.1 = (f32[512,3072]{1,0:T(8,128)}, f32[512,256]{1,0:T(8,128)}, f32[128,3072]{1,0:T(8,128)}) custom-call(f32[520,3456]{1,0:T(8,128)} %fusion.164.step_ref.xv_ref.xk_ref.x_ref, f32[520,3456]{1,0:T(8,128)} %fusion.164.step_ref.xv_ref.xk_ref.x_ref, f32[8,3328]{1,0:T(8,128)} %maximum_maximum_fusion.4.tv_ref.tk_ref.tap_ref, ...), custom_call_target="tpu_custom_call" | custom-call | flops 2000000000 | bytes 20000000 | tf_op jit(solution)/shard_map/conv_state/pallas_call | solution.py:221
  191.3 19.2 %local_out.1.y_ref = f32[512,3072]{1,0:T(8,128)} custom-call(f32[512,3072]{1,0:T(8,128)} %get-tuple-element.110.v_ref, f32[512,256]{1,0:T(8,128)} %get-tuple-element.111.kq_ref, f32[6,512,8]{2,1,0:T(8,128)} %get-tuple-element.112.delta_ref, f32[6,512,8]{2,1,0:T(8,128)} %get-tuple-element.113.cum_ref, f32[48,512]{1,0:T(8,128)} %get-tuple-element.114.cumt_ref, ...), custom_call_target="tpu_custom_call" | custom-call | flops 2000000000 | bytes 20000000 | tf_op jit(solution)/shard_map/local_out/pallas_call | solution.py:303
  217.3 10.9 %fusion.135.z_ref = f32[512,3072]{1,0:T(8,128)} fusion(bf16[1536,3072]{1,0:T(8,128)(2,1)} %all-gather.6.cloned.1.call-done, bf16[520,1536]{1,0:T(8,128)(2,1)S(1)} %copy-done.15), kind=kOutput, calls=%fused_computation.384 | convolution fusion | flops 4831838208 | bytes 17301504 | tf_op jit(solution)/shard_map/dot_general | solution.py:995
  228.2 12.5 %all-gather.8.cloned.1.call-done = bf16[3072,1536]{1,0:T(8,128)(2,1)} async-done(((bf16[384,1536]{1,0:T(8,128)(2,1)}), bf16[3072,1536]{1,0:T(8,128)(2,1)}) %all-gather.8.cloned.1.call-update) | async-done | bytes 9437200 | tf_op jit(solution)/shard_map/all_gather | solution.py:735
  245.9 9.8 %convolution_bitcast_fusion.g_ref = f32[512,3072]{1,0:T(8,128)} fusion(bf16[3072,1536]{1,0:T(8,128)(2,1)} %all-gather.8.cloned.1.call-done, bf16[512,1536]{1,0:T(8,128)(2,1)} %convert_element_type.316), kind=kOutput, calls=%fused_computation.5 | convolution fusion | flops 4831838208 | bytes 17301504 | tf_op jit(solution)/shard_map/dot_general | solution.py:997
  264.0 20.4 %gate.1 = (bf16[512,3072]{1,0:T(8,128)(2,1)}, f32[512,3072]{1,0:T(8,128)}, bf16[528,3072]{1,0:T(8,128)(2,1)}, f32[128,3072]{1,0:T(8,128)}, f32[8,3072]{1,0:T(8,128)}) custom-call(f32[512,3072]{1,0:T(8,128)} %local_out.1.y_ref, f32[512,3072]{1,0:T(8,128)} %get-tuple-element.110.v_ref, f32[512,3072]{1,0:T(8,128)} %fusion.135.z_ref, ...), custom_call_target="tpu_custom_call" | custom-call | flops 1000000000 | bytes 40000000 | tf_op jit(solution)/shard_map/gate/pallas_call | solution.py:383
  286.0 10.7 %convolution_add_fusion = f32[512,1536]{1,0:T(8,128)} fusion(f32[512,1536]{1,0:T(8,128)S(1)} %copy-done, bf16[512,3072]{1,0:T(8,128)(2,1)} %get-tuple-element.125, bf16[3072,1536]{1,0:T(8,128)(2,1)} %all-gather.8.cloned.1.call-done), kind=kOutput, calls=%fused_computation.21 | convolution fusion | flops 4832624640 | bytes 18874368 | tf_op jit(solution)/shard_map/dot_general | solution.py:1010
  306.1 10.7 %fusion.137 = f32[512,1536]{1,0:T(8,128)} fusion(bf16[1536,3072]{1,0:T(8,128)(2,1)} %all-gather.6.cloned.1.call-done, bf16[528,3072]{1,0:T(8,128)(2,1)} %broadcast_dynamic-update-slice_fusion), kind=kOutput, calls=%fused_computation.386 | convolution fusion | flops 4831838208 | bytes 15728640 | tf_op jit(solution)/shard_map/dot_general | solution.py:1017
  343.6 7.3 fusion.20
  375.3 48.9 %back_first.1 = (f32[512,1536]{1,0:T(8,128)}, f32[512,256]{1,0:T(8,128)}, f32[512,128]{1,0:T(8,128)}, f32[3,512,8]{2,1,0:T(8,128)}, f32[3,512,8]{2,1,0:T(8,128)}, /*index=5*/f32[24,512]{1,0:T(8,128)}, f32[8,1536]{1,0:T(8,128)}) custom-call(f32[512,3072]{1,0:T(8,128)} %get-tuple-element.110.v_ref, f32[512,3072]{1,0:T(8,128)} %get-tuple-element.141.dy_ref, ...), custom_call_target="tpu_custom_call" | custom-call | flops 15000000512 | bytes 15000000 | tf_op jit(solution)/shard_map/back_first/pallas_call | solution.py:539
  438.1 11.1 %shard_map.581 = (bf16[528,1536]{1,0:T(8,128)(2,1)}, f32[16,1536]{1,0:T(8,128)}, f32[8,1536]{1,0:T(8,128)}) custom-call(f32[520,3456]{1,0:T(8,128)} %fusion.164.step_ref.xv_ref.xk_ref.x_ref, f32[8,3328]{1,0:T(8,128)} %maximum_maximum_fusion.4.tv_ref.tk_ref.tap_ref, f32[3,512,128]{2,1,0:T(8,128)} %broadcast_in_dim.284.match_ref, ...), custom_call_target="tpu_custom_call" | custom-call | flops 100000000 | bytes 10000000 | tf_op jit(solution)/shard_map/pallas_call | solution.py:690
  465.3 23.8 %collective-permute-done.26 = f16[208,3072]{1,0:T(8,128)(2,1)} collective-permute-done((f16[208,3072]{1,0:T(8,128)(2,1)}, f16[208,3072]{1,0:T(8,128)(2,1)}, u32[]{:S(2)}, u32[]{:S(2)}) %collective-permute-start.26) | collective-permute-done | bytes 1277984 | tf_op jit(solution)/shard_map/ppermute | solution.py:749
  508.2 48.7 %back_second.1 = (f32[512,1536]{1,0:T(8,128)}, f32[512,256]{1,0:T(8,128)}, f32[512,128]{1,0:T(8,128)}, f32[3,512,8]{2,1,0:T(8,128)}, f32[3,512,8]{2,1,0:T(8,128)}, /*index=5*/f32[24,512]{1,0:T(8,128)}, f32[8,1536]{1,0:T(8,128)}) custom-call(f32[512,3072]{1,0:T(8,128)} %get-tuple-element.110.v_ref, f32[512,3072]{1,0:T(8,128)} %get-tuple-element.141.dy_ref, ...), custom_call_target="tpu_custom_call" | custom-call | flops 15000000512 | bytes 15000000 | tf_op jit(solution)/shard_map/back_second/pallas_call | solution.py:539
  556.9 8.5 %step_back.1 = (bf16[528,128]{1,0:T(8,128)(2,1)}, f32[8,48]{1,0:T(8,128)}) custom-call(f32[520,3456]{1,0:T(8,128)} %fusion.164.step_ref.xv_ref.xk_ref.x_ref, f32[8,48]{1,0:T(8,128)} %maximum_maximum_fusion.5.par_ref, f32[3,512,8]{2,1,0:T(8,128)} %get-tuple-element.152.ddelta_a, f32[3,512,8]{2,1,0:T(8,128)} %get-tuple-element.153.ddelta_b, ...), custom_call_target="tpu_custom_call" | custom-call | flops 10000000 | bytes 10000000 | tf_op jit(solution)/shard_map/step_back/pallas_call | solution.py:628
  569.4 12.6 %shard_map.582 = (bf16[528,1792]{1,0:T(8,128)(2,1)}, f32[16,1792]{1,0:T(8,128)}, f32[8,1792]{1,0:T(8,128)}) custom-call(f32[520,3456]{1,0:T(8,128)} %fusion.164.step_ref.xv_ref.xk_ref.x_ref, f32[8,3328]{1,0:T(8,128)} %maximum_maximum_fusion.4.tv_ref.tk_ref.tap_ref, f32[3,512,128]{2,1,0:T(8,128)} %broadcast_in_dim.284.match_ref, ...), custom_call_target="tpu_custom_call" | custom-call | flops 100000000 | bytes 10000000 | tf_op jit(solution)/shard_map/pallas_call | solution.py:690
  626.2 23.6 %collective-permute-done.41 = f16[64,3072]{1,0:T(8,128)(2,1)S(1)} collective-permute-done((f16[64,3072]{1,0:T(8,128)(2,1)S(1)}, f16[64,3072]{1,0:T(8,128)(2,1)S(1)}, u32[]{:S(2)}, u32[]{:S(2)}) %collective-permute-start.41) | collective-permute-done | bytes 393248 | tf_op jit(solution)/shard_map/ppermute | solution.py:749
  691.9 8.6 %collective-permute-start.38 = (f32[168,128]{1,0:T(8,128)S(1)}, f32[168,128]{1,0:T(8,128)S(1)}, u32[]{:S(2)}, u32[]{:S(2)}) collective-permute-start(f32[168,128]{1,0:T(8,128)S(1)} %add.544), channel_id=1, source_target_pairs={{0,1},{1,0},{2,3},{3,2},{4,5},{5,4},{6,7},{7,6},{8,9},{9,8},{10,11... | collective-permute-start | bytes 258056 | tf_op jit(solution)/shard_map/ppermute | solution.py:876
  (498 shorter events, 347.1 us)
Async XLA Ops:
  7.2 142.1 %all-gather.4.cloned.1.call-start = ((), (), s32[]{:S(2)}) async-start(), calls=%async_computation | async-start | bytes 11943936 | tf_op jit(solution)/shard_map/all_gather | solution.py:735
  12.8 25.8 %collective-permute-start.2 = (bf16[48,3456]{1,0:T(8,128)(2,1)S(1)}, bf16[48,3456]{1,0:T(8,128)(2,1)S(1)}, u32[]{:S(2)}, u32[]{:S(2)}) collective-permute-start(bf16[48,3456]{1,0:T(8,128)(2,1)S(1)} %get-tuple-element.305), channel_id=1, source_target_pairs={{0,2},{1,3},{2,0},{3,1},{4,6},{5,7},{6,4},{7,5},{8,10},{9,11},{10,... | collective-permute-start | bytes 995336 | tf_op jit(solution)/shard_map/ppermute | solution.py:749
  39.8 170.7 %all-gather.6.cloned.1.call-start = ((), (), s32[]{:S(2)}) async-start(), calls=%async_computation.1 | async-start | bytes 10616832 | tf_op jit(solution)/shard_map/all_gather | solution.py:735
  53.9 32.1 %collective-permute-start.4 = (bf16[512,1536]{1,0:T(8,128)(2,1)}, bf16[512,1536]{1,0:T(8,128)(2,1)}, u32[]{:S(2)}, u32[]{:S(2)}) collective-permute-start(bf16[512,1536]{1,0:T(8,128)(2,1)} %convert_element_type.316), channel_id=1, source_target_pairs={{0,4},{4,0},{8,12},{12,8},{16,20},{20,16},{24,28},{28,24},{1,5},{5... | collective-permute-start | bytes 4718600 | tf_op jit(solution)/shard_map/ppermute | solution.py:749
  118.1 122.5 %all-gather.8.cloned.1.call-start = ((), (), s32[]{:S(2)}) async-start(), calls=%async_computation.2 | async-start | bytes 10616832 | tf_op jit(solution)/shard_map/all_gather | solution.py:735
  214.0 26.7 %collective-permute-start.13 = (bf16[128,3072]{1,0:T(8,128)(2,1)}, bf16[128,3072]{1,0:T(8,128)(2,1)}, u32[]{:S(2)}, u32[]{:S(2)}) collective-permute-start(bf16[128,3072]{1,0:T(8,128)(2,1)} %add_convert_fusion.3), channel_id=1, source_target_pairs={{0,1},{1,2},{2,3},{4,5},{5,6},{6,7},{8,9},{9,10},{10,11},{12,13},{... | collective-permute-start | bytes 2359304 | tf_op jit(solution)/shard_map/ppermute | solution.py:728
  286.0 67.9 %collective-permute-start.19 = (bf16[528,3072]{1,0:T(8,128)(2,1)}, bf16[528,3072]{1,0:T(8,128)(2,1)}, u32[]{:S(2)}, u32[]{:S(2)}) collective-permute-start(bf16[528,3072]{1,0:T(8,128)(2,1)} %broadcast_dynamic-update-slice_fusion), channel_id=1, source_target_pairs={{0,4},{4,0},{8,12},{12,8},{16,20},{20,16},{24,28},{28,24},{1,5},{5... | collective-permute-start | bytes 9732104 | tf_op jit(solution)/shard_map/ppermute | solution.py:749
  301.7 29.3 %collective-permute-start.18 = (bf16[512,784]{0,1:T(8,128)(2,1)}, bf16[512,784]{0,1:T(8,128)(2,1)}, u32[]{:S(2)}, u32[]{:S(2)}) collective-permute-start(bf16[512,784]{0,1:T(8,128)(2,1)} %copy.89), channel_id=1, source_target_pairs={{0,4},{4,0},{8,12},{12,8},{16,20},{20,16},{24,28},{28,24},{1,5},{5... | collective-permute-start | bytes 2408456 | tf_op jit(solution)/shard_map/ppermute | solution.py:749
  339.9 84.2 %collective-permute-start.21 = (f16[784,1536]{1,0:T(8,128)(2,1)}, f16[784,1536]{1,0:T(8,128)(2,1)}, u32[]{:S(2)}, u32[]{:S(2)}) collective-permute-start(f16[784,1536]{1,0:T(8,128)(2,1)} %select_convert_fusion.1), channel_id=1, source_target_pairs={{0,8},{4,12},{8,0},{12,4},{16,24},{20,28},{24,16},{28,20},{1,9},{5... | collective-permute-start | bytes 7225352 | tf_op jit(solution)/shard_map/ppermute | solution.py:749
  361.8 68.9 %collective-permute-start.22 = (f16[400,3072]{1,0:T(8,128)(2,1)}, f16[400,3072]{1,0:T(8,128)(2,1)}, u32[]{:S(2)}, u32[]{:S(2)}) collective-permute-start(f16[400,3072]{1,0:T(8,128)(2,1)} %select_convert_fusion), channel_id=1, source_target_pairs={{0,16},{4,20},{8,24},{12,28},{16,0},{20,4},{24,8},{28,12},{1,17},{... | collective-permute-start | bytes 7372808 | tf_op jit(solution)/shard_map/ppermute | solution.py:749
  458.3 30.8 %collective-permute-start.26 = (f16[208,3072]{1,0:T(8,128)(2,1)}, f16[208,3072]{1,0:T(8,128)(2,1)}, u32[]{:S(2)}, u32[]{:S(2)}) collective-permute-start(f16[208,3072]{1,0:T(8,128)(2,1)} %fusion.12), channel_id=1, source_target_pairs={{0,8},{4,12},{8,0},{12,4},{16,24},{20,28},{24,16},{28,20},{1,9},{5... | collective-permute-start | bytes 3833864 | tf_op jit(solution)/shard_map/ppermute | solution.py:749
  459.5 35.0 %collective-permute-start.25 = (f16[400,1536]{1,0:T(8,128)(2,1)}, f16[400,1536]{1,0:T(8,128)(2,1)}, u32[]{:S(2)}, u32[]{:S(2)}) collective-permute-start(f16[400,1536]{1,0:T(8,128)(2,1)} %fusion.14), channel_id=1, source_target_pairs={{0,16},{4,20},{8,24},{12,28},{16,0},{20,4},{24,8},{28,12},{1,17},{... | collective-permute-start | bytes 3686408 | tf_op jit(solution)/shard_map/ppermute | solution.py:749
  499.7 65.7 %collective-permute-start.27 = (f16[400,768]{1,0:T(8,128)(2,1)}, f16[400,768]{1,0:T(8,128)(2,1)}, u32[]{:S(2)}, u32[]{:S(2)}) collective-permute-start(f16[400,768]{1,0:T(8,128)(2,1)} %fusion.38), channel_id=1, source_target_pairs={{0,8},{4,12},{8,0},{12,4},{16,24},{20,28},{24,16},{28,20},{1,9},{5... | collective-permute-start | bytes 1843208 | tf_op jit(solution)/shard_map/ppermute | solution.py:749
  502.0 65.8 %collective-permute-start.28 = (f16[400,768]{1,0:T(8,128)(2,1)}, f16[400,768]{1,0:T(8,128)(2,1)S(1)}, u32[]{:S(2)}, u32[]{:S(2)}) collective-permute-start(f16[400,768]{1,0:T(8,128)(2,1)} %fusion.37), channel_id=1, source_target_pairs={{0,16},{4,20},{8,24},{12,28},{16,0},{20,4},{24,8},{28,12},{1,17},{... | collective-permute-start | bytes 1843208 | tf_op jit(solution)/shard_map/ppermute | solution.py:749
  504.2 114.6 %collective-permute-start.51 = (f16[112,1536]{1,0:T(8,128)(2,1)}, f16[112,1536]{1,0:T(8,128)(2,1)}, u32[]{:S(2)}, u32[]{:S(2)}) collective-permute-start(f16[112,1536]{1,0:T(8,128)(2,1)} %get-tuple-element.272), channel_id=1, source_target_pairs={{0,1},{1,0},{2,3},{3,2},{4,5},{5,4},{6,7},{7,6},{8,9},{9,8},{10,11... | collective-permute-start | bytes 1032200 | tf_op jit(solution)/shard_map/ppermute | solution.py:749
  505.9 115.8 %collective-permute-start.52 = (f16[112,1536]{1,0:T(8,128)(2,1)}, f16[112,1536]{1,0:T(8,128)(2,1)}, u32[]{:S(2)}, u32[]{:S(2)}) collective-permute-start(f16[112,1536]{1,0:T(8,128)(2,1)} %get-tuple-element.271), channel_id=1, source_target_pairs={{0,2},{1,3},{2,0},{3,1},{4,6},{5,7},{6,4},{7,5},{8,10},{9,11},{10,... | collective-permute-start | bytes 1032200 | tf_op jit(solution)/shard_map/ppermute | solution.py:749
  596.2 25.5 %collective-permute-start.53 = (f16[112,1536]{1,0:T(8,128)(2,1)S(1)}, f16[112,1536]{1,0:T(8,128)(2,1)S(1)}, u32[]{:S(2)}, u32[]{:S(2)}) collective-permute-start(f16[112,1536]{1,0:T(8,128)(2,1)S(1)} %copy-done.54), channel_id=1, source_target_pairs={{0,3},{1,2},{2,1},{3,0},{4,7},{5,6},{6,5},{7,4},{8,11},{9,10},{10,... | collective-permute-start | bytes 1032200 | tf_op jit(solution)/shard_map/ppermute | solution.py:749
  604.8 44.9 %collective-permute-start.41 = (f16[64,3072]{1,0:T(8,128)(2,1)S(1)}, f16[64,3072]{1,0:T(8,128)(2,1)S(1)}, u32[]{:S(2)}, u32[]{:S(2)}) collective-permute-start(f16[64,3072]{1,0:T(8,128)(2,1)S(1)} %copy-done.52), channel_id=1, source_target_pairs={{0,2},{1,3},{2,0},{3,1},{4,6},{5,7},{6,4},{7,5},{8,10},{9,11},{10,... | collective-permute-start | bytes 1179656 | tf_op jit(solution)/shard_map/ppermute | solution.py:749
  618.8 32.0 %collective-permute-start.42 = (f16[64,3072]{1,0:T(8,128)(2,1)S(1)}, f16[64,3072]{1,0:T(8,128)(2,1)S(1)}, u32[]{:S(2)}, u32[]{:S(2)}) collective-permute-start(f16[64,3072]{1,0:T(8,128)(2,1)S(1)} %copy-done.51), channel_id=1, source_target_pairs={{0,3},{1,2},{2,1},{3,0},{4,7},{5,6},{6,5},{7,4},{8,11},{9,10},{10,... | collective-permute-start | bytes 1179656 | tf_op jit(solution)/shard_map/ppermute | solution.py:749
  621.7 55.1 %collective-permute-start.43 = (f16[64,1536]{1,0:T(8,128)(2,1)}, f16[64,1536]{1,0:T(8,128)(2,1)}, u32[]{:S(2)}, u32[]{:S(2)}) collective-permute-start(f16[64,1536]{1,0:T(8,128)(2,1)} %get-tuple-element.287), channel_id=1, source_target_pairs={{0,1},{1,0},{2,3},{3,2},{4,5},{5,4},{6,7},{7,6},{8,9},{9,8},{10,11... | collective-permute-start | bytes 589832 | tf_op jit(solution)/shard_map/ppermute | solution.py:749
  621.8 55.1 %collective-permute-start.44 = (f16[64,1536]{1,0:T(8,128)(2,1)}, f16[64,1536]{1,0:T(8,128)(2,1)}, u32[]{:S(2)}, u32[]{:S(2)}) collective-permute-start(f16[64,1536]{1,0:T(8,128)(2,1)} %get-tuple-element.288), channel_id=1, source_target_pairs={{0,2},{1,3},{2,0},{3,1},{4,6},{5,7},{6,4},{7,5},{8,10},{9,11},{10,... | collective-permute-start | bytes 589832 | tf_op jit(solution)/shard_map/ppermute | solution.py:749
  623.2 53.7 %collective-permute-start.45 = (f16[64,1536]{1,0:T(8,128)(2,1)S(1)}, f16[64,1536]{1,0:T(8,128)(2,1)}, u32[]{:S(2)}, u32[]{:S(2)}) collective-permute-start(f16[64,1536]{1,0:T(8,128)(2,1)S(1)} %get-tuple-element.286), channel_id=1, source_target_pairs={{0,3},{1,2},{2,1},{3,0},{4,7},{5,6},{6,5},{7,4},{8,11},{9,10},{10,... | collective-permute-start | bytes 589832 | tf_op jit(solution)/shard_map/ppermute | solution.py:749
  671.6 28.9 %collective-permute-start.46 = (f16[208,896]{1,0:T(8,128)(2,1)S(1)}, f16[208,896]{1,0:T(8,128)(2,1)S(1)}, u32[]{:S(2)}, u32[]{:S(2)}) collective-permute-start(f16[208,896]{1,0:T(8,128)(2,1)S(1)} %fusion.44), channel_id=1, source_target_pairs={{0,16},{4,20},{8,24},{12,28},{16,0},{20,4},{24,8},{28,12},{1,17},{... | collective-permute-start | bytes 1118216 | tf_op jit(solution)/shard_map/ppermute | solution.py:749
  675.9 30.1 %collective-permute-start.47 = (f16[208,1024]{1,0:T(8,128)(2,1)S(1)}, f16[208,1024]{1,0:T(8,128)(2,1)S(1)}, u32[]{:S(2)}, u32[]{:S(2)}) collective-permute-start(f16[208,1024]{1,0:T(8,128)(2,1)S(1)} %fusion.42), channel_id=1, source_target_pairs={{0,8},{4,12},{8,0},{12,4},{16,24},{20,28},{24,16},{28,20},{1,9},{5... | collective-permute-start | bytes 1277960 | tf_op jit(solution)/shard_map/ppermute | solution.py:749
  (122 other events, 2121.5 us)
Sparse Core Ops, SparseCore 0:
  39.9 68.5 all-gather.3
  118.3 61.1 all-gather.5
  181.9 58.6 all-gather.7

commit v4 on v3

--- a/solution.py
+++ b/solution.py
@@ -179,7 +179,7 @@
 
 
 def conv_kernel(
-    xv_ref, xk_ref, tv_ref, tk_ref, match_ref, taild_ref, v_ref, kq_ref, state_ref, kt_hi, kt_lo
+    xv_ref, xk_ref, tv_ref, tk_ref, match_ref, taild_ref, v_ref, kq_ref, state_ref, state_half_ref, kt_hi, kt_lo
 ):
     length = v_ref.shape[0]
     count = length // Q
@@ -212,6 +212,7 @@
         kh, kl = kt_hi[:, rows], kt_lo[:, rows]
         total = total + (dot1(kh, hi) + (dot1(kh, lo) + dot1(kl, hi)))
     state_ref[...] = total
+    state_half_ref[...] = total.astype(bf16)
 
 
 def conv_state(rest, taps, match, taild):
@@ -233,11 +234,13 @@
             pl.BlockSpec((length, GW), lambda g: (0, g)),
             pl.BlockSpec((length, 2 * STATE), lambda g: (0, 0)),
             pl.BlockSpec((STATE, GW), lambda g: (0, g)),
+            pl.BlockSpec((STATE, GW), lambda g: (0, g)),
         ),
         out_shape=(
             jax.ShapeDtypeStruct((length, DI), f32),
             jax.ShapeDtypeStruct((length, 2 * STATE), f32),
             jax.ShapeDtypeStruct((STATE, DI), f32),
+            jax.ShapeDtypeStruct((STATE, DI), bf16),
         ),
         scratch_shapes=[pltpu.VMEM((STATE, length), bf16), pltpu.VMEM((STATE, length), bf16)],
         compiler_params=params(),
@@ -326,8 +329,8 @@
 
 
 def gate_kernel(
-    y_ref, v_ref, z_ref, g_ref, kq_ref, inc_ref, infd_ref, dir_ref, gam_ref,
-    out_ref, dy_ref, dz_ref, dinc_ref, small_ref, ybuf, rbuf,
+    block, at_ref, y_ref, v_ref, z_ref, g_ref, kq_ref, inc_ref, infd_ref, dir_ref, gam_ref,
+    out_ref, blocks_ref, dy_ref, dz_ref, dinc_ref, dinc_half_ref, small_ref, ybuf, rbuf,
 ):
     first = pl.program_id(0) == 0
     rows = y_ref.shape[0]
@@ -359,7 +362,14 @@
         gated = rbuf[:, cols]
         scaled = gated * inv
         gam = gam_ref[0:1, cols]
-        out_ref[:, cols] = (scaled * gam).astype(bf16)
+        half = (scaled * gam).astype(bf16)
+        out_ref[:, cols] = half
+        if block:
+            per = block // 128
+            far = ((j // per) >> 1) ^ at_ref[0]
+            which = 2 * (((j // per) & 1) ^ at_ref[1]) + (far & 1)
+            place = pl.multiple_of((far >> 1) * block + (j % per) * 128, 128)
+            blocks_ref[which, :, pl.ds(place, 128)] = half
         g = g_ref[:, cols]
         dgated = inv * (g * gam) - gated * slope
         z = z_ref[:, cols]
@@ -375,39 +385,48 @@
         small_ref[1:2, cols] += jnp.sum(dy * v_ref[:, cols], axis=0, keepdims=True)
         dinc_ref[:, cols] += dot3(qt, dy * pair_lanes(inflow, j))
 
-
-def gate(y, v, z, g, kq, inc, infd, dirx, gam):
+    @pl.when(pl.program_id(0) == pl.num_programs(0) - 1)
+    def _():
+        dinc_half_ref[...] = dinc_ref[...].astype(bf16)
+
+
+def gate(block, at, y, v, z, g, kq, inc, infd, dirx, gam):
     length = y.shape[0]
     tile = Q
-    big = pl.BlockSpec((tile, DI), lambda i: (i, 0))
+    big = pl.BlockSpec((tile, DI), lambda i, at: (i, 0))
+    fixed = lambda rows: pl.BlockSpec((rows, DI), lambda i, at: (0, 0))
+    spare = 2 * block if block else 128
     return pl.pallas_call(
-        gate_kernel,
-        grid=(length // tile,),
-        in_specs=[
-            big, big, big, big,
-            pl.BlockSpec((tile, 2 * STATE), lambda i: (i, 0)),
-            pl.BlockSpec((STATE, DI), lambda i: (0, 0)),
-            pl.BlockSpec((tile, HEADS), lambda i: (i, 0)),
-            pl.BlockSpec((8, DI), lambda i: (0, 0)),
-            pl.BlockSpec((8, DI), lambda i: (0, 0)),
-        ],
-        out_specs=(
-            big, big, big,
-            pl.BlockSpec((STATE, DI), lambda i: (0, 0)),
-            pl.BlockSpec((8, DI), lambda i: (0, 0)),
+        functools.partial(gate_kernel, block),
+        grid_spec=pltpu.PrefetchScalarGridSpec(
+            num_scalar_prefetch=1,
+            grid=(length // tile,),
+            in_specs=[
+                big, big, big, big,
+                pl.BlockSpec((tile, 2 * STATE), lambda i, at: (i, 0)),
+                fixed(STATE),
+                pl.BlockSpec((tile, HEADS), lambda i, at: (i, 0)),
+                fixed(8), fixed(8),
+            ],
+            out_specs=(
+                big, pl.BlockSpec((4, tile, spare), lambda i, at: (0, i, 0)), big, big,
+                fixed(STATE), fixed(STATE), fixed(8),
+            ),
+            scratch_shapes=[pltpu.VMEM((tile, DI), f32), pltpu.VMEM((tile, DI), f32)],
         ),
         out_shape=(
             jax.ShapeDtypeStruct((length, DI), bf16),
+            jax.ShapeDtypeStruct((4, length, spare), bf16),
             jax.ShapeDtypeStruct((length, DI), f32),
             jax.ShapeDtypeStruct((length + PAD, DI), bf16),
             jax.ShapeDtypeStruct((STATE, DI), f32),
+            jax.ShapeDtypeStruct((STATE, DI), bf16),
             jax.ShapeDtypeStruct((8, DI), f32),
         ),
-        scratch_shapes=[pltpu.VMEM((tile, DI), f32), pltpu.VMEM((tile, DI), f32)],
         compiler_params=params(),
         cost_estimate=pl.CostEstimate(flops=10**9, bytes_accessed=4 * 10**7, transcendentals=4 * 10**6),
         name="gate",
-    )(y, v, z, g, kq, inc, infd, dirx, gam)
+    )(at, y, v, z, g, kq, inc, infd, dirx, gam)
 
 
 def back_kernel(
@@ -735,13 +754,13 @@
     return lax.all_gather(value, "dp", axis=0, tiled=True)
 
 
-def shard_gathered(value):
+def shard_gathered(value, *earlier):
     count, here = lax.axis_size("shard"), lax.axis_index("shard")
     rows, width = value.shape
+    parts = [exchanged(value, "shard", k) for k in range(1, count)]
     held = jnp.zeros((count * rows, width), value.dtype)
-    for k in range(count):
-        part = exchanged(value, "shard", k) if k else value
-        held = lax.dynamic_update_slice(held, part, ((here ^ k) * rows, 0))
+    for k, part in enumerate([value] + parts):
+        held = lax.dynamic_update_slice(held, after(part, earlier) if k else part, ((here ^ k) * rows, 0))
     return held
 
 
@@ -772,13 +791,17 @@
 
 
 def coded(total, power, rows):
-    own = iota(total.shape, 0) < rows
-    return jnp.where(own, total * jnp.exp2(15.0 - power), power).astype(jnp.float16)
-
-
-def decoded(payload, rows):
-    power = payload[rows : rows + 1].astype(f32)
-    return payload.astype(f32) * jnp.exp2(power - 15.0), power
+    scaled = total * jnp.exp2(15.0 - power)
+    if total.shape[0] > rows:
+        scaled = jnp.where(iota(total.shape, 0) < rows, scaled, power)
+    return scaled.astype(jnp.float16)
+
+
+def decoded(payload, power, rows):
+    if payload.shape[0] == rows:
+        return payload.astype(f32) * jnp.exp2(power - 15.0), power
+    other = payload[rows : rows + 1].astype(f32)
+    return payload.astype(f32) * jnp.exp2(other - 15.0), jnp.maximum(power, other) + 1.0
 
 
 def after(value, *earlier):
@@ -794,21 +817,22 @@
     return kept, sends
 
 
-def columns_of(blocks, order):
+def columns_of(blocks, order, pad):
     kept, sends = split_plan(order)
-    zeros = jnp.zeros((blocks[0].shape[0], PAD), bf16)
+    zeros = [jnp.zeros((blocks[0].shape[0], pad), bf16)] if pad else []
     return (
-        jnp.concatenate([blocks[j] for j in sends[0]] + [zeros], axis=1),
-        jnp.concatenate([blocks[j] for j in kept[: len(sends[0])]] + [zeros], axis=1),
+        jnp.concatenate([blocks[j] for j in kept[: len(sends[0])]] + zeros, axis=1),
+        jnp.concatenate([blocks[j] for j in sends[0]] + zeros, axis=1),
     )
 
 
 class Sum:
-    def __init__(self, sent, held, rhs, bound, order):
-        self.sent, self.held, self.rhs = sent, held, rhs
-        self.power = exponent(bound)
+    def __init__(self, held, sent, rhs, power, order, pad):
+        self.held, self.sent, self.rhs = held, sent, rhs
+        self.power = power
         self.order = order
-        self.rows = 2 * (sent.shape[1] - PAD)
+        self.pad = pad
+        self.rows = 2 * (sent.shape[1] - pad)
         self.total = None
         self.at = 0
 
@@ -817,7 +841,7 @@
         if self.total is None:
             part = lax.dot_general(self.sent, self.rhs, TOKENS, preferred_element_type=f32)
         else:
-            part = self.total[self.rows : 2 * self.rows + PAD]
+            part = self.total[self.rows : 2 * self.rows + self.pad]
         self.payload = coded(part, self.power, self.rows)
 
     def send(self):
@@ -827,9 +851,8 @@
             self.total = lax.dot_general(self.held, self.rhs, TOKENS, preferred_element_type=f32)
 
     def take(self, *earlier):
-        got, other = decoded(after(self.got, earlier), self.rows)
-        self.total = self.total[: self.rows + PAD] + got
-        self.power = jnp.maximum(self.power, other) + 1.0
+        got, self.power = decoded(after(self.got, earlier), self.power, self.rows)
+        self.total = self.total[: self.rows + self.pad] + got
 
     def more(self):
         return self.at < len(self.order)
@@ -846,13 +869,10 @@
         count, here = lax.axis_size("shard"), lax.axis_index("shard")
         self.rows = sums[0].rows // count
         self.total = jnp.concatenate([one.total for one in sums], axis=1) if len(sums) > 1 else sums[0].total
-        power = jnp.concatenate([one.power for one in sums], axis=1) if len(sums) > 1 else sums[0].power
-        width = self.total.shape[1]
+        self.power = jnp.concatenate([one.power for one in sums], axis=1) if len(sums) > 1 else sums[0].power
+        taken = (self.rows + sums[0].pad, self.total.shape[1])
         self.payloads = [
-            coded(
-                lax.dynamic_slice(self.total, ((here ^ k) * self.rows, 0), (self.rows + PAD, width)),
-                power, self.rows,
-            )
+            coded(lax.dynamic_slice(self.total, ((here ^ k) * self.rows, 0), taken), self.power, self.rows)
             for k in range(1, count)
         ]
         self.parts = [exchanged(part, "shard", k + 1) for k, part in enumerate(self.payloads)]
@@ -861,7 +881,7 @@
         here = lax.axis_index("shard")
         result = lax.dynamic_slice(self.total, (here * self.rows, 0), (self.rows, self.total.shape[1]))
         for part in self.parts:
-            result = result + decoded(after(part, earlier), self.rows)[0][: self.rows]
+            result = result + decoded(after(part, earlier), self.power, self.rows)[0][: self.rows]
         return result
 
 
@@ -878,8 +898,8 @@
     return value
 
 
-def carried(state, factor, by):
-    incoming = shifted(state.astype(bf16), "shard", by)
+def carried(state, half, factor, by):
+    incoming = shifted(half, "shard", by)
     for _ in range(1, lax.axis_size("shard") - 1):
         passed = (state + factor * incoming.astype(f32)).astype(bf16)
         incoming = shifted(passed, "shard", by)
@@ -902,9 +922,10 @@
 
 def rest_sums(both, bound, in_columns, orders):
     middle = both.shape[1] // 256 * 128
+    power = exponent(bound)
     return [
-        Sum(*in_columns[0], both[:, :middle], bound[:, :middle], orders[0]),
-        Sum(*in_columns[1], both[:, middle:], bound[:, middle:], orders[1]),
+        Sum(*in_columns[0], both[:, :middle], power[:, :middle], orders[0], PAD),
+        Sum(*in_columns[1], both[:, middle:], power[:, middle:], orders[1], PAD),
     ]
 
 
@@ -920,7 +941,12 @@
     length, width = hidden_in.shape
     own_inputs = param_inputs.astype(bf16)
     spare = -(param_inputs.shape[1] - DI) % 128
-    rest_rows = shard_gathered(jnp.pad(own_inputs[:, DI:], ((0, 0), (0, spare))))
+    upstream = cotangent.astype(bf16)
+    own_rows = param_inputs.shape[0]
+    most = jnp.broadcast_to((jnp.max(jnp.abs(cotangent)) * 1.01).astype(bf16), (own_rows, 1))
+    rest_rows = shard_gathered(
+        jnp.concatenate([own_inputs[:, DI:], most, jnp.zeros((own_rows, spare - 1), bf16)], axis=1),
+    )
     rest_w = gathered(rest_rows)
 
     seg = segment_ids.astype(f32)
@@ -963,53 +989,59 @@
     inv = lax.rsqrt(jnp.mean(hidden * hidden, axis=1, keepdims=True) + norm_eps)
     normed = (hidden * inv * param_prenorm).astype(bf16)
     own_normed = normed[HALO:]
-    upstream = cotangent.astype(bf16)
 
     groups = lax.axis_size("shard")
     spots = [bit for bit in range(20) if (2 << bit) < lax.axis_size("dp")]
     orders = (spots, spots[::-1])
     in_block, out_block = groups * param_inputs.shape[0], groups * param_outputs.shape[0]
-    up_both = both_cores(upstream)
+    up_both = both_cores(after(upstream, rest_rows))
     own_blocks, partner_blocks = own_and_partner(own_normed, in_block)
     arrived = exchanged(jnp.concatenate(partner_blocks, axis=1), "dp", 1)
     both_blocks = [
         jnp.concatenate([one, arrived[:, j * in_block : (j + 1) * in_block]], axis=0)
         for j, one in enumerate(own_blocks)
     ]
-    in_columns = [columns_of(both_blocks, order) for order in orders]
+    in_columns = [columns_of(both_blocks, order, PAD) for order in orders]
     norm_bound = 2.02 * length * width**0.5 * jnp.max(jnp.abs(param_prenorm))
-    out_bound = 2.02 * length * DI**0.5 * jnp.max(jnp.abs(param_gating))
-    out_bound = out_bound * jnp.max(jnp.abs(up_both), axis=0, keepdims=True).astype(f32)
-    early = (match, mask, segc, segr, taps, pars, dirx, gam, up_both, out_bound, norm_bound, in_columns, normed)
-    gate_rows = shard_gathered(after(own_inputs[:, :DI], rest_rows, early))
+    early = (match, mask, segc, segr, taps, pars, dirx, gam, up_both, norm_bound, in_columns, normed)
+    gate_rows = shard_gathered(after(own_inputs[:, :DI], rest_rows), early)
     gate_w = gathered(gate_rows)
-    out_w = gathered(shard_gathered(after(param_outputs.astype(bf16), gate_rows)))
     rest_w = after(rest_w, early)
 
     rest = jnp.dot(normed, rest_w, preferred_element_type=f32)
     delta, cum, cumt, infc, tailc, tailn, taild, infd, keep, factor = prep(rest, pars, mask)
-    v, kq, state = conv_state(rest, taps, match, taild)
-    incoming = carried(state, factor[0:1], 1)
+    v, kq, state, state_half = conv_state(rest, taps, match, taild)
+    out_rows = shard_gathered(after(param_outputs.astype(bf16), gate_rows), v)
+    out_w = gathered(out_rows)
+    state = after(state, out_rows)
+    incoming = carried(state, state_half, factor[0:1], 1)
     y = local_out(v, kq, delta, cum, cumt, infc, tailc, keep, segc, segr)
     gate_w = after(gate_w, y)
     z = jnp.dot(own_normed, gate_w, preferred_element_type=f32)
     out_w = after(out_w, z)
     back_gated = lax.dot_general(upstream, out_w, NT, preferred_element_type=f32)
-    gated, dy, dz, dinc, small = gate(y, v, z, back_gated, kq, incoming, infd, dirx, gam)
-
-    outgoing = carried(dinc, factor[0:1], -1)
-    own_blocks, partner_blocks = own_and_partner(gated, out_block)
-    out_columns = [
-        jnp.concatenate([mine, exchanged(theirs, "dp", 1)], axis=0)
-        for mine, theirs in zip(columns_of(own_blocks, spots), columns_of(partner_blocks, spots))
-    ]
+    tokens = length * lax.axis_size("dp") * groups
+    cotangent_most = jnp.max(rest_w[:, param_inputs.shape[1] - DI]).astype(f32)
+    out_power = exponent(1.02 * tokens * DI**0.5 * jnp.max(jnp.abs(param_gating)) * cotangent_most)
+    place = lax.axis_index("dp")
+    block = out_block if out_block % 128 == 0 and len(spots) == 2 else 0
+    at = jnp.stack([place // 2, place % 2]).astype(jnp.int32)
+    gated, blocks, dy, dz, dinc, dinc_half, small = gate(
+        block, at, y, v, z, back_gated, kq, incoming, infd, dirx, gam
+    )
+
+    outgoing = carried(dinc, dinc_half, factor[0:1], -1)
+    if not block:
+        own_blocks, partner_blocks = own_and_partner(gated, out_block)
+        blocks = jnp.stack([*columns_of(own_blocks, spots, 0), *columns_of(partner_blocks, spots, 0)])
+    arrived = exchanged(blocks[2:], "dp", 1)
+    out_columns = [jnp.concatenate([blocks[i], arrived[i]], axis=0) for i in range(2)]
     dz_most = jnp.broadcast_to(small[2:3] * 1.01, (PAD, DI)).astype(bf16)
     dz = lax.dynamic_update_slice(dz, dz_most, (length, 0))
     dz_both, dz_bound = both_with_most(dz)
-    dz = dz[:length]
     block_out = hidden_in + jnp.dot(gated, out_w, preferred_element_type=f32)
-    out_sum = Sum(*out_columns, up_both, out_bound, spots)
-    gate_sum = Sum(*in_columns[1], dz_both, norm_bound * dz_bound, spots[::-1])
+    out_sum = Sum(*out_columns, up_both, out_power, spots, 0)
+    gate_sum = Sum(*in_columns[1], dz_both, exponent(norm_bound * dz_bound), spots[::-1], PAD)
     first_sums = [out_sum, gate_sum]
     for one in first_sums:
         one.prepare()
@@ -1062,16 +1094,17 @@
     shard1 = ShardSum(sums1)
     drest1, drest2 = after((drest1, drest2), shard1.payloads, [two.payload for two in sums2])
     wide1 = drest1.shape[1]
-    back_normed = back_normed + lax.dot_general(drest1[:length], rest_w[:, :wide1], NT, preferred_element_type=f32)
-    back_normed = back_normed + lax.dot_general(drest2[:length], rest_w[:, wide1:], NT, preferred_element_type=f32)
-    grad_outputs = shard_out.take(drest2)
-    grad_gate = shard_gate.take(drest2)
+    back_normed = back_normed + lax.dot_general(drest1, rest_w[:, :wide1], NT, preferred_element_type=f32)
+    back_normed = back_normed + lax.dot_general(drest2, rest_w[:, wide1:], NT, preferred_element_type=f32)
+    back_normed = back_normed[:length]
     for one in sums2:
         one.take(back_normed)
         if one.more():
             one.prepare()
             one.send()
     sent = [one.payload for one in sums2]
+    grad_outputs = shard_out.take(sent)
+    grad_gate = shard_gate.take(sent)
     for one in sums2:
         one.take()
         one.finish()

time: 749 us -> 718 us (0.959)
  other arithmetic: 115 us -> 95.7 us
    ppermute x40 -> x39, waiting for transfers between devices: 110 us -> 86.8 us  [exchanged(): lax.ppermute(value, axis, [(i, i ^ by) for i in range(lax.axis_size(axis))])]
    all_gather x3, waiting for transfers between devices: 12.5 us -> 29.4 us  [gathered(): return lax.all_gather(value, 'dp', axis=0, tiled=True)]
    add x17 -> x16, other arithmetic: 21.5 us -> 18.1 us  [the longest x9 13.2 us: take(): self.total = self.total[:self.rows + self.pad] + got]
    ppermute x40 -> x39, starting transfers between devices: 50.1 us -> 50.1 us  [exchanged(): lax.ppermute(value, axis, [(i, i ^ by) for i in range(lax.axis_size(axis))])]
  transfers between devices with their start and end apart: 57 -> 56, of which waited for: 20 -> 20; matrix products, arithmetic and copies ran while one was open for 34% -> 31% of each run, Pallas kernels for 21% -> 22%
where the time goes in v4:
time: 718 us; the launch traced here: 709 us
  Pallas kernels  192 us (27%)
  waiting for transfers between devices  166 us (23%)
  matrix products  97.6 us (14%)
  other arithmetic  95.7 us (13%)
  starting transfers between devices  83.7 us (12%)
  local copies, waits for them, and re-layouts  55.3 us (8%)
  between operations  18.5 us (3%)
    pallas_call x2, Pallas kernels, back_local(): pl.pallas_call(functools.partial(back_kernel, last == NG), grid=(groups,)...  97.6 us
    ppermute x39, waiting for transfers between devices, exchanged(): lax.ppermute(value, axis, [(i, i ^ by) for i in range(lax.axis_size(axis))])  86.8 us
    ppermute x39, starting transfers between devices, exchanged(): lax.ppermute(value, axis, [(i, i ^ by) for i in range(lax.axis_size(axis))])  50.1 us
    ppermute x9, waiting for transfers between devices, shifted(): return lax.ppermute(value, axis, pairs)  32.4 us
    all_gather x3, waiting for transfers between devices, gathered(): return lax.all_gather(value, 'dp', axis=0, tiled=True)  29.4 us
    ppermute x9, starting transfers between devices, shifted(): return lax.ppermute(value, axis, pairs)  26.4 us
    pallas_call x2, Pallas kernels, unconv(): pl.pallas_call(functools.partial(unconv_kernel, mixed), grid=(tiles,), in...  23.7 us
    pallas_call x1, Pallas kernels, gate(): pl.pallas_call(functools.partial(gate_kernel, block), grid_spec=pltpu.Pre...  23.1 us
  transfers between devices with their start and end apart: 56, of which 20 were waited for; matrix products, arithmetic and copies ran while one was open for 31% of the time, Pallas kernels for 22%

profile of v4, /device:TPU:0, one launch (start us, length us, event | category | flops | bytes accessed | tf_op | source)
XLA Modules:
  0.0 708.6 jit_solution(14903234888333054559)
XLA Ops:
  21.7 9.6 %collective-permute-done.1 = bf16[48,3456]{1,0:T(8,128)(2,1)S(1)} collective-permute-done((bf16[48,3456]{1,0:T(8,128)(2,1)S(1)}, bf16[48,3456]{1,0:T(8,128)(2,1)S(1)}, u32[]{:S(2)}, u32[]{:S(2)}) %collective-permute-start.1) | collective-permute-done | bytes 331808 | tf_op jit(solution)/shard_map/ppermute | solution.py:768
  32.1 11.0 %collective-permute-done.2 = bf16[48,3456]{1,0:T(8,128)(2,1)} collective-permute-done((bf16[48,3456]{1,0:T(8,128)(2,1)S(1)}, bf16[48,3456]{1,0:T(8,128)(2,1)}, u32[]{:S(2)}, u32[]{:S(2)}) %collective-permute-start.2) | collective-permute-done | bytes 331808 | tf_op jit(solution)/shard_map/ppermute | solution.py:768
  113.7 12.3 %fusion.130.step_ref.xv_ref.xk_ref.x_ref = f32[520,3456]{1,0:T(8,128)} fusion(bf16[520,1536]{1,0:T(8,128)(2,1)} %copy-done.12, bf16[1536,3456]{1,0:T(8,128)(2,1)} %all-gather.4.cloned.1.call-done), kind=kOutput, calls=%fused_computation.354 | convolution fusion | flops 5520752640 | bytes 19402752 | tf_op jit(solution)/shard_map/dot_general | solution.py:1011
  126.0 7.1 %prep.1 = (f32[6,512,8]{2,1,0:T(8,128)}, f32[6,512,8]{2,1,0:T(8,128)}, f32[48,512]{1,0:T(8,128)}, f32[6,512,8]{2,1,0:T(8,128)}, f32[6,512,8]{2,1,0:T(8,128)}, /*...) custom-call(f32[520,3456]{1,0:T(8,128)} %fusion.130.step_ref.xv_ref., ...), custom_call_target="tpu_custom_call" | custom-call | flops 10000000 | bytes 10000000 | tf_op jit(solution)/shard_map/prep/pallas_call | solution.py:159
  133.1 12.7 %conv_state.1 = (f32[512,3072]{1,0:T(8,128)}, f32[512,256]{1,0:T(8,128)}, f32[128,3072]{1,0:T(8,128)}, bf16[128,3072]{1,0:T(8,128)(2,1)}) custom-call(f32[520,3456]{1,0:T(8,128)} %fusion.130.step_ref.xv_ref.xk_ref.x_ref, f32[520,3456]{1,0:T(8,128)} %fusion.130.step_ref.xv_ref.xk_ref.x_ref, f32[8,3328]{1,0:T(8,128)} %maximum_maximum_fusion.4.tv_ref.tk_ref.tap_ref, ...), custom_call_target="tpu_custom_call" | custom-call | flops 2000000000 | bytes 20000000 | tf_op jit(solution)/shard_map/conv_state/pallas_call | solution.py:222
  158.1 19.1 %local_out.1.y_ref = f32[512,3072]{1,0:T(8,128)} custom-call(f32[512,3072]{1,0:T(8,128)} %get-tuple-element.122.v_ref, f32[512,256]{1,0:T(8,128)} %get-tuple-element.123.kq_ref, f32[6,512,8]{2,1,0:T(8,128)} %get-tuple-element.124.delta_ref, f32[6,512,8]{2,1,0:T(8,128)} %get-tuple-element.125.cum_ref, f32[48,512]{1,0:T(8,128)} %get-tuple-element.126.cumt_ref, ...), custom_call_target="tpu_custom_call" | custom-call | flops 2000000000 | bytes 20000000 | tf_op jit(solution)/shard_map/local_out/pallas_call | solution.py:306
  185.0 11.4 %fusion.107.z_ref = f32[512,3072]{1,0:T(8,128)} fusion(bf16[1536,3072]{1,0:T(8,128)(2,1)} %all-gather.6.cloned.1.call-done, bf16[520,1536]{1,0:T(8,128)(2,1)S(1)} %copy-done.13), kind=kOutput, calls=%fused_computation.345 | convolution fusion | flops 4831838208 | bytes 17301504 | tf_op jit(solution)/shard_map/dot_general | solution.py:1020
  207.7 28.3 %all-gather.8.cloned.1.call-done = bf16[3072,1536]{1,0:T(8,128)(2,1)} async-done(((bf16[384,1536]{1,0:T(8,128)(2,1)}), bf16[3072,1536]{1,0:T(8,128)(2,1)}) %all-gather.8.cloned.1.call-update) | async-done | bytes 9437200 | tf_op jit(solution)/shard_map/all_gather | solution.py:754
  236.0 9.8 %convolution_bitcast_fusion.g_ref = f32[512,3072]{1,0:T(8,128)} fusion(bf16[3072,1536]{1,0:T(8,128)(2,1)} %all-gather.8.cloned.1.call-done, bf16[512,1536]{1,0:T(8,128)(2,1)} %get-tuple-element.119), kind=kOutput, calls=%fused_computation.5 | convolution fusion | flops 4831838208 | bytes 17301504 | tf_op jit(solution)/shard_map/dot_general | solution.py:1022
  245.8 23.1 %gate.1 = (bf16[512,3072]{1,0:T(8,128)(2,1)}, bf16[4,512,768]{2,1,0:T(8,128)(2,1)}, f32[512,3072]{1,0:T(8,128)}, bf16[528,3072]{1,0:T(8,128)(2,1)}, f32[128,3072...) custom-call(s32[2]{0:T(128)} %pad_add_fusion.at_ref, f32[512,3072]{1,0:T(8,128)} %local_out.1.y_ref, ...), custom_call_target="tpu_custom_call" | custom-call | flops 1000000000 | bytes 40000000 | tf_op jit(solution)/shard_map/gate/pallas_call | solution.py:399
  271.8 10.1 %fusion.131 = f32[528,1536]{1,0:T(8,128)} fusion(bf16[528,3072]{1,0:T(8,128)(2,1)} %broadcast_dynamic-update-slice_fusion, bf16[1536,3072]{1,0:T(8,128)(2,1)} %all-gather.6.cloned.1.call-done), kind=kOutput, calls=%fused_computation.355 | convolution fusion | flops 4982833152 | bytes 15925248 | tf_op jit(solution)/shard_map/dot_general | solution.py:1049
  282.6 9.0 %collective-permute-done.15 = bf16[128,3072]{1,0:T(8,128)(2,1)S(1)} collective-permute-done((bf16[128,3072]{1,0:T(8,128)(2,1)}, bf16[128,3072]{1,0:T(8,128)(2,1)S(1)}, u32[]{:S(2)}, u32[]{:S(2)}) %collective-permute-start.15) | collective-permute-done | bytes 786464 | tf_op jit(solution)/shard_map/ppermute | solution.py:747
  293.4 7.8 %convolution_add_fusion = f32[512,1536]{1,0:T(8,128)} fusion(f32[512,1536]{1,0:T(8,128)S(1)} %copy-done, bf16[512,3072]{1,0:T(8,128)(2,1)} %get-tuple-element.145, bf16[3072,1536]{1,0:T(8,128)(2,1)S(1)} %bitcast.121), kind=kOutput, calls=%fused_computation.19 | convolution fusion | flops 4832624640 | bytes 18874368 | tf_op jit(solution)/shard_map/dot_general | solution.py:1042
  301.5 11.1 %collective-permute-done.16 = bf16[128,3072]{1,0:T(8,128)(2,1)S(1)} collective-permute-done((bf16[128,3072]{1,0:T(8,128)(2,1)S(1)}, bf16[128,3072]{1,0:T(8,128)(2,1)S(1)}, u32[]{:S(2)}, u32[]{:S(2)}) %collective-permute-start.16) | collective-permute-done | bytes 786464 | tf_op jit(solution)/shard_map/ppermute | solution.py:747
  339.8 48.9 %back_first.1 = (f32[512,1536]{1,0:T(8,128)}, f32[512,256]{1,0:T(8,128)}, f32[512,128]{1,0:T(8,128)}, f32[3,512,8]{2,1,0:T(8,128)}, f32[3,512,8]{2,1,0:T(8,128)}, /*index=5*/f32[24,512]{1,0:T(8,128)}, f32[8,1536]{1,0:T(8,128)}) custom-call(f32[512,3072]{1,0:T(8,128)} %get-tuple-element.122.v_ref, f32[512,3072]{1,0:T(8,128)} %get-tuple-element.163.dy_ref, ...), custom_call_target="tpu_custom_call" | custom-call | flops 15000000512 | bytes 15000000 | tf_op jit(solution)/shard_map/back_first/pallas_call | solution.py:558
  401.7 11.1 %shard_map.581 = (bf16[528,1536]{1,0:T(8,128)(2,1)}, f32[16,1536]{1,0:T(8,128)}, f32[8,1536]{1,0:T(8,128)}) custom-call(f32[520,3456]{1,0:T(8,128)} %fusion.130.step_ref.xv_ref.xk_ref.x_ref, f32[8,3328]{1,0:T(8,128)} %maximum_maximum_fusion.4.tv_ref.tk_ref.tap_ref, f32[3,512,128]{2,1,0:T(8,128)} %broadcast_in_dim.257.match_ref, ...), custom_call_target="tpu_custom_call" | custom-call | flops 100000000 | bytes 10000000 | tf_op jit(solution)/shard_map/pallas_call | solution.py:709
  428.8 24.4 %collective-permute-done.25 = f16[208,3072]{1,0:T(8,128)(2,1)} collective-permute-done((f16[208,3072]{1,0:T(8,128)(2,1)}, f16[208,3072]{1,0:T(8,128)(2,1)}, u32[]{:S(2)}, u32[]{:S(2)}) %collective-permute-start.25) | collective-permute-done | bytes 1277984 | tf_op jit(solution)/shard_map/ppermute | solution.py:768
  470.7 48.7 %back_second.1 = (f32[512,1536]{1,0:T(8,128)}, f32[512,256]{1,0:T(8,128)}, f32[512,128]{1,0:T(8,128)}, f32[3,512,8]{2,1,0:T(8,128)}, f32[3,512,8]{2,1,0:T(8,128)}, /*index=5*/f32[24,512]{1,0:T(8,128)}, f32[8,1536]{1,0:T(8,128)}) custom-call(f32[512,3072]{1,0:T(8,128)} %get-tuple-element.122.v_ref, f32[512,3072]{1,0:T(8,128)} %get-tuple-element.163.dy_ref, ...), custom_call_target="tpu_custom_call" | custom-call | flops 15000000512 | bytes 15000000 | tf_op jit(solution)/shard_map/back_second/pallas_call | solution.py:558
  519.5 8.5 %step_back.1 = (bf16[528,128]{1,0:T(8,128)(2,1)}, f32[8,48]{1,0:T(8,128)}) custom-call(f32[520,3456]{1,0:T(8,128)} %fusion.130.step_ref.xv_ref.xk_ref.x_ref, f32[8,48]{1,0:T(8,128)} %maximum_maximum_fusion.5.par_ref, f32[3,512,8]{2,1,0:T(8,128)} %get-tuple-element.174.ddelta_a, f32[3,512,8]{2,1,0:T(8,128)} %get-tuple-element.175.ddelta_b, ...), custom_call_target="tpu_custom_call" | custom-call | flops 10000000 | bytes 10000000 | tf_op jit(solution)/shard_map/step_back/pallas_call | solution.py:647
  532.6 12.6 %shard_map.582 = (bf16[528,1792]{1,0:T(8,128)(2,1)}, f32[16,1792]{1,0:T(8,128)}, f32[8,1792]{1,0:T(8,128)}) custom-call(f32[520,3456]{1,0:T(8,128)} %fusion.130.step_ref.xv_ref.xk_ref.x_ref, f32[8,3328]{1,0:T(8,128)} %maximum_maximum_fusion.4.tv_ref.tk_ref.tap_ref, f32[3,512,128]{2,1,0:T(8,128)} %broadcast_in_dim.257.match_ref, ...), custom_call_target="tpu_custom_call" | custom-call | flops 100000000 | bytes 10000000 | tf_op jit(solution)/shard_map/pallas_call | solution.py:709
  608.2 18.9 %collective-permute-done.40 = f16[64,3072]{1,0:T(8,128)(2,1)S(1)} collective-permute-done((f16[64,3072]{1,0:T(8,128)(2,1)S(1)}, f16[64,3072]{1,0:T(8,128)(2,1)S(1)}, u32[]{:S(2)}, u32[]{:S(2)}) %collective-permute-start.40) | collective-permute-done | bytes 393248 | tf_op jit(solution)/shard_map/ppermute | solution.py:768
  627.1 7.4 %collective-permute-start.43 = (f16[64,1536]{1,0:T(8,128)(2,1)S(1)}, f16[64,1536]{1,0:T(8,128)(2,1)S(1)}, u32[]{:S(2)}, u32[]{:S(2)}) collective-permute-start(f16[64,1536]{1,0:T(8,128)(2,1)S(1)} %copy-done.54), channel_id=1, source_target_pairs={{0,2},{1,3},{2,0},{3,1},{4,6},{5,7},{6,4},{7,5},{8,10},{9,11},{10,... | collective-permute-start | bytes 589832 | tf_op jit(solution)/shard_map/ppermute | solution.py:768
  638.5 9.4 %collective-permute-done.43 = f16[64,1536]{1,0:T(8,128)(2,1)S(1)} collective-permute-done((f16[64,1536]{1,0:T(8,128)(2,1)S(1)}, f16[64,1536]{1,0:T(8,128)(2,1)S(1)}, u32[]{:S(2)}, u32[]{:S(2)}) %collective-permute-start.43) | collective-permute-done | bytes 196640 | tf_op jit(solution)/shard_map/ppermute | solution.py:768
  675.9 7.4 %collective-permute-done.38 = f32[168,128]{1,0:T(8,128)S(1)} collective-permute-done((f32[168,128]{1,0:T(8,128)S(1)}, f32[168,128]{1,0:T(8,128)S(1)}, u32[]{:S(2)}, u32[]{:S(2)}) %collective-permute-start.38) | collective-permute-done | bytes 86048 | tf_op jit(solution)/shard_map/ppermute | solution.py:896
  (477 shorter events, 310.3 us)
Async XLA Ops:
  7.2 106.4 %all-gather.4.cloned.1.call-start = ((), (), s32[]{:S(2)}) async-start(), calls=%async_computation | async-start | bytes 11943936 | tf_op jit(solution)/shard_map/all_gather | solution.py:754
  46.6 130.6 %all-gather.6.cloned.1.call-start = ((), (), s32[]{:S(2)}) async-start(), calls=%async_computation.1 | async-start | bytes 10616832 | tf_op jit(solution)/shard_map/all_gather | solution.py:754
  74.3 28.3 %collective-permute-start.7 = (bf16[48,3072]{1,0:T(8,128)(2,1)S(1)}, bf16[48,3072]{1,0:T(8,128)(2,1)S(1)}, u32[]{:S(2)}, u32[]{:S(2)}) collective-permute-start(bf16[48,3072]{1,0:T(8,128)(2,1)S(1)} %slice.463), channel_id=1, source_target_pairs={{0,2},{1,3},{2,0},{3,1},{4,6},{5,7},{6,4},{7,5},{8,10},{9,11},{10,... | collective-permute-start | bytes 884744 | tf_op jit(solution)/shard_map/ppermute | solution.py:768
  104.8 131.2 %all-gather.8.cloned.1.call-start = ((), (), s32[]{:S(2)}) async-start(), calls=%async_computation.2 | async-start | bytes 10616832 | tf_op jit(solution)/shard_map/all_gather | solution.py:754
  106.3 39.5 %collective-permute-start.11 = (bf16[96,1536]{1,0:T(8,128)(2,1)S(1)}, bf16[96,1536]{1,0:T(8,128)(2,1)}, u32[]{:S(2)}, u32[]{:S(2)}) collective-permute-start(bf16[96,1536]{1,0:T(8,128)(2,1)S(1)} %convert_element_type.281), channel_id=1, source_target_pairs={{0,3},{1,2},{2,1},{3,0},{4,7},{5,6},{6,5},{7,4},{8,11},{9,10},{10,... | collective-permute-start | bytes 884744 | tf_op jit(solution)/shard_map/ppermute | solution.py:768
  107.4 38.3 %collective-permute-start.10 = (bf16[96,1536]{1,0:T(8,128)(2,1)S(1)}, bf16[96,1536]{1,0:T(8,128)(2,1)}, u32[]{:S(2)}, u32[]{:S(2)}) collective-permute-start(bf16[96,1536]{1,0:T(8,128)(2,1)S(1)} %convert_element_type.281), channel_id=1, source_target_pairs={{0,2},{1,3},{2,0},{3,1},{4,6},{5,7},{6,4},{7,5},{8,10},{9,11},{10,... | collective-permute-start | bytes 884744 | tf_op jit(solution)/shard_map/ppermute | solution.py:768
  107.4 38.4 %collective-permute-start.9 = (bf16[96,1536]{1,0:T(8,128)(2,1)S(1)}, bf16[96,1536]{1,0:T(8,128)(2,1)}, u32[]{:S(2)}, u32[]{:S(2)}) collective-permute-start(bf16[96,1536]{1,0:T(8,128)(2,1)S(1)} %convert_element_type.281), channel_id=1, source_target_pairs={{0,1},{1,0},{2,3},{3,2},{4,5},{5,4},{6,7},{7,6},{8,9},{9,8},{10,11... | collective-permute-start | bytes 884744 | tf_op jit(solution)/shard_map/ppermute | solution.py:768
  151.0 28.8 %collective-permute-start.12 = (bf16[128,3072]{1,0:T(8,128)(2,1)}, bf16[128,3072]{1,0:T(8,128)(2,1)}, u32[]{:S(2)}, u32[]{:S(2)}) collective-permute-start(bf16[128,3072]{1,0:T(8,128)(2,1)} %get-tuple-element.143), channel_id=1, source_target_pairs={{0,1},{1,2},{2,3},{4,5},{5,6},{6,7},{8,9},{9,10},{10,11},{12,13},{... | collective-permute-start | bytes 2359304 | tf_op jit(solution)/shard_map/ppermute | solution.py:747
  202.4 43.4 %collective-permute-start.14 = (bf16[128,3072]{1,0:T(8,128)(2,1)}, bf16[128,3072]{1,0:T(8,128)(2,1)}, u32[]{:S(2)}, u32[]{:S(2)}) collective-permute-start(bf16[128,3072]{1,0:T(8,128)(2,1)} %add_convert_fusion.2), channel_id=1, source_target_pairs={{0,1},{1,2},{2,3},{4,5},{5,6},{6,7},{8,9},{9,10},{10,11},{12,13},{... | collective-permute-start | bytes 2359304 | tf_op jit(solution)/shard_map/ppermute | solution.py:747
  281.9 45.7 %collective-permute-start.19 = (bf16[528,3072]{1,0:T(8,128)(2,1)S(1)}, bf16[528,3072]{1,0:T(8,128)(2,1)S(1)}, u32[]{:S(2)}, u32[]{:S(2)}) collective-permute-start(bf16[528,3072]{1,0:T(8,128)(2,1)S(1)} %copy-done.31), channel_id=1, source_target_pairs={{0,4},{4,0},{8,12},{12,8},{16,20},{20,16},{24,28},{28,24},{1,5},{5... | collective-permute-start | bytes 9732104 | tf_op jit(solution)/shard_map/ppermute | solution.py:768
  282.3 31.9 %collective-permute-start.18 = (bf16[2,512,768]{2,1,0:T(8,128)(2,1)S(1)}, bf16[2,512,768]{2,1,0:T(8,128)(2,1)S(1)}, u32[]{:S(2)}, u32[]{:S(2)}) collective-permute-start(bf16[2,512,768]{2,1,0:T(8,128)(2,1)S(1)} %slice.366), channel_id=1, source_target_pairs={{0,4},{4,0},{8,12},{12,8},{16,20},{20,16},{24,28},{28,24},{1,5},{5... | collective-permute-start | bytes 4718600 | tf_op jit(solution)/shard_map/ppermute | solution.py:768
  320.1 68.6 %collective-permute-start.20 = (f16[768,1536]{1,0:T(8,128)(2,1)}, f16[768,1536]{1,0:T(8,128)(2,1)}, u32[]{:S(2)}, u32[]{:S(2)}) collective-permute-start(f16[768,1536]{1,0:T(8,128)(2,1)} %multiply_convert_fusion), channel_id=1, source_target_pairs={{0,8},{4,12},{8,0},{12,4},{16,24},{20,28},{24,16},{28,20},{1,9},{5... | collective-permute-start | bytes 7077896 | tf_op jit(solution)/shard_map/ppermute | solution.py:768
  333.2 60.9 %collective-permute-start.21 = (f16[400,3072]{1,0:T(8,128)(2,1)}, f16[400,3072]{1,0:T(8,128)(2,1)}, u32[]{:S(2)}, u32[]{:S(2)}) collective-permute-start(f16[400,3072]{1,0:T(8,128)(2,1)} %select_convert_fusion), channel_id=1, source_target_pairs={{0,16},{4,20},{8,24},{12,28},{16,0},{20,4},{24,8},{28,12},{1,17},{... | collective-permute-start | bytes 7372808 | tf_op jit(solution)/shard_map/ppermute | solution.py:768
  422.5 30.8 %collective-permute-start.25 = (f16[208,3072]{1,0:T(8,128)(2,1)}, f16[208,3072]{1,0:T(8,128)(2,1)}, u32[]{:S(2)}, u32[]{:S(2)}) collective-permute-start(f16[208,3072]{1,0:T(8,128)(2,1)} %fusion.6), channel_id=1, source_target_pairs={{0,8},{4,12},{8,0},{12,4},{16,24},{20,28},{24,16},{28,20},{1,9},{5... | collective-permute-start | bytes 3833864 | tf_op jit(solution)/shard_map/ppermute | solution.py:768
  423.8 34.9 %collective-permute-start.24 = (f16[384,1536]{1,0:T(8,128)(2,1)}, f16[384,1536]{1,0:T(8,128)(2,1)S(1)}, u32[]{:S(2)}, u32[]{:S(2)}) collective-permute-start(f16[384,1536]{1,0:T(8,128)(2,1)} %fusion.7), channel_id=1, source_target_pairs={{0,16},{4,20},{8,24},{12,28},{16,0},{20,4},{24,8},{28,12},{1,17},{... | collective-permute-start | bytes 3538952 | tf_op jit(solution)/shard_map/ppermute | solution.py:768
  462.8 65.2 %collective-permute-start.26 = (f16[400,768]{1,0:T(8,128)(2,1)}, f16[400,768]{1,0:T(8,128)(2,1)S(1)}, u32[]{:S(2)}, u32[]{:S(2)}) collective-permute-start(f16[400,768]{1,0:T(8,128)(2,1)} %fusion.23), channel_id=1, source_target_pairs={{0,8},{4,12},{8,0},{12,4},{16,24},{20,28},{24,16},{28,20},{1,9},{5... | collective-permute-start | bytes 1843208 | tf_op jit(solution)/shard_map/ppermute | solution.py:768
  465.6 62.4 %collective-permute-start.27 = (f16[400,768]{1,0:T(8,128)(2,1)}, f16[400,768]{1,0:T(8,128)(2,1)}, u32[]{:S(2)}, u32[]{:S(2)}) collective-permute-start(f16[400,768]{1,0:T(8,128)(2,1)} %fusion.22), channel_id=1, source_target_pairs={{0,16},{4,20},{8,24},{12,28},{16,0},{20,4},{24,8},{28,12},{1,17},{... | collective-permute-start | bytes 1843208 | tf_op jit(solution)/shard_map/ppermute | solution.py:768
  466.5 168.0 %collective-permute-start.50 = (f16[96,1536]{1,0:T(8,128)(2,1)}, f16[96,1536]{1,0:T(8,128)(2,1)}, u32[]{:S(2)}, u32[]{:S(2)}) collective-permute-start(f16[96,1536]{1,0:T(8,128)(2,1)} %get-tuple-element.279), channel_id=1, source_target_pairs={{0,1},{1,0},{2,3},{3,2},{4,5},{5,4},{6,7},{7,6},{8,9},{9,8},{10,11... | collective-permute-start | bytes 884744 | tf_op jit(solution)/shard_map/ppermute | solution.py:768
  468.5 168.0 %collective-permute-start.51 = (f16[96,1536]{1,0:T(8,128)(2,1)}, f16[96,1536]{1,0:T(8,128)(2,1)}, u32[]{:S(2)}, u32[]{:S(2)}) collective-permute-start(f16[96,1536]{1,0:T(8,128)(2,1)} %get-tuple-element.278), channel_id=1, source_target_pairs={{0,2},{1,3},{2,0},{3,1},{4,6},{5,7},{6,4},{7,5},{8,10},{9,11},{10,... | collective-permute-start | bytes 884744 | tf_op jit(solution)/shard_map/ppermute | solution.py:768
  559.3 78.0 %collective-permute-start.52 = (f16[96,1536]{1,0:T(8,128)(2,1)}, f16[96,1536]{1,0:T(8,128)(2,1)}, u32[]{:S(2)}, u32[]{:S(2)}) collective-permute-start(f16[96,1536]{1,0:T(8,128)(2,1)} %get-tuple-element.277), channel_id=1, source_target_pairs={{0,3},{1,2},{2,1},{3,0},{4,7},{5,6},{6,5},{7,4},{8,11},{9,10},{10,... | collective-permute-start | bytes 884744 | tf_op jit(solution)/shard_map/ppermute | solution.py:768
  571.1 26.3 %collective-permute-start.33 = (f16[400,1024]{1,0:T(8,128)(2,1)}, f16[400,1024]{1,0:T(8,128)(2,1)}, u32[]{:S(2)}, u32[]{:S(2)}) collective-permute-start(f16[400,1024]{1,0:T(8,128)(2,1)} %select_convert_fusion.1), channel_id=1, source_target_pairs={{0,16},{4,20},{8,24},{12,28},{16,0},{20,4},{24,8},{28,12},{1,17},{... | collective-permute-start | bytes 2457608 | tf_op jit(solution)/shard_map/ppermute | solution.py:768
  597.4 29.6 %collective-permute-start.40 = (f16[64,3072]{1,0:T(8,128)(2,1)S(1)}, f16[64,3072]{1,0:T(8,128)(2,1)S(1)}, u32[]{:S(2)}, u32[]{:S(2)}) collective-permute-start(f16[64,3072]{1,0:T(8,128)(2,1)S(1)} %copy-done.50), channel_id=1, source_target_pairs={{0,2},{1,3},{2,0},{3,1},{4,6},{5,7},{6,4},{7,5},{8,10},{9,11},{10,... | collective-permute-start | bytes 1179656 | tf_op jit(solution)/shard_map/ppermute | solution.py:768
  636.5 28.7 %collective-permute-start.45 = (f16[208,896]{1,0:T(8,128)(2,1)S(1)}, f16[208,896]{1,0:T(8,128)(2,1)S(1)}, u32[]{:S(2)}, u32[]{:S(2)}) collective-permute-start(f16[208,896]{1,0:T(8,128)(2,1)S(1)} %fusion.29), channel_id=1, source_target_pairs={{0,16},{4,20},{8,24},{12,28},{16,0},{20,4},{24,8},{28,12},{1,17},{... | collective-permute-start | bytes 1118216 | tf_op jit(solution)/shard_map/ppermute | solution.py:768
  637.3 33.0 %collective-permute-start.46 = (f16[208,1024]{1,0:T(8,128)(2,1)S(1)}, f16[208,1024]{1,0:T(8,128)(2,1)S(1)}, u32[]{:S(2)}, u32[]{:S(2)}) collective-permute-start(f16[208,1024]{1,0:T(8,128)(2,1)S(1)} %fusion.27), channel_id=1, source_target_pairs={{0,8},{4,12},{8,0},{12,4},{16,24},{20,28},{24,16},{28,20},{1,9},{5... | collective-permute-start | bytes 1277960 | tf_op jit(solution)/shard_map/ppermute | solution.py:768
  (114 other events, 1594.6 us)
Sparse Core Ops, SparseCore 0:
  46.7 66.8 all-gather.3
  116.1 58.6 all-gather.5
  177.3 58.6 all-gather.7

commit v5 on v4

--- a/solution.py
+++ b/solution.py
@@ -54,6 +54,10 @@
     return dot1(ah, bh, dims) + (dot1(ah, bl, dims) + dot1(al, bh, dims))
 
 
+def dot_halves(a, b, dims=NN):
+    return dot1(a[0], b[0], dims) + (dot1(a[0], b[1], dims) + dot1(a[1], b[0], dims))
+
+
 def dotf(a, b, dims=NN):
     return lax.dot_general(a, b, dims, precision=highest, preferred_element_type=f32)
 
@@ -63,7 +67,7 @@
 
 
 def sigmoid(x):
-    return 1.0 / (1.0 + jnp.exp(-x))
+    return 0.5 * jnp.tanh(0.5 * x) + 0.5
 
 
 def softplus(x):
@@ -91,7 +95,7 @@
 
 
 def prep_kernel(
-    step_ref, par_ref, mask_ref, delta_ref, cum_ref, cumt_ref, infc_ref, tailc_ref, tailn_ref,
+    step_ref, par_ref, mask_ref, delta_ref, cum_ref, cumt_ref, tailc_ref,
     taild_ref, infd_ref, keep_ref, factor_ref,
 ):
     length = mask_ref.shape[0]
@@ -108,18 +112,13 @@
         cum = dotf(tri, -delta * rate)
         cumt_ref[:, rows] = dotf(eye, cum, NT)
         last = cum[Q - 1 : Q, :]
-        alive, ending = mask_ref[rows, 0:1], mask_ref[rows, 1:2]
-        infc = jnp.exp(cum) * alive
-        tailn = jnp.exp(last - cum) * ending
-        tailc = tailn * delta
+        tailc = jnp.exp(last - cum) * mask_ref[rows, 1:2] * delta
         for g in range(NG):
             part = slice(g * GH, (g + 1) * GH)
             delta_ref[g, rows, :] = delta[:, part]
             cum_ref[g, rows, :] = cum[:, part]
-            infc_ref[g, rows, :] = infc[:, part]
-            tailn_ref[g, rows, :] = tailn[:, part]
             tailc_ref[g, rows, :] = tailc[:, part]
-        keeps.append(infc[Q - 1 : Q, :])
+        keeps.append(jnp.exp(last) * mask_ref[(c + 1) * Q - 1 : (c + 1) * Q, 0:1])
         whole = cum + base
         infd_ref[rows, :] = jnp.exp(whole) * mask_ref[rows, 2:3]
         held.append((whole, delta))
@@ -153,7 +152,7 @@
     cols = jax.ShapeDtypeStruct((NG, length, GH), f32)
     wide = jax.ShapeDtypeStruct((8, DI), f32)
     shapes = (
-        cols, cols, jax.ShapeDtypeStruct((HEADS, length), f32), cols, cols, cols, cols,
+        cols, cols, jax.ShapeDtypeStruct((HEADS, length), f32), cols, cols,
         jax.ShapeDtypeStruct((length, HEADS), f32), wide, wide,
     )
     return pl.pallas_call(
@@ -257,8 +256,8 @@
 
 
 def local_kernel(
-    v_ref, kq_ref, delta_ref, cum_ref, cumt_ref, infc_ref, tailc_ref, keep_ref, segc_ref, segr_ref,
-    y_ref, gram, bias, kt,
+    v_ref, kq_ref, delta_ref, cum_ref, cumt_ref, mask_ref, keep_ref, segc_ref, segr_ref,
+    y_ref, gram, bias, kt_hi, kt_lo,
 ):
     length = v_ref.shape[0]
     count = length // Q
@@ -270,37 +269,47 @@
             k, q = kq_ref[rows, :STATE], kq_ref[rows, STATE:]
             bias[rows, :] = masks_of(segc_ref, segr_ref, rows)[0]
             gram[rows, :] = dot3(q, k, NT)
-            kt[:, rows] = k.T
+            kt_hi[:, rows], kt_lo[:, rows] = halves(k.T)
 
     low = iota((Q, 128), 1) < HEAD_DIM
     state = None
     for c in range(count):
         rows = slice(c * Q, (c + 1) * Q)
-        delta, cum, tail, inflow = (r[0, rows, :] for r in (delta_ref, cum_ref, tailc_ref, infc_ref))
-        g, b = gram[rows, :], bias[rows, :]
+        delta, cum = delta_ref[0, rows, :], cum_ref[0, rows, :]
+        alive = jnp.broadcast_to(mask_ref[rows, 0:1], (Q, 128))
+        ending = jnp.broadcast_to(mask_ref[rows, 1:2], (Q, 128))
         if c:
             carried = dot3(kq_ref[rows, STATE:], state)
         tails = []
         for j in range(GW // 128):
             cols = slice(128 * j, 128 * (j + 1))
-            v = v_ref[rows, cols]
-            w = v * pair_lanes(delta, j)
+            w = v_ref[rows, cols] * pair_lanes(delta, j)
+            run = pair_lanes(cum, j)
             both = []
             for i in (2 * j, 2 * j + 1):
-                both.append((g * jnp.exp(cum[:, i : i + 1] - cumt_ref[i : i + 1, rows] + b)))
-            stacked = jnp.concatenate([jnp.where(low, w, 0.0), jnp.where(low, 0.0, w)], axis=0)
-            y = dot3(jnp.concatenate(both, axis=1), stacked)
+                fade = jnp.exp(cum[:, i : i + 1] - cumt_ref[i : i + 1, rows] + bias[rows, :])
+                both.append(halves(gram[rows, :] * fade))
+            parts = halves(w)
+            zero = jnp.zeros_like(parts[0])
+            stacked = tuple(
+                jnp.concatenate([jnp.where(low, part, zero), jnp.where(low, zero, part)], axis=0)
+                for part in parts
+            )
+            y = dot_halves(tuple(jnp.concatenate([both[0][i], both[1][i]], axis=1) for i in (0, 1)), stacked)
             if c:
-                y = y + carried[:, cols] * pair_lanes(inflow, j)
+                y = y + carried[:, cols] * (jnp.exp(run) * alive)
             y_ref[rows, cols] = y
             if c < count - 1:
-                tails.append(v * pair_lanes(tail, j))
+                tails.append(halves(w * (jnp.exp(run[Q - 1 : Q, :] - run) * ending)))
         if c < count - 1:
-            fresh = dot3(kt[:, rows], jnp.concatenate(tails, axis=1))
+            fresh = dot_halves(
+                (kt_hi[:, rows], kt_lo[:, rows]),
+                tuple(jnp.concatenate([part[i] for part in tails], axis=1) for i in (0, 1)),
+            )
             state = fresh if state is None else state * keep_ref[c : c + 1, :] + fresh
 
 
-def local_out(v, kq, delta, cum, cumt, infc, tailc, keep, segc, segr):
+def local_out(v, kq, delta, cum, cumt, mask, keep, segc, segr):
     length = v.shape[0]
     cols = pl.BlockSpec((1, length, GH), lambda g: (g, 0, 0))
     return pl.pallas_call(
@@ -311,7 +320,7 @@
             pl.BlockSpec((length, 2 * STATE), lambda g: (0, 0)),
             cols, cols,
             pl.BlockSpec((GH, length), lambda g: (g, 0)),
-            cols, cols,
+            pl.BlockSpec((length, 8), lambda g: (0, 0)),
             pl.BlockSpec((8, GW), lambda g: (0, g)),
             pl.BlockSpec((length, 8), lambda g: (0, 0)),
             pl.BlockSpec((8, length), lambda g: (0, 0)),
@@ -320,12 +329,12 @@
         out_shape=jax.ShapeDtypeStruct((length, DI), f32),
         scratch_shapes=[
             pltpu.VMEM((length, Q), f32), pltpu.VMEM((length, Q), f32),
-            pltpu.VMEM((STATE, length), f32),
+            pltpu.VMEM((STATE, length), bf16), pltpu.VMEM((STATE, length), bf16),
         ],
         compiler_params=params(),
         cost_estimate=pl.CostEstimate(flops=2 * 10**9, bytes_accessed=2 * 10**7, transcendentals=4 * 10**6),
         name="local_out",
-    )(v, kq, delta, cum, cumt, infc, tailc, keep, segc, segr)
+    )(v, kq, delta, cum, cumt, mask, keep, segc, segr)
 
 
 def gate_kernel(
@@ -430,10 +439,10 @@
 
 
 def back_kernel(
-    final, v_ref, dy_ref, kq_ref, delta_ref, cum_ref, cumt_ref, infc_ref, tailc_ref, tailn_ref,
-    keep_ref, inc_ref, dout_ref, dir_ref, segc_ref, segr_ref, dkq_in, dgram_in,
+    final, v_ref, dy_ref, kq_ref, delta_ref, cum_ref, cumt_ref, tailc_ref, mask_ref, keep_ref,
+    inc_ref, dout_ref, dir_ref, segc_ref, segr_ref, dkq_in, dgram_in,
     dv_ref, dkq_ref, dgram, ddelta_ref, dcum_ref, drow_ref, flow_ref,
-    gram, gramt, bias, biast, kt, qt, states,
+    gram, gramt, bias, biast, kt_hi, kt_lo, qt_hi, qt_lo, kq_hi, kq_lo, states,
 ):
     length = v_ref.shape[0]
     count = length // Q
@@ -450,8 +459,9 @@
             scores = dot3(q, k, NT)
             gram[rows, :] = scores
             gramt[rows, :] = scores.T
-            kt[:, rows] = k.T
-            qt[:, rows] = q.T
+            kt_hi[:, rows], kt_lo[:, rows] = halves(k.T)
+            qt_hi[:, rows], qt_lo[:, rows] = halves(q.T)
+            kq_hi[rows, :], kq_lo[rows, :] = halves(kq_ref[rows, :])
         dgram[...] = dgram_in[...]
         dkq_ref[...] = dkq_in[...]
 
@@ -462,8 +472,10 @@
     states[0] = inc_ref[...].astype(f32)
     for c in range(count):
         rows = slice(c * Q, (c + 1) * Q)
-        weighted = v_ref[rows, :] * group_lanes(tailc_ref[0, rows, :])
-        states[c + 1] = states[c] * keep_ref[c : c + 1, :] + dot3(kt[:, rows], weighted)
+        weighted = halves(v_ref[rows, :] * group_lanes(tailc_ref[0, rows, :]))
+        states[c + 1] = states[c] * keep_ref[c : c + 1, :] + dot_halves(
+            (kt_hi[:, rows], kt_lo[:, rows]), weighted
+        )
 
     back = dout_ref[...].astype(f32)
     flows = jnp.zeros((8, GW), f32)
@@ -471,14 +483,13 @@
         rows = slice(c * Q, (c + 1) * Q)
         flows = jnp.where(line == c, jnp.sum(back * states[c + 1], axis=0, keepdims=True), flows)
         delta, cum = delta_ref[0, rows, :], cum_ref[0, rows, :]
-        inflow, tailc, tailn = infc_ref[0, rows, :], tailc_ref[0, rows, :], tailn_ref[0, rows, :]
-        k, q = kq_ref[rows, :STATE], kq_ref[rows, STATE:]
-        before = states[c]
-        after = back
-        y_in = dot3(q, before)
-        w_in = dot3(k, after)
-        g, gt, b, bt = gram[rows, :], gramt[rows, :], bias[rows, :], biast[rows, :]
-        dg = dgram[rows, :]
+        before = halves(states[c])
+        after = halves(back)
+        k, q = (kq_hi[rows, :STATE], kq_lo[rows, :STATE]), (kq_hi[rows, STATE:], kq_lo[rows, STATE:])
+        y_in = dot_halves(q, before)
+        w_in = dot_halves(k, after)
+        alive = jnp.broadcast_to(mask_ref[rows, 0:1], (Q, 128))
+        ending = jnp.broadcast_to(mask_ref[rows, 1:2], (Q, 128))
         ddelta = jnp.zeros((Q, GH), f32)
         dcum = jnp.zeros((Q, GH), f32)
         dys, ws = [], []
@@ -487,45 +498,47 @@
             dy, v = dy_ref[rows, cols], v_ref[rows, cols]
             spread = pair_lanes(delta, j)
             w = v * spread
-            stacked = jnp.concatenate(
-                [jnp.where(low, dy, 0.0), jnp.where(low, 0.0, dy)], axis=0
+            dy_hi, dy_lo = halves(dy)
+            zero = jnp.zeros_like(dy_hi)
+            stacked = tuple(
+                jnp.concatenate([jnp.where(low, part, zero), jnp.where(low, zero, part)], axis=0)
+                for part in (dy_hi, dy_lo)
             )
-            inner = dot3(stacked, w, NT)
+            inner = dot_halves(stacked, halves(w), NT)
+            run = jnp.where(low, cum[:, 2 * j : 2 * j + 1], cum[:, 2 * j + 1 : 2 * j + 2])
+            dflow = dy * (jnp.exp(run) * alive)
+            tail = jnp.exp(run[Q - 1 : Q, :] - run) * ending
+            dw_in = w_in[:, cols] * tail
+            one = dflow * y_in[:, cols] - w * dw_in
             turned = []
             for i in (0, 1):
                 h = 2 * j + i
                 col, row = cum[:, h : h + 1], cumt_ref[h : h + 1, rows]
-                turned.append(gt * jnp.exp(row - col + bt))
-                weighed = inner[Q * i : Q * (i + 1), :] * jnp.exp(col - row + b)
-                dg = dg + weighed
-                full = weighed * g
-                dcum = dcum + jnp.where(lane == h, jnp.sum(full, axis=1, keepdims=True), 0.0)
+                turned.append(halves(gramt[rows, :] * jnp.exp(row - col + biast[rows, :])))
+                weighed = inner[Q * i : Q * (i + 1), :] * jnp.exp(col - row + bias[rows, :])
+                dgram[rows, :] += weighed
+                full = weighed * gram[rows, :]
                 drow_ref[h : h + 1, rows] = jnp.sum(full, axis=0, keepdims=True)
-            dw_in = w_in[:, cols] * pair_lanes(tailn, j)
-            dw = dot3(jnp.concatenate(turned, axis=1), stacked) + dw_in
+                keep = low if i == 0 else jnp.logical_not(low)
+                full = full + jnp.where(keep, one, 0.0)
+                dcum_ref[0, rows, h : h + 1] = jnp.sum(full, axis=1, keepdims=True)
+            dw = dot_halves(
+                tuple(jnp.concatenate([turned[0][i], turned[1][i]], axis=1) for i in (0, 1)), stacked
+            ) + dw_in
             dv_ref[rows, cols] = spread * dw + dir_ref[0:1, cols] * dy
-            dflow = dy * pair_lanes(inflow, j)
-            one = dflow * y_in[:, cols] - w * dw_in
             two = v * dw
             for i in (0, 1):
+                keep = low if i == 0 else jnp.logical_not(low)
                 h = 2 * j + i
-                keep = low if i == 0 else jnp.logical_not(low)
-                dcum = dcum + jnp.where(
-                    lane == h, jnp.sum(jnp.where(keep, one, 0.0), axis=1, keepdims=True), 0.0
-                )
-                ddelta = ddelta + jnp.where(
-                    lane == h, jnp.sum(jnp.where(keep, two, 0.0), axis=1, keepdims=True), 0.0
-                )
-            dys.append(dflow)
-            ws.append(v * pair_lanes(tailc, j))
-        dgram[rows, :] = dg
-        ddelta_ref[0, rows, :] = ddelta
-        dcum_ref[0, rows, :] = dcum
-        flowing = jnp.concatenate(dys, axis=1)
-        dkq_ref[rows, STATE:] += dot3(flowing, before, NT)
-        dkq_ref[rows, :STATE] += dot3(jnp.concatenate(ws, axis=1), after, NT)
+                ddelta_ref[0, rows, h : h + 1] = jnp.sum(jnp.where(keep, two, 0.0), axis=1, keepdims=True)
+            dys.append(halves(dflow))
+            ws.append(halves(w * tail))
+        flowing = tuple(jnp.concatenate([part[i] for part in dys], axis=1) for i in (0, 1))
+        leaving = tuple(jnp.concatenate([part[i] for part in ws], axis=1) for i in (0, 1))
+        dkq_ref[rows, STATE:] += dot_halves(flowing, before, NT)
+        dkq_ref[rows, :STATE] += dot_halves(leaving, after, NT)
         if c:
-            back = back * keep_ref[c : c + 1, :] + dot3(qt[:, rows], flowing)
+            back = back * keep_ref[c : c + 1, :] + dot_halves((qt_hi[:, rows], qt_lo[:, rows]), flowing)
     flow_ref[...] = flows
 
     @pl.when(jnp.logical_and(step == pl.num_programs(0) - 1, final))
@@ -539,7 +552,7 @@
 
 
 def back_local(
-    first, last, held, v, dy, kq, delta, cum, cumt, infc, tailc, tailn, keep, inc, dout, dirx, segc, segr
+    first, last, held, v, dy, kq, delta, cum, cumt, tailc, mask, keep, inc, dout, dirx, segc, segr
 ):
     length = v.shape[0]
     count = length // Q
@@ -559,7 +572,8 @@
         functools.partial(back_kernel, last == NG),
         grid=(groups,),
         in_specs=[
-            wide, wide, whole, cols, cols, turned, cols, cols, cols, lines, state, state, lines,
+            wide, wide, whole, cols, cols, turned, cols, pl.BlockSpec((length, 8), lambda g: (0, 0)), lines,
+            state, state, lines,
             pl.BlockSpec((length, 8), lambda g: (0, 0)),
             pl.BlockSpec((8, length), lambda g: (0, 0)),
             whole, table,
@@ -580,7 +594,8 @@
         ),
         scratch_shapes=[
             square, square, square, square,
-            pltpu.VMEM((STATE, length), f32), pltpu.VMEM((STATE, length), f32),
+            *[pltpu.VMEM((STATE, length), bf16) for _ in range(4)],
+            *[pltpu.VMEM((length, 2 * STATE), bf16) for _ in range(2)],
             pltpu.VMEM((count + 1, STATE, GW), f32),
         ],
         compiler_params=params(),
@@ -588,7 +603,7 @@
             flops=groups * 5 * 10**9, bytes_accessed=groups * 5 * 10**6, transcendentals=groups * 10**6
         ),
         name="back_first" if first == 0 else "back_second",
-    )(v, dy, kq, delta, cum, cumt, infc, tailc, tailn, keep, inc, dout, dirx, segc, segr, *held)
+    )(v, dy, kq, delta, cum, cumt, tailc, mask, keep, inc, dout, dirx, segc, segr, *held)
 
 
 def step_kernel(
@@ -1009,13 +1024,13 @@
     rest_w = after(rest_w, early)
 
     rest = jnp.dot(normed, rest_w, preferred_element_type=f32)
-    delta, cum, cumt, infc, tailc, tailn, taild, infd, keep, factor = prep(rest, pars, mask)
+    delta, cum, cumt, tailc, taild, infd, keep, factor = prep(rest, pars, mask)
     v, kq, state, state_half = conv_state(rest, taps, match, taild)
     out_rows = shard_gathered(after(param_outputs.astype(bf16), gate_rows), v)
     out_w = gathered(out_rows)
     state = after(state, out_rows)
     incoming = carried(state, state_half, factor[0:1], 1)
-    y = local_out(v, kq, delta, cum, cumt, infc, tailc, keep, segc, segr)
+    y = local_out(v, kq, delta, cum, cumt, mask, keep, segc, segr)
     gate_w = after(gate_w, y)
     z = jnp.dot(own_normed, gate_w, preferred_element_type=f32)
     out_w = after(out_w, z)
@@ -1051,7 +1066,7 @@
         outgoing, out_sum.payload, gate_sum.payload, out_sum.total, gate_sum.total, back_normed, block_out
     )
 
-    ssm = (kq, delta, cum, cumt, infc, tailc, tailn, keep, incoming)
+    ssm = (kq, delta, cum, cumt, tailc, mask, keep, incoming)
     half = NG // 2
     dv1, *held1 = back_local(0, half, None, v, dy, *ssm, outgoing, dirx, segc, segr)
     for one in first_sums:

time: 718 us -> 683 us (0.951)
  Pallas kernels: 192 us -> 134 us
  waiting for transfers between devices: 166 us -> 186 us
    pallas_call x2, Pallas kernels: 97.6 us -> 43.5 us  [back_local(): pl.pallas_call(functools.partial(back_kernel, last == NG), grid=(groups,)...]
    ppermute x39, waiting for transfers between devices: 86.8 us -> 106 us  [exchanged(): lax.ppermute(value, axis, [(i, i ^ by) for i in range(lax.axis_size(axis))])]
  transfers between devices with their start and end apart: 56 -> 56, of which waited for: 20 -> 23; matrix products, arithmetic and copies ran while one was open for 31% -> 32% of each run, Pallas kernels for 22% -> 15%
where the time goes in v5:
time: 683 us; the launch traced here: 673 us
  waiting for transfers between devices  186 us (27%)
  Pallas kernels  134 us (20%)
  matrix products  98 us (14%)
  other arithmetic  95.7 us (14%)
  starting transfers between devices  86.2 us (13%)
  local copies, waits for them, and re-layouts  55.3 us (8%)
  between operations  18.4 us (3%)
    ppermute x39, waiting for transfers between devices, exchanged(): lax.ppermute(value, axis, [(i, i ^ by) for i in range(lax.axis_size(axis))])  106 us
    ppermute x39, starting transfers between devices, exchanged(): lax.ppermute(value, axis, [(i, i ^ by) for i in range(lax.axis_size(axis))])  49.9 us
    pallas_call x2, Pallas kernels, back_local(): pl.pallas_call(functools.partial(back_kernel, last == NG), grid=(groups,)...  43.5 us
    ppermute x9, waiting for transfers between devices, shifted(): return lax.ppermute(value, axis, pairs)  31.9 us
    all_gather x3, waiting for transfers between devices, gathered(): return lax.all_gather(value, 'dp', axis=0, tiled=True)  31.8 us
    ppermute x9, starting transfers between devices, shifted(): return lax.ppermute(value, axis, pairs)  27.3 us
    pallas_call x2, Pallas kernels, unconv(): pl.pallas_call(functools.partial(unconv_kernel, mixed), grid=(tiles,), in...  23.3 us
    pallas_call x1, Pallas kernels, gate(): pl.pallas_call(functools.partial(gate_kernel, block), grid_spec=pltpu.Pre...  22.8 us
  transfers between devices with their start and end apart: 56, of which 23 were waited for; matrix products, arithmetic and copies ran while one was open for 32% of the time, Pallas kernels for 15%

profile of v5, /device:TPU:0, one launch (start us, length us, event | category | flops | bytes accessed | tf_op | source)
XLA Modules:
  0.0 673.3 jit_solution(893210962440672877)
XLA Ops:
  21.7 9.6 %collective-permute-done.1 = bf16[48,3456]{1,0:T(8,128)(2,1)S(1)} collective-permute-done((bf16[48,3456]{1,0:T(8,128)(2,1)S(1)}, bf16[48,3456]{1,0:T(8,128)(2,1)S(1)}, u32[]{:S(2)}, u32[]{:S(2)}) %collective-permute-start.1) | collective-permute-done | bytes 331808 | tf_op jit(solution)/shard_map/ppermute | solution.py:783
  32.1 11.0 %collective-permute-done.2 = bf16[48,3456]{1,0:T(8,128)(2,1)} collective-permute-done((bf16[48,3456]{1,0:T(8,128)(2,1)S(1)}, bf16[48,3456]{1,0:T(8,128)(2,1)}, u32[]{:S(2)}, u32[]{:S(2)}) %collective-permute-start.2) | collective-permute-done | bytes 331808 | tf_op jit(solution)/shard_map/ppermute | solution.py:783
  113.7 12.3 %fusion.130.step_ref.xv_ref.xk_ref.x_ref = f32[520,3456]{1,0:T(8,128)} fusion(bf16[520,1536]{1,0:T(8,128)(2,1)} %copy-done.12, bf16[1536,3456]{1,0:T(8,128)(2,1)} %all-gather.4.cloned.1.call-done), kind=kOutput, calls=%fused_computation.354 | convolution fusion | flops 5520752640 | bytes 19402752 | tf_op jit(solution)/shard_map/dot_general | solution.py:1026
  131.4 12.4 %conv_state.1 = (f32[512,3072]{1,0:T(8,128)}, f32[512,256]{1,0:T(8,128)}, f32[128,3072]{1,0:T(8,128)}, bf16[128,3072]{1,0:T(8,128)(2,1)}) custom-call(f32[520,3456]{1,0:T(8,128)} %fusion.130.step_ref.xv_ref.xk_ref.x_ref, f32[520,3456]{1,0:T(8,128)} %fusion.130.step_ref.xv_ref.xk_ref.x_ref, f32[8,3328]{1,0:T(8,128)} %maximum_maximum_fusion.4.tv_ref.tk_ref.tap_ref, ...), custom_call_target="tpu_custom_call" | custom-call | flops 2000000000 | bytes 20000000 | tf_op jit(solution)/shard_map/conv_state/pallas_call | solution.py:221
  156.1 17.5 %local_out.1.y_ref = f32[512,3072]{1,0:T(8,128)} custom-call(f32[512,3072]{1,0:T(8,128)} %get-tuple-element.120.v_ref, f32[512,256]{1,0:T(8,128)} %get-tuple-element.121.kq_ref, f32[6,512,8]{2,1,0:T(8,128)} %get-tuple-element.122.delta_ref, f32[6,512,8]{2,1,0:T(8,128)} %get-tuple-element.123.cum_ref, f32[48,512]{1,0:T(8,128)} %get-tuple-element.124.cumt_ref, ...), custom_call_target="tpu_custom_call" | custom-call | flops 2000000000 | bytes 20000000 | tf_op jit(solution)/shard_map/local_out/pallas_call | solution.py:315
  183.4 11.9 %fusion.107.z_ref = f32[512,3072]{1,0:T(8,128)} fusion(bf16[1536,3072]{1,0:T(8,128)(2,1)} %all-gather.6.cloned.1.call-done, bf16[520,1536]{1,0:T(8,128)(2,1)S(1)} %copy-done.13), kind=kOutput, calls=%fused_computation.345 | convolution fusion | flops 4831838208 | bytes 17301504 | tf_op jit(solution)/shard_map/dot_general | solution.py:1035
  206.6 29.5 %all-gather.8.cloned.1.call-done = bf16[3072,1536]{1,0:T(8,128)(2,1)} async-done(((bf16[384,1536]{1,0:T(8,128)(2,1)}), bf16[3072,1536]{1,0:T(8,128)(2,1)}) %all-gather.8.cloned.1.call-update) | async-done | bytes 9437200 | tf_op jit(solution)/shard_map/all_gather | solution.py:769
  236.0 9.8 %convolution_bitcast_fusion.g_ref = f32[512,3072]{1,0:T(8,128)} fusion(bf16[3072,1536]{1,0:T(8,128)(2,1)} %all-gather.8.cloned.1.call-done, bf16[512,1536]{1,0:T(8,128)(2,1)} %get-tuple-element.117), kind=kOutput, calls=%fused_computation.5 | convolution fusion | flops 4831838208 | bytes 17301504 | tf_op jit(solution)/shard_map/dot_general | solution.py:1037
  245.8 22.8 %gate.1 = (bf16[512,3072]{1,0:T(8,128)(2,1)}, bf16[4,512,768]{2,1,0:T(8,128)(2,1)}, f32[512,3072]{1,0:T(8,128)}, bf16[528,3072]{1,0:T(8,128)(2,1)}, f32[128,3072...) custom-call(s32[2]{0:T(128)} %pad_add_fusion.at_ref, f32[512,3072]{1,0:T(8,128)} %local_out.1.y_ref, ...), custom_call_target="tpu_custom_call" | custom-call | flops 1000000000 | bytes 40000000 | tf_op jit(solution)/shard_map/gate/pallas_call | solution.py:408
  271.5 10.1 %fusion.131 = f32[528,1536]{1,0:T(8,128)} fusion(bf16[528,3072]{1,0:T(8,128)(2,1)} %broadcast_dynamic-update-slice_fusion, bf16[1536,3072]{1,0:T(8,128)(2,1)} %all-gather.6.cloned.1.call-done), kind=kOutput, calls=%fused_computation.355 | convolution fusion | flops 4982833152 | bytes 15925248 | tf_op jit(solution)/shard_map/dot_general | solution.py:1064
  282.4 9.0 %collective-permute-done.15 = bf16[128,3072]{1,0:T(8,128)(2,1)S(1)} collective-permute-done((bf16[128,3072]{1,0:T(8,128)(2,1)}, bf16[128,3072]{1,0:T(8,128)(2,1)S(1)}, u32[]{:S(2)}, u32[]{:S(2)}) %collective-permute-start.15) | collective-permute-done | bytes 786464 | tf_op jit(solution)/shard_map/ppermute | solution.py:762
  301.1 11.3 %collective-permute-done.16 = bf16[128,3072]{1,0:T(8,128)(2,1)S(1)} collective-permute-done((bf16[128,3072]{1,0:T(8,128)(2,1)S(1)}, bf16[128,3072]{1,0:T(8,128)(2,1)S(1)}, u32[]{:S(2)}, u32[]{:S(2)}) %collective-permute-start.16) | collective-permute-done | bytes 786464 | tf_op jit(solution)/shard_map/ppermute | solution.py:762
  339.7 21.6 %back_first.1 = (f32[512,1536]{1,0:T(8,128)}, f32[512,256]{1,0:T(8,128)}, f32[512,128]{1,0:T(8,128)}, f32[3,512,8]{2,1,0:T(8,128)}, f32[3,512,8]{2,1,0:T(8,128)}, /*index=5*/f32[24,512]{1,0:T(8,128)}, f32[8,1536]{1,0:T(8,128)}) custom-call(f32[512,3072]{1,0:T(8,128)} %get-tuple-element.120.v_ref, f32[512,3072]{1,0:T(8,128)} %get-tuple-element.159.dy_ref, ...), custom_call_target="tpu_custom_call" | custom-call | flops 15000000512 | bytes 15000000 | tf_op jit(solution)/shard_map/back_first/pallas_call | solution.py:571
  361.3 10.7 %collective-permute-done.20 = f16[768,1536]{1,0:T(8,128)(2,1)} collective-permute-done((f16[768,1536]{1,0:T(8,128)(2,1)}, f16[768,1536]{1,0:T(8,128)(2,1)}, u32[]{:S(2)}, u32[]{:S(2)}) %collective-permute-start.20) | collective-permute-done | bytes 2359328 | tf_op jit(solution)/shard_map/ppermute | solution.py:783
  377.4 9.5 %collective-permute-done.21 = f16[400,3072]{1,0:T(8,128)(2,1)} collective-permute-done((f16[400,3072]{1,0:T(8,128)(2,1)}, f16[400,3072]{1,0:T(8,128)(2,1)}, u32[]{:S(2)}, u32[]{:S(2)}) %collective-permute-start.21) | collective-permute-done | bytes 2457632 | tf_op jit(solution)/shard_map/ppermute | solution.py:783
  394.4 10.9 %shard_map.581 = (bf16[528,1536]{1,0:T(8,128)(2,1)}, f32[16,1536]{1,0:T(8,128)}, f32[8,1536]{1,0:T(8,128)}) custom-call(f32[520,3456]{1,0:T(8,128)} %fusion.130.step_ref.xv_ref.xk_ref.x_ref, f32[8,3328]{1,0:T(8,128)} %maximum_maximum_fusion.4.tv_ref.tk_ref.tap_ref, f32[3,512,128]{2,1,0:T(8,128)} %broadcast_in_dim.257.match_ref, ...), custom_call_target="tpu_custom_call" | custom-call | flops 100000000 | bytes 10000000 | tf_op jit(solution)/shard_map/pallas_call | solution.py:724
  420.7 24.8 %collective-permute-done.25 = f16[208,3072]{1,0:T(8,128)(2,1)} collective-permute-done((f16[208,3072]{1,0:T(8,128)(2,1)}, f16[208,3072]{1,0:T(8,128)(2,1)}, u32[]{:S(2)}, u32[]{:S(2)}) %collective-permute-start.25) | collective-permute-done | bytes 1277984 | tf_op jit(solution)/shard_map/ppermute | solution.py:783
  462.6 22.0 %back_second.1 = (f32[512,1536]{1,0:T(8,128)}, f32[512,256]{1,0:T(8,128)}, f32[512,128]{1,0:T(8,128)}, f32[3,512,8]{2,1,0:T(8,128)}, f32[3,512,8]{2,1,0:T(8,128)}, /*index=5*/f32[24,512]{1,0:T(8,128)}, f32[8,1536]{1,0:T(8,128)}) custom-call(f32[512,3072]{1,0:T(8,128)} %get-tuple-element.120.v_ref, f32[512,3072]{1,0:T(8,128)} %get-tuple-element.159.dy_ref, ...), custom_call_target="tpu_custom_call" | custom-call | flops 15000000512 | bytes 15000000 | tf_op jit(solution)/shard_map/back_second/pallas_call | solution.py:571
  484.6 8.5 %step_back.1 = (bf16[528,128]{1,0:T(8,128)(2,1)}, f32[8,48]{1,0:T(8,128)}) custom-call(f32[520,3456]{1,0:T(8,128)} %fusion.130.step_ref.xv_ref.xk_ref.x_ref, f32[8,48]{1,0:T(8,128)} %maximum_maximum_fusion.5.par_ref, f32[3,512,8]{2,1,0:T(8,128)} %get-tuple-element.170.ddelta_a, f32[3,512,8]{2,1,0:T(8,128)} %get-tuple-element.171.ddelta_b, ...), custom_call_target="tpu_custom_call" | custom-call | flops 10000000 | bytes 10000000 | tf_op jit(solution)/shard_map/step_back/pallas_call | solution.py:662
  497.7 12.4 %shard_map.582 = (bf16[528,1792]{1,0:T(8,128)(2,1)}, f32[16,1792]{1,0:T(8,128)}, f32[8,1792]{1,0:T(8,128)}) custom-call(f32[520,3456]{1,0:T(8,128)} %fusion.130.step_ref.xv_ref.xk_ref.x_ref, f32[8,3328]{1,0:T(8,128)} %maximum_maximum_fusion.4.tv_ref.tk_ref.tap_ref, f32[3,512,128]{2,1,0:T(8,128)} %broadcast_in_dim.257.match_ref, ...), custom_call_target="tpu_custom_call" | custom-call | flops 100000000 | bytes 10000000 | tf_op jit(solution)/shard_map/pallas_call | solution.py:724
  572.8 19.0 %collective-permute-done.40 = f16[64,3072]{1,0:T(8,128)(2,1)S(1)} collective-permute-done((f16[64,3072]{1,0:T(8,128)(2,1)S(1)}, f16[64,3072]{1,0:T(8,128)(2,1)S(1)}, u32[]{:S(2)}, u32[]{:S(2)}) %collective-permute-start.40) | collective-permute-done | bytes 393248 | tf_op jit(solution)/shard_map/ppermute | solution.py:783
  591.8 7.8 %collective-permute-start.43 = (f16[64,1536]{1,0:T(8,128)(2,1)S(1)}, f16[64,1536]{1,0:T(8,128)(2,1)S(1)}, u32[]{:S(2)}, u32[]{:S(2)}) collective-permute-start(f16[64,1536]{1,0:T(8,128)(2,1)S(1)} %copy-done.54), channel_id=1, source_target_pairs={{0,2},{1,3},{2,0},{3,1},{4,6},{5,7},{6,4},{7,5},{8,10},{9,11},{10,... | collective-permute-start | bytes 589832 | tf_op jit(solution)/shard_map/ppermute | solution.py:783
  603.2 9.3 %collective-permute-done.43 = f16[64,1536]{1,0:T(8,128)(2,1)S(1)} collective-permute-done((f16[64,1536]{1,0:T(8,128)(2,1)S(1)}, f16[64,1536]{1,0:T(8,128)(2,1)S(1)}, u32[]{:S(2)}, u32[]{:S(2)}) %collective-permute-start.43) | collective-permute-done | bytes 196640 | tf_op jit(solution)/shard_map/ppermute | solution.py:783
  640.7 7.8 %collective-permute-done.38 = f32[168,128]{1,0:T(8,128)S(1)} collective-permute-done((f32[168,128]{1,0:T(8,128)S(1)}, f32[168,128]{1,0:T(8,128)S(1)}, u32[]{:S(2)}, u32[]{:S(2)}) %collective-permute-start.38) | collective-permute-done | bytes 86048 | tf_op jit(solution)/shard_map/ppermute | solution.py:911
  (477 shorter events, 323.2 us)
Async XLA Ops:
  7.2 106.4 %all-gather.4.cloned.1.call-start = ((), (), s32[]{:S(2)}) async-start(), calls=%async_computation | async-start | bytes 11943936 | tf_op jit(solution)/shard_map/all_gather | solution.py:769
  17.2 25.9 %collective-permute-start.2 = (bf16[48,3456]{1,0:T(8,128)(2,1)S(1)}, bf16[48,3456]{1,0:T(8,128)(2,1)}, u32[]{:S(2)}, u32[]{:S(2)}) collective-permute-start(bf16[48,3456]{1,0:T(8,128)(2,1)S(1)} %concatenate.125), channel_id=1, source_target_pairs={{0,2},{1,3},{2,0},{3,1},{4,6},{5,7},{6,4},{7,5},{8,10},{9,11},{10,... | collective-permute-start | bytes 995336 | tf_op jit(solution)/shard_map/ppermute | solution.py:783
  46.6 128.2 %all-gather.6.cloned.1.call-start = ((), (), s32[]{:S(2)}) async-start(), calls=%async_computation.1 | async-start | bytes 10616832 | tf_op jit(solution)/shard_map/all_gather | solution.py:769
  74.2 28.3 %collective-permute-start.7 = (bf16[48,3072]{1,0:T(8,128)(2,1)S(1)}, bf16[48,3072]{1,0:T(8,128)(2,1)S(1)}, u32[]{:S(2)}, u32[]{:S(2)}) collective-permute-start(bf16[48,3072]{1,0:T(8,128)(2,1)S(1)} %slice.463), channel_id=1, source_target_pairs={{0,2},{1,3},{2,0},{3,1},{4,6},{5,7},{6,4},{7,5},{8,10},{9,11},{10,... | collective-permute-start | bytes 884744 | tf_op jit(solution)/shard_map/ppermute | solution.py:783
  104.8 131.3 %all-gather.8.cloned.1.call-start = ((), (), s32[]{:S(2)}) async-start(), calls=%async_computation.2 | async-start | bytes 10616832 | tf_op jit(solution)/shard_map/all_gather | solution.py:769
  106.3 37.6 %collective-permute-start.11 = (bf16[96,1536]{1,0:T(8,128)(2,1)S(1)}, bf16[96,1536]{1,0:T(8,128)(2,1)}, u32[]{:S(2)}, u32[]{:S(2)}) collective-permute-start(bf16[96,1536]{1,0:T(8,128)(2,1)S(1)} %convert_element_type.281), channel_id=1, source_target_pairs={{0,3},{1,2},{2,1},{3,0},{4,7},{5,6},{6,5},{7,4},{8,11},{9,10},{10,... | collective-permute-start | bytes 884744 | tf_op jit(solution)/shard_map/ppermute | solution.py:783
  107.4 36.4 %collective-permute-start.10 = (bf16[96,1536]{1,0:T(8,128)(2,1)S(1)}, bf16[96,1536]{1,0:T(8,128)(2,1)}, u32[]{:S(2)}, u32[]{:S(2)}) collective-permute-start(bf16[96,1536]{1,0:T(8,128)(2,1)S(1)} %convert_element_type.281), channel_id=1, source_target_pairs={{0,2},{1,3},{2,0},{3,1},{4,6},{5,7},{6,4},{7,5},{8,10},{9,11},{10,... | collective-permute-start | bytes 884744 | tf_op jit(solution)/shard_map/ppermute | solution.py:783
  107.4 36.4 %collective-permute-start.9 = (bf16[96,1536]{1,0:T(8,128)(2,1)S(1)}, bf16[96,1536]{1,0:T(8,128)(2,1)}, u32[]{:S(2)}, u32[]{:S(2)}) collective-permute-start(bf16[96,1536]{1,0:T(8,128)(2,1)S(1)} %convert_element_type.281), channel_id=1, source_target_pairs={{0,1},{1,0},{2,3},{3,2},{4,5},{5,4},{6,7},{7,6},{8,9},{9,8},{10,11... | collective-permute-start | bytes 884744 | tf_op jit(solution)/shard_map/ppermute | solution.py:783
  149.0 28.5 %collective-permute-start.12 = (bf16[128,3072]{1,0:T(8,128)(2,1)}, bf16[128,3072]{1,0:T(8,128)(2,1)}, u32[]{:S(2)}, u32[]{:S(2)}) collective-permute-start(bf16[128,3072]{1,0:T(8,128)(2,1)} %get-tuple-element.139), channel_id=1, source_target_pairs={{0,1},{1,2},{2,3},{4,5},{5,6},{6,7},{8,9},{9,10},{10,11},{12,13},{... | collective-permute-start | bytes 2359304 | tf_op jit(solution)/shard_map/ppermute | solution.py:762
  201.3 44.5 %collective-permute-start.14 = (bf16[128,3072]{1,0:T(8,128)(2,1)}, bf16[128,3072]{1,0:T(8,128)(2,1)}, u32[]{:S(2)}, u32[]{:S(2)}) collective-permute-start(bf16[128,3072]{1,0:T(8,128)(2,1)} %add_convert_fusion.2), channel_id=1, source_target_pairs={{0,1},{1,2},{2,3},{4,5},{5,6},{6,7},{8,9},{9,10},{10,11},{12,13},{... | collective-permute-start | bytes 2359304 | tf_op jit(solution)/shard_map/ppermute | solution.py:762
  281.7 45.9 %collective-permute-start.19 = (bf16[528,3072]{1,0:T(8,128)(2,1)S(1)}, bf16[528,3072]{1,0:T(8,128)(2,1)S(1)}, u32[]{:S(2)}, u32[]{:S(2)}) collective-permute-start(bf16[528,3072]{1,0:T(8,128)(2,1)S(1)} %copy-done.31), channel_id=1, source_target_pairs={{0,4},{4,0},{8,12},{12,8},{16,20},{20,16},{24,28},{28,24},{1,5},{5... | collective-permute-start | bytes 9732104 | tf_op jit(solution)/shard_map/ppermute | solution.py:783
  282.0 32.1 %collective-permute-start.18 = (bf16[2,512,768]{2,1,0:T(8,128)(2,1)S(1)}, bf16[2,512,768]{2,1,0:T(8,128)(2,1)S(1)}, u32[]{:S(2)}, u32[]{:S(2)}) collective-permute-start(bf16[2,512,768]{2,1,0:T(8,128)(2,1)S(1)} %slice.366), channel_id=1, source_target_pairs={{0,4},{4,0},{8,12},{12,8},{16,20},{20,16},{24,28},{28,24},{1,5},{5... | collective-permute-start | bytes 4718600 | tf_op jit(solution)/shard_map/ppermute | solution.py:783
  320.0 52.0 %collective-permute-start.20 = (f16[768,1536]{1,0:T(8,128)(2,1)}, f16[768,1536]{1,0:T(8,128)(2,1)}, u32[]{:S(2)}, u32[]{:S(2)}) collective-permute-start(f16[768,1536]{1,0:T(8,128)(2,1)} %multiply_convert_fusion), channel_id=1, source_target_pairs={{0,8},{4,12},{8,0},{12,4},{16,24},{20,28},{24,16},{28,20},{1,9},{5... | collective-permute-start | bytes 7077896 | tf_op jit(solution)/shard_map/ppermute | solution.py:783
  333.2 53.8 %collective-permute-start.21 = (f16[400,3072]{1,0:T(8,128)(2,1)}, f16[400,3072]{1,0:T(8,128)(2,1)}, u32[]{:S(2)}, u32[]{:S(2)}) collective-permute-start(f16[400,3072]{1,0:T(8,128)(2,1)} %select_convert_fusion), channel_id=1, source_target_pairs={{0,16},{4,20},{8,24},{12,28},{16,0},{20,4},{24,8},{28,12},{1,17},{... | collective-permute-start | bytes 7372808 | tf_op jit(solution)/shard_map/ppermute | solution.py:783
  414.8 30.8 %collective-permute-start.25 = (f16[208,3072]{1,0:T(8,128)(2,1)}, f16[208,3072]{1,0:T(8,128)(2,1)}, u32[]{:S(2)}, u32[]{:S(2)}) collective-permute-start(f16[208,3072]{1,0:T(8,128)(2,1)} %fusion.6), channel_id=1, source_target_pairs={{0,8},{4,12},{8,0},{12,4},{16,24},{20,28},{24,16},{28,20},{1,9},{5... | collective-permute-start | bytes 3833864 | tf_op jit(solution)/shard_map/ppermute | solution.py:783
  415.6 35.4 %collective-permute-start.24 = (f16[384,1536]{1,0:T(8,128)(2,1)}, f16[384,1536]{1,0:T(8,128)(2,1)S(1)}, u32[]{:S(2)}, u32[]{:S(2)}) collective-permute-start(f16[384,1536]{1,0:T(8,128)(2,1)} %fusion.7), channel_id=1, source_target_pairs={{0,16},{4,20},{8,24},{12,28},{16,0},{20,4},{24,8},{28,12},{1,17},{... | collective-permute-start | bytes 3538952 | tf_op jit(solution)/shard_map/ppermute | solution.py:783
  455.1 38.0 %collective-permute-start.26 = (f16[400,768]{1,0:T(8,128)(2,1)}, f16[400,768]{1,0:T(8,128)(2,1)S(1)}, u32[]{:S(2)}, u32[]{:S(2)}) collective-permute-start(f16[400,768]{1,0:T(8,128)(2,1)} %fusion.23), channel_id=1, source_target_pairs={{0,8},{4,12},{8,0},{12,4},{16,24},{20,28},{24,16},{28,20},{1,9},{5... | collective-permute-start | bytes 1843208 | tf_op jit(solution)/shard_map/ppermute | solution.py:783
  457.3 35.7 %collective-permute-start.27 = (f16[400,768]{1,0:T(8,128)(2,1)}, f16[400,768]{1,0:T(8,128)(2,1)}, u32[]{:S(2)}, u32[]{:S(2)}) collective-permute-start(f16[400,768]{1,0:T(8,128)(2,1)} %fusion.22), channel_id=1, source_target_pairs={{0,16},{4,20},{8,24},{12,28},{16,0},{20,4},{24,8},{28,12},{1,17},{... | collective-permute-start | bytes 1843208 | tf_op jit(solution)/shard_map/ppermute | solution.py:783
  458.4 141.2 %collective-permute-start.50 = (f16[96,1536]{1,0:T(8,128)(2,1)}, f16[96,1536]{1,0:T(8,128)(2,1)}, u32[]{:S(2)}, u32[]{:S(2)}) collective-permute-start(f16[96,1536]{1,0:T(8,128)(2,1)} %get-tuple-element.275), channel_id=1, source_target_pairs={{0,1},{1,0},{2,3},{3,2},{4,5},{5,4},{6,7},{7,6},{8,9},{9,8},{10,11... | collective-permute-start | bytes 884744 | tf_op jit(solution)/shard_map/ppermute | solution.py:783
  460.4 140.7 %collective-permute-start.51 = (f16[96,1536]{1,0:T(8,128)(2,1)}, f16[96,1536]{1,0:T(8,128)(2,1)}, u32[]{:S(2)}, u32[]{:S(2)}) collective-permute-start(f16[96,1536]{1,0:T(8,128)(2,1)} %get-tuple-element.274), channel_id=1, source_target_pairs={{0,2},{1,3},{2,0},{3,1},{4,6},{5,7},{6,4},{7,5},{8,10},{9,11},{10,... | collective-permute-start | bytes 884744 | tf_op jit(solution)/shard_map/ppermute | solution.py:783
  524.3 78.3 %collective-permute-start.52 = (f16[96,1536]{1,0:T(8,128)(2,1)}, f16[96,1536]{1,0:T(8,128)(2,1)}, u32[]{:S(2)}, u32[]{:S(2)}) collective-permute-start(f16[96,1536]{1,0:T(8,128)(2,1)} %get-tuple-element.273), channel_id=1, source_target_pairs={{0,3},{1,2},{2,1},{3,0},{4,7},{5,6},{6,5},{7,4},{8,11},{9,10},{10,... | collective-permute-start | bytes 884744 | tf_op jit(solution)/shard_map/ppermute | solution.py:783
  562.0 29.7 %collective-permute-start.40 = (f16[64,3072]{1,0:T(8,128)(2,1)S(1)}, f16[64,3072]{1,0:T(8,128)(2,1)S(1)}, u32[]{:S(2)}, u32[]{:S(2)}) collective-permute-start(f16[64,3072]{1,0:T(8,128)(2,1)S(1)} %copy-done.50), channel_id=1, source_target_pairs={{0,2},{1,3},{2,0},{3,1},{4,6},{5,7},{6,4},{7,5},{8,10},{9,11},{10,... | collective-permute-start | bytes 1179656 | tf_op jit(solution)/shard_map/ppermute | solution.py:783
  601.2 29.0 %collective-permute-start.45 = (f16[208,896]{1,0:T(8,128)(2,1)S(1)}, f16[208,896]{1,0:T(8,128)(2,1)S(1)}, u32[]{:S(2)}, u32[]{:S(2)}) collective-permute-start(f16[208,896]{1,0:T(8,128)(2,1)S(1)} %fusion.29), channel_id=1, source_target_pairs={{0,16},{4,20},{8,24},{12,28},{16,0},{20,4},{24,8},{28,12},{1,17},{... | collective-permute-start | bytes 1118216 | tf_op jit(solution)/shard_map/ppermute | solution.py:783
  602.6 32.4 %collective-permute-start.46 = (f16[208,1024]{1,0:T(8,128)(2,1)S(1)}, f16[208,1024]{1,0:T(8,128)(2,1)S(1)}, u32[]{:S(2)}, u32[]{:S(2)}) collective-permute-start(f16[208,1024]{1,0:T(8,128)(2,1)S(1)} %fusion.27), channel_id=1, source_target_pairs={{0,8},{4,12},{8,0},{12,4},{16,24},{20,28},{24,16},{28,20},{1,9},{5... | collective-permute-start | bytes 1277960 | tf_op jit(solution)/shard_map/ppermute | solution.py:783
  (114 other events, 1599.1 us)
Sparse Core Ops, SparseCore 0:
  46.7 66.8 all-gather.3
  116.1 58.6 all-gather.5
  177.3 58.6 all-gather.7

commit v6 on v5

--- a/solution.py
+++ b/solution.py
@@ -900,17 +900,27 @@
         return result
 
 
-def summed(value):
-    for axis in ("dp", "shard"):
-        count = lax.axis_size(axis)
-        if count & (count - 1):
-            value = lax.psum(value, axis)
-            continue
-        by = 1
-        while by < count:
-            value = value + lax.ppermute(value, axis, [(i, i ^ by) for i in range(count)])
-            by *= 2
-    return value
+class Everywhere:
+    def __init__(self, value):
+        self.value = value
+        self.steps = []
+        for axis in ("dp", "shard"):
+            count, by = lax.axis_size(axis), 1
+            while by < count:
+                self.steps.append((axis, by))
+                by *= 2
+
+    def send(self):
+        self.got = exchanged(self.value, *self.steps.pop(0))
+
+    def take(self, *earlier):
+        self.value = self.value + after(self.got, earlier)
+
+    def finish(self):
+        while self.steps:
+            self.send()
+            self.take()
+        return self.value
 
 
 def carried(state, half, factor, by):
@@ -1112,22 +1122,6 @@
     back_normed = back_normed + lax.dot_general(drest1, rest_w[:, :wide1], NT, preferred_element_type=f32)
     back_normed = back_normed + lax.dot_general(drest2, rest_w[:, wide1:], NT, preferred_element_type=f32)
     back_normed = back_normed[:length]
-    for one in sums2:
-        one.take(back_normed)
-        if one.more():
-            one.prepare()
-            one.send()
-    sent = [one.payload for one in sums2]
-    grad_outputs = shard_out.take(sent)
-    grad_gate = shard_gate.take(sent)
-    for one in sums2:
-        one.take()
-        one.finish()
-    shard2 = ShardSum(sums2)
-    grad_rest = jnp.concatenate([shard1.take(sent), shard2.take()], axis=1)
-    grad_inputs = jnp.concatenate([grad_gate, grad_rest[:, : param_inputs.shape[1] - DI]], axis=1)
-    dtap = jnp.concatenate([dtap1, dtap2], axis=1)
-
     own_inv = inv[HALO:]
     scaled = hidden_in * own_inv
     gained = back_normed * param_prenorm
@@ -1136,6 +1130,7 @@
     )
     grad_prenorm = jnp.sum(back_normed * scaled, axis=0)
 
+    dtap = jnp.concatenate([dtap1, dtap2], axis=1)
     pieces = [
         grad_prenorm,
         dtap[:KW].reshape(-1),
@@ -1145,10 +1140,30 @@
         jnp.sum(small[1].reshape(HEADS, HEAD_DIM), axis=1),
         small[0],
     ]
-    flat = after(jnp.concatenate(pieces), sent)
+    flat = jnp.concatenate(pieces)
     count = flat.shape[0]
     lines = -(-count // 1024) * 8
-    total = summed(jnp.pad(flat, (0, lines * 128 - count)).reshape(lines, 128)).reshape(-1)
+    everywhere = Everywhere(jnp.pad(flat, (0, lines * 128 - count)).reshape(lines, 128))
+    everywhere.send()
+    for one in sums2:
+        one.take(back_normed)
+        if one.more():
+            one.prepare()
+            one.send()
+    sent = [one.payload for one in sums2]
+    everywhere.take(sent)
+    everywhere.send()
+    for one in sums2:
+        one.take(everywhere.value)
+        one.finish()
+    shard2 = ShardSum(sums2)
+    sent = shard2.payloads
+    everywhere.take(sent)
+    total = everywhere.finish().reshape(-1)
+    grad_outputs = shard_out.take(sent)
+    grad_gate = shard_gate.take(sent)
+    grad_rest = jnp.concatenate([shard1.take(sent), shard2.take()], axis=1)
+    grad_inputs = jnp.concatenate([grad_gate, grad_rest[:, : param_inputs.shape[1] - DI]], axis=1)
     found, at = [], 0
     for piece in pieces:
         found.append(total[at : at + piece.shape[0]])

time: 683 us -> 687 us (level)
  waiting for transfers between devices: 186 us -> 202 us
    ppermute x39 -> x44, waiting for transfers between devices: 106 us -> 138 us  [exchanged(): lax.ppermute(value, axis, [(i, i ^ by) for i in range(lax.axis_size(axis))])]
    ppermute x5 -> x0, waiting for transfers between devices: 16 us -> none  [summed(): lax.ppermute(value, axis, [(i, i ^ by) for i in range(count)])]
    ppermute x5 -> x0, starting transfers between devices: 8.68 us -> none  [summed(): lax.ppermute(value, axis, [(i, i ^ by) for i in range(count)])]
    ppermute x39 -> x44, starting transfers between devices: 49.9 us -> 56.1 us  [exchanged(): lax.ppermute(value, axis, [(i, i ^ by) for i in range(lax.axis_size(axis))])]
  transfers between devices with their start and end apart: 56 -> 56, of which waited for: 23 -> 20; matrix products, arithmetic and copies ran while one was open for 32% -> 31% of each run, Pallas kernels for 15% -> 15%
where the time goes in v6:
time: 687 us; the launch traced here: 678 us
  waiting for transfers between devices  202 us (29%)
  Pallas kernels  134 us (20%)
  matrix products  97.1 us (14%)
  other arithmetic  90 us (13%)
  starting transfers between devices  83.8 us (12%)
  local copies, waits for them, and re-layouts  53.2 us (8%)
  between operations  18.7 us (3%)
    ppermute x44, waiting for transfers between devices, exchanged(): lax.ppermute(value, axis, [(i, i ^ by) for i in range(lax.axis_size(axis))])  138 us
    ppermute x44, starting transfers between devices, exchanged(): lax.ppermute(value, axis, [(i, i ^ by) for i in range(lax.axis_size(axis))])  56.1 us
    pallas_call x2, Pallas kernels, back_local(): pl.pallas_call(functools.partial(back_kernel, last == NG), grid=(groups,)...  43.6 us
    ppermute x9, waiting for transfers between devices, shifted(): return lax.ppermute(value, axis, pairs)  31.8 us
    all_gather x3, waiting for transfers between devices, gathered(): return lax.all_gather(value, 'dp', axis=0, tiled=True)  31.7 us
    ppermute x9, starting transfers between devices, shifted(): return lax.ppermute(value, axis, pairs)  27.3 us
    pallas_call x2, Pallas kernels, unconv(): pl.pallas_call(functools.partial(unconv_kernel, mixed), grid=(tiles,), in...  23.3 us
    pallas_call x1, Pallas kernels, gate(): pl.pallas_call(functools.partial(gate_kernel, block), grid_spec=pltpu.Pre...  22.9 us
  transfers between devices with their start and end apart: 56, of which 20 were waited for; matrix products, arithmetic and copies ran while one was open for 31% of the time, Pallas kernels for 15%

profile of v6, /device:TPU:0, one launch (start us, length us, event | category | flops | bytes accessed | tf_op | source)
XLA Modules:
  0.0 678.3 jit_solution(12409813040778899345)
XLA Ops:
  21.7 9.6 %collective-permute-done.1 = bf16[48,3456]{1,0:T(8,128)(2,1)S(1)} collective-permute-done((bf16[48,3456]{1,0:T(8,128)(2,1)S(1)}, bf16[48,3456]{1,0:T(8,128)(2,1)S(1)}, u32[]{:S(2)}, u32[]{:S(2)}) %collective-permute-start.1) | collective-permute-done | bytes 331808 | tf_op jit(solution)/shard_map/ppermute | solution.py:783
  32.1 11.0 %collective-permute-done.2 = bf16[48,3456]{1,0:T(8,128)(2,1)} collective-permute-done((bf16[48,3456]{1,0:T(8,128)(2,1)S(1)}, bf16[48,3456]{1,0:T(8,128)(2,1)}, u32[]{:S(2)}, u32[]{:S(2)}) %collective-permute-start.2) | collective-permute-done | bytes 331808 | tf_op jit(solution)/shard_map/ppermute | solution.py:783
  113.7 12.4 %fusion.130.step_ref.xv_ref.xk_ref.x_ref = f32[520,3456]{1,0:T(8,128)} fusion(bf16[520,1536]{1,0:T(8,128)(2,1)} %copy-done.12, bf16[1536,3456]{1,0:T(8,128)(2,1)} %all-gather.4.cloned.1.call-done), kind=kOutput, calls=%fused_computation.352 | convolution fusion | flops 5520752640 | bytes 19402752 | tf_op jit(solution)/shard_map/dot_general | solution.py:1036
  131.4 12.4 %conv_state.1 = (f32[512,3072]{1,0:T(8,128)}, f32[512,256]{1,0:T(8,128)}, f32[128,3072]{1,0:T(8,128)}, bf16[128,3072]{1,0:T(8,128)(2,1)}) custom-call(f32[520,3456]{1,0:T(8,128)} %fusion.130.step_ref.xv_ref.xk_ref.x_ref, f32[520,3456]{1,0:T(8,128)} %fusion.130.step_ref.xv_ref.xk_ref.x_ref, f32[8,3328]{1,0:T(8,128)} %maximum_maximum_fusion.4.tv_ref.tk_ref.tap_ref, ...), custom_call_target="tpu_custom_call" | custom-call | flops 2000000000 | bytes 20000000 | tf_op jit(solution)/shard_map/conv_state/pallas_call | solution.py:221
  156.1 17.5 %local_out.1.y_ref = f32[512,3072]{1,0:T(8,128)} custom-call(f32[512,3072]{1,0:T(8,128)} %get-tuple-element.123.v_ref, f32[512,256]{1,0:T(8,128)} %get-tuple-element.124.kq_ref, f32[6,512,8]{2,1,0:T(8,128)} %get-tuple-element.125.delta_ref, f32[6,512,8]{2,1,0:T(8,128)} %get-tuple-element.126.cum_ref, f32[48,512]{1,0:T(8,128)} %get-tuple-element.127.cumt_ref, ...), custom_call_target="tpu_custom_call" | custom-call | flops 2000000000 | bytes 20000000 | tf_op jit(solution)/shard_map/local_out/pallas_call | solution.py:315
  183.5 11.9 %fusion.107.z_ref = f32[512,3072]{1,0:T(8,128)} fusion(bf16[1536,3072]{1,0:T(8,128)(2,1)} %all-gather.6.cloned.1.call-done, bf16[520,1536]{1,0:T(8,128)(2,1)S(1)} %copy-done.13), kind=kOutput, calls=%fused_computation.343 | convolution fusion | flops 4831838208 | bytes 17301504 | tf_op jit(solution)/shard_map/dot_general | solution.py:1045
  206.6 29.5 %all-gather.8.cloned.1.call-done = bf16[3072,1536]{1,0:T(8,128)(2,1)} async-done(((bf16[384,1536]{1,0:T(8,128)(2,1)}), bf16[3072,1536]{1,0:T(8,128)(2,1)}) %all-gather.8.cloned.1.call-update) | async-done | bytes 9437200 | tf_op jit(solution)/shard_map/all_gather | solution.py:769
  236.0 9.8 %convolution_bitcast_fusion.g_ref = f32[512,3072]{1,0:T(8,128)} fusion(bf16[3072,1536]{1,0:T(8,128)(2,1)} %all-gather.8.cloned.1.call-done, bf16[512,1536]{1,0:T(8,128)(2,1)} %get-tuple-element.120), kind=kOutput, calls=%fused_computation.5 | convolution fusion | flops 4831838208 | bytes 17301504 | tf_op jit(solution)/shard_map/dot_general | solution.py:1047
  245.8 22.9 %gate.1 = (bf16[512,3072]{1,0:T(8,128)(2,1)}, bf16[4,512,768]{2,1,0:T(8,128)(2,1)}, f32[512,3072]{1,0:T(8,128)}, bf16[528,3072]{1,0:T(8,128)(2,1)}, f32[128,3072...) custom-call(s32[2]{0:T(128)} %pad_add_fusion.at_ref, f32[512,3072]{1,0:T(8,128)} %local_out.1.y_ref, ...), custom_call_target="tpu_custom_call" | custom-call | flops 1000000000 | bytes 40000000 | tf_op jit(solution)/shard_map/gate/pallas_call | solution.py:408
  271.6 10.1 %fusion.131 = f32[528,1536]{1,0:T(8,128)} fusion(bf16[528,3072]{1,0:T(8,128)(2,1)} %broadcast_dynamic-update-slice_fusion, bf16[1536,3072]{1,0:T(8,128)(2,1)} %all-gather.6.cloned.1.call-done), kind=kOutput, calls=%fused_computation.353 | convolution fusion | flops 4982833152 | bytes 15925248 | tf_op jit(solution)/shard_map/dot_general | solution.py:1074
  282.4 9.0 %collective-permute-done.15 = bf16[128,3072]{1,0:T(8,128)(2,1)S(1)} collective-permute-done((bf16[128,3072]{1,0:T(8,128)(2,1)}, bf16[128,3072]{1,0:T(8,128)(2,1)S(1)}, u32[]{:S(2)}, u32[]{:S(2)}) %collective-permute-start.15) | collective-permute-done | bytes 786464 | tf_op jit(solution)/shard_map/ppermute | solution.py:762
  301.1 11.3 %collective-permute-done.16 = bf16[128,3072]{1,0:T(8,128)(2,1)S(1)} collective-permute-done((bf16[128,3072]{1,0:T(8,128)(2,1)S(1)}, bf16[128,3072]{1,0:T(8,128)(2,1)S(1)}, u32[]{:S(2)}, u32[]{:S(2)}) %collective-permute-start.16) | collective-permute-done | bytes 786464 | tf_op jit(solution)/shard_map/ppermute | solution.py:762
  339.8 21.6 %back_first.1 = (f32[512,1536]{1,0:T(8,128)}, f32[512,256]{1,0:T(8,128)}, f32[512,128]{1,0:T(8,128)}, f32[3,512,8]{2,1,0:T(8,128)}, f32[3,512,8]{2,1,0:T(8,128)}, /*index=5*/f32[24,512]{1,0:T(8,128)}, f32[8,1536]{1,0:T(8,128)}) custom-call(f32[512,3072]{1,0:T(8,128)} %get-tuple-element.123.v_ref, f32[512,3072]{1,0:T(8,128)} %get-tuple-element.162.dy_ref, ...), custom_call_target="tpu_custom_call" | custom-call | flops 15000000512 | bytes 15000000 | tf_op jit(solution)/shard_map/back_first/pallas_call | solution.py:571
  361.4 10.6 %collective-permute-done.20 = f16[768,1536]{1,0:T(8,128)(2,1)} collective-permute-done((f16[768,1536]{1,0:T(8,128)(2,1)}, f16[768,1536]{1,0:T(8,128)(2,1)}, u32[]{:S(2)}, u32[]{:S(2)}) %collective-permute-start.20) | collective-permute-done | bytes 2359328 | tf_op jit(solution)/shard_map/ppermute | solution.py:783
  377.4 9.6 %collective-permute-done.21 = f16[400,3072]{1,0:T(8,128)(2,1)} collective-permute-done((f16[400,3072]{1,0:T(8,128)(2,1)}, f16[400,3072]{1,0:T(8,128)(2,1)}, u32[]{:S(2)}, u32[]{:S(2)}) %collective-permute-start.21) | collective-permute-done | bytes 2457632 | tf_op jit(solution)/shard_map/ppermute | solution.py:783
  394.4 10.9 %shard_map.581 = (bf16[528,1536]{1,0:T(8,128)(2,1)}, f32[16,1536]{1,0:T(8,128)}, f32[8,1536]{1,0:T(8,128)}) custom-call(f32[520,3456]{1,0:T(8,128)} %fusion.130.step_ref.xv_ref.xk_ref.x_ref, f32[8,3328]{1,0:T(8,128)} %maximum_maximum_fusion.4.tv_ref.tk_ref.tap_ref, f32[3,512,128]{2,1,0:T(8,128)} %broadcast_in_dim.257.match_ref, ...), custom_call_target="tpu_custom_call" | custom-call | flops 100000000 | bytes 10000000 | tf_op jit(solution)/shard_map/pallas_call | solution.py:724
  420.7 24.8 %collective-permute-done.25 = f16[208,3072]{1,0:T(8,128)(2,1)} collective-permute-done((f16[208,3072]{1,0:T(8,128)(2,1)}, f16[208,3072]{1,0:T(8,128)(2,1)}, u32[]{:S(2)}, u32[]{:S(2)}) %collective-permute-start.25) | collective-permute-done | bytes 1277984 | tf_op jit(solution)/shard_map/ppermute | solution.py:783
  462.5 22.0 %back_second.1 = (f32[512,1536]{1,0:T(8,128)}, f32[512,256]{1,0:T(8,128)}, f32[512,128]{1,0:T(8,128)}, f32[3,512,8]{2,1,0:T(8,128)}, f32[3,512,8]{2,1,0:T(8,128)}, /*index=5*/f32[24,512]{1,0:T(8,128)}, f32[8,1536]{1,0:T(8,128)}) custom-call(f32[512,3072]{1,0:T(8,128)} %get-tuple-element.123.v_ref, f32[512,3072]{1,0:T(8,128)} %get-tuple-element.162.dy_ref, ...), custom_call_target="tpu_custom_call" | custom-call | flops 15000000512 | bytes 15000000 | tf_op jit(solution)/shard_map/back_second/pallas_call | solution.py:571
  484.5 8.5 %step_back.1 = (bf16[528,128]{1,0:T(8,128)(2,1)}, f32[8,48]{1,0:T(8,128)}) custom-call(f32[520,3456]{1,0:T(8,128)} %fusion.130.step_ref.xv_ref.xk_ref.x_ref, f32[8,48]{1,0:T(8,128)} %maximum_maximum_fusion.5.par_ref, f32[3,512,8]{2,1,0:T(8,128)} %get-tuple-element.173.ddelta_a, f32[3,512,8]{2,1,0:T(8,128)} %get-tuple-element.174.ddelta_b, ...), custom_call_target="tpu_custom_call" | custom-call | flops 10000000 | bytes 10000000 | tf_op jit(solution)/shard_map/step_back/pallas_call | solution.py:662
  497.6 12.4 %shard_map.582 = (bf16[528,1792]{1,0:T(8,128)(2,1)}, f32[16,1792]{1,0:T(8,128)}, f32[8,1792]{1,0:T(8,128)}) custom-call(f32[520,3456]{1,0:T(8,128)} %fusion.130.step_ref.xv_ref.xk_ref.x_ref, f32[8,3328]{1,0:T(8,128)} %maximum_maximum_fusion.4.tv_ref.tk_ref.tap_ref, f32[3,512,128]{2,1,0:T(8,128)} %broadcast_in_dim.257.match_ref, ...), custom_call_target="tpu_custom_call" | custom-call | flops 100000000 | bytes 10000000 | tf_op jit(solution)/shard_map/pallas_call | solution.py:724
  574.3 10.3 %collective-permute-done.37 = f16[208,1024]{1,0:T(8,128)(2,1)S(1)} collective-permute-done((f16[208,1024]{1,0:T(8,128)(2,1)S(1)}, f16[208,1024]{1,0:T(8,128)(2,1)S(1)}, u32[]{:S(2)}, u32[]{:S(2)}) %collective-permute-start.37) | collective-permute-done | bytes 426016 | tf_op jit(solution)/shard_map/ppermute | solution.py:783
  588.8 23.7 %collective-permute-done.42 = f16[64,3072]{1,0:T(8,128)(2,1)S(1)} collective-permute-done((f16[64,3072]{1,0:T(8,128)(2,1)S(1)}, f16[64,3072]{1,0:T(8,128)(2,1)S(1)}, u32[]{:S(2)}, u32[]{:S(2)}) %collective-permute-start.42) | collective-permute-done | bytes 393248 | tf_op jit(solution)/shard_map/ppermute | solution.py:783
  612.6 9.2 %collective-permute-start.45 = (f16[64,1536]{1,0:T(8,128)(2,1)S(1)}, f16[64,1536]{1,0:T(8,128)(2,1)S(1)}, u32[]{:S(2)}, u32[]{:S(2)}) collective-permute-start(f16[64,1536]{1,0:T(8,128)(2,1)S(1)} %copy-done.57), channel_id=1, source_target_pairs={{0,2},{1,3},{2,0},{3,1},{4,6},{5,7},{6,4},{7,5},{8,10},{9,11},{10,... | collective-permute-start | bytes 589832 | tf_op jit(solution)/shard_map/ppermute | solution.py:783
  626.2 20.2 %collective-permute-done.45 = f16[64,1536]{1,0:T(8,128)(2,1)S(1)} collective-permute-done((f16[64,1536]{1,0:T(8,128)(2,1)S(1)}, f16[64,1536]{1,0:T(8,128)(2,1)S(1)}, u32[]{:S(2)}, u32[]{:S(2)}) %collective-permute-start.45) | collective-permute-done | bytes 196640 | tf_op jit(solution)/shard_map/ppermute | solution.py:783
  (513 shorter events, 308.5 us)
Async XLA Ops:
  7.2 106.4 %all-gather.4.cloned.1.call-start = ((), (), s32[]{:S(2)}) async-start(), calls=%async_computation | async-start | bytes 11943936 | tf_op jit(solution)/shard_map/all_gather | solution.py:769
  46.6 128.2 %all-gather.6.cloned.1.call-start = ((), (), s32[]{:S(2)}) async-start(), calls=%async_computation.1 | async-start | bytes 10616832 | tf_op jit(solution)/shard_map/all_gather | solution.py:769
  74.3 28.3 %collective-permute-start.7 = (bf16[48,3072]{1,0:T(8,128)(2,1)S(1)}, bf16[48,3072]{1,0:T(8,128)(2,1)S(1)}, u32[]{:S(2)}, u32[]{:S(2)}) collective-permute-start(bf16[48,3072]{1,0:T(8,128)(2,1)S(1)} %slice.463), channel_id=1, source_target_pairs={{0,2},{1,3},{2,0},{3,1},{4,6},{5,7},{6,4},{7,5},{8,10},{9,11},{10,... | collective-permute-start | bytes 884744 | tf_op jit(solution)/shard_map/ppermute | solution.py:783
  104.8 131.2 %all-gather.8.cloned.1.call-start = ((), (), s32[]{:S(2)}) async-start(), calls=%async_computation.2 | async-start | bytes 10616832 | tf_op jit(solution)/shard_map/all_gather | solution.py:769
  106.3 37.6 %collective-permute-start.11 = (bf16[96,1536]{1,0:T(8,128)(2,1)S(1)}, bf16[96,1536]{1,0:T(8,128)(2,1)}, u32[]{:S(2)}, u32[]{:S(2)}) collective-permute-start(bf16[96,1536]{1,0:T(8,128)(2,1)S(1)} %convert_element_type.281), channel_id=1, source_target_pairs={{0,3},{1,2},{2,1},{3,0},{4,7},{5,6},{6,5},{7,4},{8,11},{9,10},{10,... | collective-permute-start | bytes 884744 | tf_op jit(solution)/shard_map/ppermute | solution.py:783
  107.4 36.4 %collective-permute-start.10 = (bf16[96,1536]{1,0:T(8,128)(2,1)S(1)}, bf16[96,1536]{1,0:T(8,128)(2,1)}, u32[]{:S(2)}, u32[]{:S(2)}) collective-permute-start(bf16[96,1536]{1,0:T(8,128)(2,1)S(1)} %convert_element_type.281), channel_id=1, source_target_pairs={{0,2},{1,3},{2,0},{3,1},{4,6},{5,7},{6,4},{7,5},{8,10},{9,11},{10,... | collective-permute-start | bytes 884744 | tf_op jit(solution)/shard_map/ppermute | solution.py:783
  107.4 36.4 %collective-permute-start.9 = (bf16[96,1536]{1,0:T(8,128)(2,1)S(1)}, bf16[96,1536]{1,0:T(8,128)(2,1)}, u32[]{:S(2)}, u32[]{:S(2)}) collective-permute-start(bf16[96,1536]{1,0:T(8,128)(2,1)S(1)} %convert_element_type.281), channel_id=1, source_target_pairs={{0,1},{1,0},{2,3},{3,2},{4,5},{5,4},{6,7},{7,6},{8,9},{9,8},{10,11... | collective-permute-start | bytes 884744 | tf_op jit(solution)/shard_map/ppermute | solution.py:783
  149.1 28.4 %collective-permute-start.12 = (bf16[128,3072]{1,0:T(8,128)(2,1)}, bf16[128,3072]{1,0:T(8,128)(2,1)}, u32[]{:S(2)}, u32[]{:S(2)}) collective-permute-start(bf16[128,3072]{1,0:T(8,128)(2,1)} %get-tuple-element.142), channel_id=1, source_target_pairs={{0,1},{1,2},{2,3},{4,5},{5,6},{6,7},{8,9},{9,10},{10,11},{12,13},{... | collective-permute-start | bytes 2359304 | tf_op jit(solution)/shard_map/ppermute | solution.py:762
  201.3 44.5 %collective-permute-start.14 = (bf16[128,3072]{1,0:T(8,128)(2,1)}, bf16[128,3072]{1,0:T(8,128)(2,1)}, u32[]{:S(2)}, u32[]{:S(2)}) collective-permute-start(bf16[128,3072]{1,0:T(8,128)(2,1)} %add_convert_fusion.2), channel_id=1, source_target_pairs={{0,1},{1,2},{2,3},{4,5},{5,6},{6,7},{8,9},{9,10},{10,11},{12,13},{... | collective-permute-start | bytes 2359304 | tf_op jit(solution)/shard_map/ppermute | solution.py:762
  281.7 45.9 %collective-permute-start.19 = (bf16[528,3072]{1,0:T(8,128)(2,1)S(1)}, bf16[528,3072]{1,0:T(8,128)(2,1)S(1)}, u32[]{:S(2)}, u32[]{:S(2)}) collective-permute-start(bf16[528,3072]{1,0:T(8,128)(2,1)S(1)} %copy-done.31), channel_id=1, source_target_pairs={{0,4},{4,0},{8,12},{12,8},{16,20},{20,16},{24,28},{28,24},{1,5},{5... | collective-permute-start | bytes 9732104 | tf_op jit(solution)/shard_map/ppermute | solution.py:783
  282.1 32.0 %collective-permute-start.18 = (bf16[2,512,768]{2,1,0:T(8,128)(2,1)S(1)}, bf16[2,512,768]{2,1,0:T(8,128)(2,1)S(1)}, u32[]{:S(2)}, u32[]{:S(2)}) collective-permute-start(bf16[2,512,768]{2,1,0:T(8,128)(2,1)S(1)} %slice.366), channel_id=1, source_target_pairs={{0,4},{4,0},{8,12},{12,8},{16,20},{20,16},{24,28},{28,24},{1,5},{5... | collective-permute-start | bytes 4718600 | tf_op jit(solution)/shard_map/ppermute | solution.py:783
  320.0 52.0 %collective-permute-start.20 = (f16[768,1536]{1,0:T(8,128)(2,1)}, f16[768,1536]{1,0:T(8,128)(2,1)}, u32[]{:S(2)}, u32[]{:S(2)}) collective-permute-start(f16[768,1536]{1,0:T(8,128)(2,1)} %multiply_convert_fusion), channel_id=1, source_target_pairs={{0,8},{4,12},{8,0},{12,4},{16,24},{20,28},{24,16},{28,20},{1,9},{5... | collective-permute-start | bytes 7077896 | tf_op jit(solution)/shard_map/ppermute | solution.py:783
  333.2 53.8 %collective-permute-start.21 = (f16[400,3072]{1,0:T(8,128)(2,1)}, f16[400,3072]{1,0:T(8,128)(2,1)}, u32[]{:S(2)}, u32[]{:S(2)}) collective-permute-start(f16[400,3072]{1,0:T(8,128)(2,1)} %select_convert_fusion), channel_id=1, source_target_pairs={{0,16},{4,20},{8,24},{12,28},{16,0},{20,4},{24,8},{28,12},{1,17},{... | collective-permute-start | bytes 7372808 | tf_op jit(solution)/shard_map/ppermute | solution.py:783
  414.7 30.8 %collective-permute-start.25 = (f16[208,3072]{1,0:T(8,128)(2,1)}, f16[208,3072]{1,0:T(8,128)(2,1)}, u32[]{:S(2)}, u32[]{:S(2)}) collective-permute-start(f16[208,3072]{1,0:T(8,128)(2,1)} %fusion.6), channel_id=1, source_target_pairs={{0,8},{4,12},{8,0},{12,4},{16,24},{20,28},{24,16},{28,20},{1,9},{5... | collective-permute-start | bytes 3833864 | tf_op jit(solution)/shard_map/ppermute | solution.py:783
  415.5 35.4 %collective-permute-start.24 = (f16[384,1536]{1,0:T(8,128)(2,1)}, f16[384,1536]{1,0:T(8,128)(2,1)S(1)}, u32[]{:S(2)}, u32[]{:S(2)}) collective-permute-start(f16[384,1536]{1,0:T(8,128)(2,1)} %fusion.7), channel_id=1, source_target_pairs={{0,16},{4,20},{8,24},{12,28},{16,0},{20,4},{24,8},{28,12},{1,17},{... | collective-permute-start | bytes 3538952 | tf_op jit(solution)/shard_map/ppermute | solution.py:783
  455.0 38.0 %collective-permute-start.26 = (f16[400,768]{1,0:T(8,128)(2,1)}, f16[400,768]{1,0:T(8,128)(2,1)S(1)}, u32[]{:S(2)}, u32[]{:S(2)}) collective-permute-start(f16[400,768]{1,0:T(8,128)(2,1)} %fusion.23), channel_id=1, source_target_pairs={{0,8},{4,12},{8,0},{12,4},{16,24},{20,28},{24,16},{28,20},{1,9},{5... | collective-permute-start | bytes 1843208 | tf_op jit(solution)/shard_map/ppermute | solution.py:783
  457.3 35.7 %collective-permute-start.27 = (f16[400,768]{1,0:T(8,128)(2,1)}, f16[400,768]{1,0:T(8,128)(2,1)}, u32[]{:S(2)}, u32[]{:S(2)}) collective-permute-start(f16[400,768]{1,0:T(8,128)(2,1)} %fusion.22), channel_id=1, source_target_pairs={{0,16},{4,20},{8,24},{12,28},{16,0},{20,4},{24,8},{28,12},{1,17},{... | collective-permute-start | bytes 1843208 | tf_op jit(solution)/shard_map/ppermute | solution.py:783
  458.3 163.4 %collective-permute-start.50 = (f16[96,1536]{1,0:T(8,128)(2,1)}, f16[96,1536]{1,0:T(8,128)(2,1)}, u32[]{:S(2)}, u32[]{:S(2)}) collective-permute-start(f16[96,1536]{1,0:T(8,128)(2,1)} %get-tuple-element.281), channel_id=1, source_target_pairs={{0,1},{1,0},{2,3},{3,2},{4,5},{5,4},{6,7},{7,6},{8,9},{9,8},{10,11... | collective-permute-start | bytes 884744 | tf_op jit(solution)/shard_map/ppermute | solution.py:783
  460.3 163.1 %collective-permute-start.51 = (f16[96,1536]{1,0:T(8,128)(2,1)}, f16[96,1536]{1,0:T(8,128)(2,1)}, u32[]{:S(2)}, u32[]{:S(2)}) collective-permute-start(f16[96,1536]{1,0:T(8,128)(2,1)} %get-tuple-element.280), channel_id=1, source_target_pairs={{0,2},{1,3},{2,0},{3,1},{4,6},{5,7},{6,4},{7,5},{8,10},{9,11},{10,... | collective-permute-start | bytes 884744 | tf_op jit(solution)/shard_map/ppermute | solution.py:783
  524.2 100.3 %collective-permute-start.52 = (f16[96,1536]{1,0:T(8,128)(2,1)}, f16[96,1536]{1,0:T(8,128)(2,1)}, u32[]{:S(2)}, u32[]{:S(2)}) collective-permute-start(f16[96,1536]{1,0:T(8,128)(2,1)} %get-tuple-element.279), channel_id=1, source_target_pairs={{0,3},{1,2},{2,1},{3,0},{4,7},{5,6},{6,5},{7,4},{8,11},{9,10},{10,... | collective-permute-start | bytes 884744 | tf_op jit(solution)/shard_map/ppermute | solution.py:783
  584.5 28.0 %collective-permute-start.42 = (f16[64,3072]{1,0:T(8,128)(2,1)S(1)}, f16[64,3072]{1,0:T(8,128)(2,1)S(1)}, u32[]{:S(2)}, u32[]{:S(2)}) collective-permute-start(f16[64,3072]{1,0:T(8,128)(2,1)S(1)} %copy-done.50), channel_id=1, source_target_pairs={{0,2},{1,3},{2,0},{3,1},{4,6},{5,7},{6,4},{7,5},{8,10},{9,11},{10,... | collective-permute-start | bytes 1179656 | tf_op jit(solution)/shard_map/ppermute | solution.py:783
  612.6 33.9 %collective-permute-start.45 = (f16[64,1536]{1,0:T(8,128)(2,1)S(1)}, f16[64,1536]{1,0:T(8,128)(2,1)S(1)}, u32[]{:S(2)}, u32[]{:S(2)}) collective-permute-start(f16[64,1536]{1,0:T(8,128)(2,1)S(1)} %copy-done.57), channel_id=1, source_target_pairs={{0,2},{1,3},{2,0},{3,1},{4,6},{5,7},{6,4},{7,5},{8,10},{9,11},{10,... | collective-permute-start | bytes 589832 | tf_op jit(solution)/shard_map/ppermute | solution.py:783
  624.5 37.4 %collective-permute-start.49 = (f16[64,1920]{1,0:T(8,128)(2,1)S(1)}, f16[64,1920]{1,0:T(8,128)(2,1)S(1)}, u32[]{:S(2)}, u32[]{:S(2)}) collective-permute-start(f16[64,1920]{1,0:T(8,128)(2,1)S(1)} %get-tuple-element.282), channel_id=1, source_target_pairs={{0,3},{1,2},{2,1},{3,0},{4,7},{5,6},{6,5},{7,4},{8,11},{9,10},{10,... | collective-permute-start | bytes 737288 | tf_op jit(solution)/shard_map/ppermute | solution.py:783
  626.2 35.7 %collective-permute-start.48 = (f16[64,1920]{1,0:T(8,128)(2,1)S(1)}, f16[64,1920]{1,0:T(8,128)(2,1)S(1)}, u32[]{:S(2)}, u32[]{:S(2)}) collective-permute-start(f16[64,1920]{1,0:T(8,128)(2,1)S(1)} %get-tuple-element.284), channel_id=1, source_target_pairs={{0,2},{1,3},{2,0},{3,1},{4,6},{5,7},{6,4},{7,5},{8,10},{9,11},{10,... | collective-permute-start | bytes 737288 | tf_op jit(solution)/shard_map/ppermute | solution.py:783
  (132 other events, 1650.6 us)
Sparse Core Ops, SparseCore 0:
  46.7 66.8 all-gather.3
  116.1 58.6 all-gather.5
  177.3 58.6 all-gather.7

commit v7 on v6

--- a/solution.py
+++ b/solution.py
@@ -619,25 +619,16 @@
     spread = head_onehot()
     wide = half * GW
     flows = dotf(flow_a[...], spread[:, :wide], NT) + dotf(flow_b[...], spread[:, wide:], NT)
-    top = half * GH
-    rise = (iota((HEADS, top), 0) == iota((HEADS, top), 1)).astype(f32)
-    fall = (iota((HEADS, HEADS - top), 0) == iota((HEADS, HEADS - top), 1) + top).astype(f32)
     times = jnp.zeros((1, HEADS), f32)
     decays = jnp.zeros((1, HEADS), f32)
     most = jnp.zeros((1, HEADS), f32)
     dstep_ref[...] = jnp.zeros_like(dstep_ref)
     for c in range(length // Q):
         rows = slice(c * Q, (c + 1) * Q)
-        ddelta = jnp.zeros((Q, HEADS), f32)
-        turned = dotf(rise, drow_a[:, rows]) + dotf(fall, drow_b[:, rows])
-        dcum = -dotf(eye, turned, NT)
-        for g in range(NG):
-            place = (iota((GH, HEADS), 0) + g * GH == iota((GH, HEADS), 1)).astype(f32)
-            one, two = (ddelta_a[g, rows, :], dcum_a[g, rows, :]) if g < half else (
-                ddelta_b[g - half, rows, :], dcum_b[g - half, rows, :]
-            )
-            ddelta = ddelta + dotf(one, place)
-            dcum = dcum + dotf(two, place)
+        turned = jnp.concatenate([drow_a[:, rows], drow_b[:, rows]], axis=0)
+        ddelta = jnp.concatenate([part[g, rows, :] for part in (ddelta_a, ddelta_b) for g in range(part.shape[0])], axis=1)
+        dcum = jnp.concatenate([part[g, rows, :] for part in (dcum_a, dcum_b) for g in range(part.shape[0])], axis=1)
+        dcum = dcum - dotf(eye, turned, NT)
         dcum = dcum + jnp.where(last, flows[c : c + 1, :], 0.0)
         x = step_ref[pl.ds(HALO + c * Q, Q), :HEADS] + par_ref[0:1, :]
         dlog = dotf(upper, dcum) * rate
@@ -863,7 +854,8 @@
         self.got = exchanged(self.payload, "dp", 2 << self.order[self.at])
         self.at += 1
         if self.total is None:
-            self.total = lax.dot_general(self.held, self.rhs, TOKENS, preferred_element_type=f32)
+            rhs = after(self.rhs, self.payload)
+            self.total = lax.dot_general(self.held, rhs, TOKENS, preferred_element_type=f32)
 
     def take(self, *earlier):
         got, self.power = decoded(after(self.got, earlier), self.power, self.rows)

time: 687 us -> 690 us (level)
  transfers between devices with their start and end apart: 56 -> 56, of which waited for: 20 -> 19; matrix products, arithmetic and copies ran while one was open for 31% -> 30% of each run, Pallas kernels for 15% -> 14%
where the time goes in v7:
time: 690 us; the launch traced here: 681 us
  waiting for transfers between devices  201 us (29%)
  Pallas kernels  129 us (19%)
  matrix products  97.1 us (14%)
  other arithmetic  92.5 us (13%)
  starting transfers between devices  85.6 us (12%)
  local copies, waits for them, and re-layouts  57 us (8%)
  between operations  18.9 us (3%)
    ppermute x44, waiting for transfers between devices, exchanged(): lax.ppermute(value, axis, [(i, i ^ by) for i in range(lax.axis_size(axis))])  132 us
    ppermute x44, starting transfers between devices, exchanged(): lax.ppermute(value, axis, [(i, i ^ by) for i in range(lax.axis_size(axis))])  57.6 us
    pallas_call x2, Pallas kernels, back_local(): pl.pallas_call(functools.partial(back_kernel, last == NG), grid=(groups,)...  43.4 us
    ppermute x9, waiting for transfers between devices, shifted(): return lax.ppermute(value, axis, pairs)  36.8 us
    all_gather x3, waiting for transfers between devices, gathered(): return lax.all_gather(value, 'dp', axis=0, tiled=True)  31.6 us
    ppermute x9, starting transfers between devices, shifted(): return lax.ppermute(value, axis, pairs)  27.4 us
    pallas_call x2, Pallas kernels, unconv(): pl.pallas_call(functools.partial(unconv_kernel, mixed), grid=(tiles,), in...  23.4 us
    pallas_call x1, Pallas kernels, gate(): pl.pallas_call(functools.partial(gate_kernel, block), grid_spec=pltpu.Pre...  22.7 us
  transfers between devices with their start and end apart: 56, of which 19 were waited for; matrix products, arithmetic and copies ran while one was open for 30% of the time, Pallas kernels for 14%

profile of v7, /device:TPU:0, one launch (start us, length us, event | category | flops | bytes accessed | tf_op | source)
XLA Modules:
  0.0 681.2 jit_solution(9282280909612646145)
XLA Ops:
  21.8 9.6 %collective-permute-done.1 = bf16[48,3456]{1,0:T(8,128)(2,1)S(1)} collective-permute-done((bf16[48,3456]{1,0:T(8,128)(2,1)S(1)}, bf16[48,3456]{1,0:T(8,128)(2,1)S(1)}, u32[]{:S(2)}, u32[]{:S(2)}) %collective-permute-start.1) | collective-permute-done | bytes 331808 | tf_op jit(solution)/shard_map/ppermute | solution.py:774
  32.1 11.0 %collective-permute-done.2 = bf16[48,3456]{1,0:T(8,128)(2,1)} collective-permute-done((bf16[48,3456]{1,0:T(8,128)(2,1)S(1)}, bf16[48,3456]{1,0:T(8,128)(2,1)}, u32[]{:S(2)}, u32[]{:S(2)}) %collective-permute-start.2) | collective-permute-done | bytes 331808 | tf_op jit(solution)/shard_map/ppermute | solution.py:774
  48.1 7.1 %collective-permute-start = (f32[16,1536]{1,0:T(8,128)}, f32[16,1536]{1,0:T(8,128)}, u32[]{:S(2)}, u32[]{:S(2)}) collective-permute-start(f32[16,1536]{1,0:T(8,128)} %pad_maximum_fusion.10), channel_id=1, source_target_pairs={{0,1},{1,2},{2,3},{4,5},{5,6},{6,7},{8,9},{9,10},{10,11},{12,13},{... | collective-permute-start | bytes 294920 | tf_op jit(solution)/shard_map/ppermute | solution.py:753
  113.7 12.4 %fusion.117.step_ref.xv_ref.xk_ref.x_ref = f32[520,3456]{1,0:T(8,128)} fusion(bf16[520,1536]{1,0:T(8,128)(2,1)} %copy-done.17, bf16[1536,3456]{1,0:T(8,128)(2,1)} %all-gather.4.cloned.1.call-done), kind=kOutput, calls=%fused_computation.343 | convolution fusion | flops 5520752640 | bytes 19402752 | tf_op jit(solution)/shard_map/dot_general | solution.py:1028
  131.4 12.4 %conv_state.1 = (f32[512,3072]{1,0:T(8,128)}, f32[512,256]{1,0:T(8,128)}, f32[128,3072]{1,0:T(8,128)}, bf16[128,3072]{1,0:T(8,128)(2,1)}) custom-call(f32[520,3456]{1,0:T(8,128)} %fusion.117.step_ref.xv_ref.xk_ref.x_ref, f32[520,3456]{1,0:T(8,128)} %fusion.117.step_ref.xv_ref.xk_ref.x_ref, f32[8,3328]{1,0:T(8,128)} %maximum_maximum_fusion.4.tv_ref.tk_ref.tap_ref, ...), custom_call_target="tpu_custom_call" | custom-call | flops 2000000000 | bytes 20000000 | tf_op jit(solution)/shard_map/conv_state/pallas_call | solution.py:221
  156.1 17.5 %local_out.1.y_ref = f32[512,3072]{1,0:T(8,128)} custom-call(f32[512,3072]{1,0:T(8,128)} %get-tuple-element.129.v_ref, f32[512,256]{1,0:T(8,128)} %get-tuple-element.130.kq_ref, f32[6,512,8]{2,1,0:T(8,128)} %get-tuple-element.131.delta_ref, f32[6,512,8]{2,1,0:T(8,128)} %get-tuple-element.132.cum_ref, f32[48,512]{1,0:T(8,128)} %get-tuple-element.133.cumt_ref, ...), custom_call_target="tpu_custom_call" | custom-call | flops 2000000000 | bytes 20000000 | tf_op jit(solution)/shard_map/local_out/pallas_call | solution.py:315
  183.2 12.0 %fusion.100.z_ref = f32[512,3072]{1,0:T(8,128)} fusion(bf16[1536,3072]{1,0:T(8,128)(2,1)} %all-gather.6.cloned.1.call-done, bf16[520,1536]{1,0:T(8,128)(2,1)S(1)} %copy-done.18), kind=kOutput, calls=%fused_computation.336 | convolution fusion | flops 4831838208 | bytes 17301504 | tf_op jit(solution)/shard_map/dot_general | solution.py:1037
  206.6 29.4 %all-gather.8.cloned.1.call-done = bf16[3072,1536]{1,0:T(8,128)(2,1)} async-done(((bf16[384,1536]{1,0:T(8,128)(2,1)}), bf16[3072,1536]{1,0:T(8,128)(2,1)}) %all-gather.8.cloned.1.call-update) | async-done | bytes 9437200 | tf_op jit(solution)/shard_map/all_gather | solution.py:760
  236.0 9.8 %convolution_bitcast_fusion.g_ref = f32[512,3072]{1,0:T(8,128)} fusion(bf16[3072,1536]{1,0:T(8,128)(2,1)} %all-gather.8.cloned.1.call-done, bf16[512,1536]{1,0:T(8,128)(2,1)} %get-tuple-element.126), kind=kOutput, calls=%fused_computation.5 | convolution fusion | flops 4831838208 | bytes 17301504 | tf_op jit(solution)/shard_map/dot_general | solution.py:1039
  245.8 22.7 %gate.1 = (bf16[512,3072]{1,0:T(8,128)(2,1)}, bf16[4,512,768]{2,1,0:T(8,128)(2,1)}, f32[512,3072]{1,0:T(8,128)}, bf16[528,3072]{1,0:T(8,128)(2,1)}, f32[128,3072...) custom-call(s32[2]{0:T(128)} %pad_add_fusion.at_ref, f32[512,3072]{1,0:T(8,128)} %local_out.1.y_ref, ...), custom_call_target="tpu_custom_call" | custom-call | flops 1000000000 | bytes 40000000 | tf_op jit(solution)/shard_map/gate/pallas_call | solution.py:408
  270.2 11.2 %fusion.118 = f32[528,1536]{1,0:T(8,128)} fusion(bf16[528,3072]{1,0:T(8,128)(2,1)} %broadcast_dynamic-update-slice_fusion, bf16[1536,3072]{1,0:T(8,128)(2,1)} %all-gather.6.cloned.1.call-done), kind=kOutput, calls=%fused_computation.344 | convolution fusion | flops 4982833152 | bytes 15925248 | tf_op jit(solution)/shard_map/dot_general | solution.py:1066
  283.6 6.7 convolution_add_fusion
  290.6 13.2 %collective-permute-done.15 = bf16[128,3072]{1,0:T(8,128)(2,1)S(1)} collective-permute-done((bf16[128,3072]{1,0:T(8,128)(2,1)S(1)}, bf16[128,3072]{1,0:T(8,128)(2,1)S(1)}, u32[]{:S(2)}, u32[]{:S(2)}) %collective-permute-start.15) | collective-permute-done | bytes 786464 | tf_op jit(solution)/shard_map/ppermute | solution.py:753
  312.7 12.0 %collective-permute-done.16 = bf16[128,3072]{1,0:T(8,128)(2,1)S(1)} collective-permute-done((bf16[128,3072]{1,0:T(8,128)(2,1)S(1)}, bf16[128,3072]{1,0:T(8,128)(2,1)S(1)}, u32[]{:S(2)}, u32[]{:S(2)}) %collective-permute-start.16) | collective-permute-done | bytes 786464 | tf_op jit(solution)/shard_map/ppermute | solution.py:753
  349.4 21.4 %back_first.1 = (f32[512,1536]{1,0:T(8,128)}, f32[512,256]{1,0:T(8,128)}, f32[512,128]{1,0:T(8,128)}, f32[3,512,8]{2,1,0:T(8,128)}, f32[3,512,8]{2,1,0:T(8,128)}, /*index=5*/f32[24,512]{1,0:T(8,128)}, f32[8,1536]{1,0:T(8,128)}) custom-call(f32[512,3072]{1,0:T(8,128)} %get-tuple-element.129.v_ref, f32[512,3072]{1,0:T(8,128)} %get-tuple-element.172.dy_ref, ...), custom_call_target="tpu_custom_call" | custom-call | flops 15000000512 | bytes 15000000 | tf_op jit(solution)/shard_map/back_first/pallas_call | solution.py:571
  376.3 20.3 %collective-permute-done.21 = f16[400,3072]{1,0:T(8,128)(2,1)} collective-permute-done((f16[400,3072]{1,0:T(8,128)(2,1)}, f16[400,3072]{1,0:T(8,128)(2,1)}, u32[]{:S(2)}, u32[]{:S(2)}) %collective-permute-start.21) | collective-permute-done | bytes 2457632 | tf_op jit(solution)/shard_map/ppermute | solution.py:774
  404.0 10.9 %shard_map.581 = (bf16[528,1536]{1,0:T(8,128)(2,1)}, f32[16,1536]{1,0:T(8,128)}, f32[8,1536]{1,0:T(8,128)}) custom-call(f32[520,3456]{1,0:T(8,128)} %fusion.117.step_ref.xv_ref.xk_ref.x_ref, f32[8,3328]{1,0:T(8,128)} %maximum_maximum_fusion.4.tv_ref.tk_ref.tap_ref, f32[3,512,128]{2,1,0:T(8,128)} %broadcast_in_dim.257.match_ref, ...), custom_call_target="tpu_custom_call" | custom-call | flops 100000000 | bytes 10000000 | tf_op jit(solution)/shard_map/pallas_call | solution.py:715
  438.0 18.9 %collective-permute-done.25 = f16[208,3072]{1,0:T(8,128)(2,1)S(1)} collective-permute-done((f16[208,3072]{1,0:T(8,128)(2,1)}, f16[208,3072]{1,0:T(8,128)(2,1)S(1)}, u32[]{:S(2)}, u32[]{:S(2)}) %collective-permute-start.25) | collective-permute-done | bytes 1277984 | tf_op jit(solution)/shard_map/ppermute | solution.py:774
  467.1 22.0 %back_second.1 = (f32[512,1536]{1,0:T(8,128)}, f32[512,256]{1,0:T(8,128)}, f32[512,128]{1,0:T(8,128)}, f32[3,512,8]{2,1,0:T(8,128)}, f32[3,512,8]{2,1,0:T(8,128)}, /*index=5*/f32[24,512]{1,0:T(8,128)}, f32[8,1536]{1,0:T(8,128)}) custom-call(f32[512,3072]{1,0:T(8,128)} %get-tuple-element.129.v_ref, f32[512,3072]{1,0:T(8,128)} %get-tuple-element.172.dy_ref, ...), custom_call_target="tpu_custom_call" | custom-call | flops 15000000512 | bytes 15000000 | tf_op jit(solution)/shard_map/back_second/pallas_call | solution.py:571
  498.2 12.5 %shard_map.582 = (bf16[528,1792]{1,0:T(8,128)(2,1)}, f32[16,1792]{1,0:T(8,128)}, f32[8,1792]{1,0:T(8,128)}) custom-call(f32[520,3456]{1,0:T(8,128)} %fusion.117.step_ref.xv_ref.xk_ref.x_ref, f32[8,3328]{1,0:T(8,128)} %maximum_maximum_fusion.4.tv_ref.tk_ref.tap_ref, f32[3,512,128]{2,1,0:T(8,128)} %broadcast_in_dim.257.match_ref, ...), custom_call_target="tpu_custom_call" | custom-call | flops 100000000 | bytes 10000000 | tf_op jit(solution)/shard_map/pallas_call | solution.py:715
  576.9 10.3 %collective-permute-done.37 = f16[208,1024]{1,0:T(8,128)(2,1)S(1)} collective-permute-done((f16[208,1024]{1,0:T(8,128)(2,1)S(1)}, f16[208,1024]{1,0:T(8,128)(2,1)S(1)}, u32[]{:S(2)}, u32[]{:S(2)}) %collective-permute-start.37) | collective-permute-done | bytes 426016 | tf_op jit(solution)/shard_map/ppermute | solution.py:774
  591.6 23.7 %collective-permute-done.42 = f16[64,3072]{1,0:T(8,128)(2,1)S(1)} collective-permute-done((f16[64,3072]{1,0:T(8,128)(2,1)S(1)}, f16[64,3072]{1,0:T(8,128)(2,1)S(1)}, u32[]{:S(2)}, u32[]{:S(2)}) %collective-permute-start.42) | collective-permute-done | bytes 393248 | tf_op jit(solution)/shard_map/ppermute | solution.py:774
  615.3 9.2 %collective-permute-start.45 = (f16[64,1536]{1,0:T(8,128)(2,1)S(1)}, f16[64,1536]{1,0:T(8,128)(2,1)S(1)}, u32[]{:S(2)}, u32[]{:S(2)}) collective-permute-start(f16[64,1536]{1,0:T(8,128)(2,1)S(1)} %copy-done.59), channel_id=1, source_target_pairs={{0,2},{1,3},{2,0},{3,1},{4,6},{5,7},{6,4},{7,5},{8,10},{9,11},{10,... | collective-permute-start | bytes 589832 | tf_op jit(solution)/shard_map/ppermute | solution.py:774
  629.0 20.2 %collective-permute-done.45 = f16[64,1536]{1,0:T(8,128)(2,1)S(1)} collective-permute-done((f16[64,1536]{1,0:T(8,128)(2,1)S(1)}, f16[64,1536]{1,0:T(8,128)(2,1)S(1)}, u32[]{:S(2)}, u32[]{:S(2)}) %collective-permute-start.45) | collective-permute-done | bytes 196640 | tf_op jit(solution)/shard_map/ppermute | solution.py:774
  (525 shorter events, 305.9 us)
Async XLA Ops:
  7.2 106.4 %all-gather.4.cloned.1.call-start = ((), (), s32[]{:S(2)}) async-start(), calls=%async_computation | async-start | bytes 11943936 | tf_op jit(solution)/shard_map/all_gather | solution.py:760
  17.2 25.9 %collective-permute-start.2 = (bf16[48,3456]{1,0:T(8,128)(2,1)S(1)}, bf16[48,3456]{1,0:T(8,128)(2,1)}, u32[]{:S(2)}, u32[]{:S(2)}) collective-permute-start(bf16[48,3456]{1,0:T(8,128)(2,1)S(1)} %concatenate.125), channel_id=1, source_target_pairs={{0,2},{1,3},{2,0},{3,1},{4,6},{5,7},{6,4},{7,5},{8,10},{9,11},{10,... | collective-permute-start | bytes 995336 | tf_op jit(solution)/shard_map/ppermute | solution.py:774
  46.6 128.2 %all-gather.6.cloned.1.call-start = ((), (), s32[]{:S(2)}) async-start(), calls=%async_computation.1 | async-start | bytes 10616832 | tf_op jit(solution)/shard_map/all_gather | solution.py:760
  74.3 28.3 %collective-permute-start.7 = (bf16[48,3072]{1,0:T(8,128)(2,1)S(1)}, bf16[48,3072]{1,0:T(8,128)(2,1)S(1)}, u32[]{:S(2)}, u32[]{:S(2)}) collective-permute-start(bf16[48,3072]{1,0:T(8,128)(2,1)S(1)} %slice.463), channel_id=1, source_target_pairs={{0,2},{1,3},{2,0},{3,1},{4,6},{5,7},{6,4},{7,5},{8,10},{9,11},{10,... | collective-permute-start | bytes 884744 | tf_op jit(solution)/shard_map/ppermute | solution.py:774
  104.8 131.2 %all-gather.8.cloned.1.call-start = ((), (), s32[]{:S(2)}) async-start(), calls=%async_computation.2 | async-start | bytes 10616832 | tf_op jit(solution)/shard_map/all_gather | solution.py:760
  106.5 37.3 %collective-permute-start.11 = (bf16[96,1536]{1,0:T(8,128)(2,1)S(1)}, bf16[96,1536]{1,0:T(8,128)(2,1)}, u32[]{:S(2)}, u32[]{:S(2)}) collective-permute-start(bf16[96,1536]{1,0:T(8,128)(2,1)S(1)} %convert_element_type.281), channel_id=1, source_target_pairs={{0,3},{1,2},{2,1},{3,0},{4,7},{5,6},{6,5},{7,4},{8,11},{9,10},{10,... | collective-permute-start | bytes 884744 | tf_op jit(solution)/shard_map/ppermute | solution.py:774
  107.7 36.1 %collective-permute-start.10 = (bf16[96,1536]{1,0:T(8,128)(2,1)S(1)}, bf16[96,1536]{1,0:T(8,128)(2,1)}, u32[]{:S(2)}, u32[]{:S(2)}) collective-permute-start(bf16[96,1536]{1,0:T(8,128)(2,1)S(1)} %convert_element_type.281), channel_id=1, source_target_pairs={{0,2},{1,3},{2,0},{3,1},{4,6},{5,7},{6,4},{7,5},{8,10},{9,11},{10,... | collective-permute-start | bytes 884744 | tf_op jit(solution)/shard_map/ppermute | solution.py:774
  107.7 36.1 %collective-permute-start.9 = (bf16[96,1536]{1,0:T(8,128)(2,1)S(1)}, bf16[96,1536]{1,0:T(8,128)(2,1)}, u32[]{:S(2)}, u32[]{:S(2)}) collective-permute-start(bf16[96,1536]{1,0:T(8,128)(2,1)S(1)} %convert_element_type.281), channel_id=1, source_target_pairs={{0,1},{1,0},{2,3},{3,2},{4,5},{5,4},{6,7},{7,6},{8,9},{9,8},{10,11... | collective-permute-start | bytes 884744 | tf_op jit(solution)/shard_map/ppermute | solution.py:774
  149.0 28.5 %collective-permute-start.12 = (bf16[128,3072]{1,0:T(8,128)(2,1)}, bf16[128,3072]{1,0:T(8,128)(2,1)}, u32[]{:S(2)}, u32[]{:S(2)}) collective-permute-start(bf16[128,3072]{1,0:T(8,128)(2,1)} %get-tuple-element.148), channel_id=1, source_target_pairs={{0,1},{1,2},{2,3},{4,5},{5,6},{6,7},{8,9},{9,10},{10,11},{12,13},{... | collective-permute-start | bytes 2359304 | tf_op jit(solution)/shard_map/ppermute | solution.py:753
  201.3 44.5 %collective-permute-start.14 = (bf16[128,3072]{1,0:T(8,128)(2,1)}, bf16[128,3072]{1,0:T(8,128)(2,1)}, u32[]{:S(2)}, u32[]{:S(2)}) collective-permute-start(bf16[128,3072]{1,0:T(8,128)(2,1)} %add_convert_fusion.2), channel_id=1, source_target_pairs={{0,1},{1,2},{2,3},{4,5},{5,6},{6,7},{8,9},{9,10},{10,11},{12,13},{... | collective-permute-start | bytes 2359304 | tf_op jit(solution)/shard_map/ppermute | solution.py:753
  281.4 51.5 %collective-permute-start.19 = (bf16[528,3072]{1,0:T(8,128)(2,1)S(1)}, bf16[528,3072]{1,0:T(8,128)(2,1)S(1)}, u32[]{:S(2)}, u32[]{:S(2)}) collective-permute-start(bf16[528,3072]{1,0:T(8,128)(2,1)S(1)} %copy-done.33), channel_id=1, source_target_pairs={{0,4},{4,0},{8,12},{12,8},{16,20},{20,16},{24,28},{28,24},{1,5},{5... | collective-permute-start | bytes 9732104 | tf_op jit(solution)/shard_map/ppermute | solution.py:774
  311.2 59.6 %collective-permute-start.20 = (f16[768,1536]{1,0:T(8,128)(2,1)}, f16[768,1536]{1,0:T(8,128)(2,1)}, u32[]{:S(2)}, u32[]{:S(2)}) collective-permute-start(f16[768,1536]{1,0:T(8,128)(2,1)} %multiply_convert_fusion), channel_id=1, source_target_pairs={{0,8},{4,12},{8,0},{12,4},{16,24},{20,28},{24,16},{28,20},{1,9},{5... | collective-permute-start | bytes 7077896 | tf_op jit(solution)/shard_map/ppermute | solution.py:774
  342.3 54.3 %collective-permute-start.21 = (f16[400,3072]{1,0:T(8,128)(2,1)}, f16[400,3072]{1,0:T(8,128)(2,1)}, u32[]{:S(2)}, u32[]{:S(2)}) collective-permute-start(f16[400,3072]{1,0:T(8,128)(2,1)} %select_convert_fusion), channel_id=1, source_target_pairs={{0,16},{4,20},{8,24},{12,28},{16,0},{20,4},{24,8},{28,12},{1,17},{... | collective-permute-start | bytes 7372808 | tf_op jit(solution)/shard_map/ppermute | solution.py:774
  424.6 32.8 %collective-permute-start.24 = (f16[384,1536]{1,0:T(8,128)(2,1)}, f16[384,1536]{1,0:T(8,128)(2,1)S(1)}, u32[]{:S(2)}, u32[]{:S(2)}) collective-permute-start(f16[384,1536]{1,0:T(8,128)(2,1)} %fusion.6), channel_id=1, source_target_pairs={{0,16},{4,20},{8,24},{12,28},{16,0},{20,4},{24,8},{28,12},{1,17},{... | collective-permute-start | bytes 3538952 | tf_op jit(solution)/shard_map/ppermute | solution.py:774
  425.8 31.2 %collective-permute-start.25 = (f16[208,3072]{1,0:T(8,128)(2,1)}, f16[208,3072]{1,0:T(8,128)(2,1)S(1)}, u32[]{:S(2)}, u32[]{:S(2)}) collective-permute-start(f16[208,3072]{1,0:T(8,128)(2,1)} %fusion.5), channel_id=1, source_target_pairs={{0,8},{4,12},{8,0},{12,4},{16,24},{20,28},{24,16},{28,20},{1,9},{5... | collective-permute-start | bytes 3833864 | tf_op jit(solution)/shard_map/ppermute | solution.py:774
  434.3 59.3 %collective-permute-start.26 = (f16[400,768]{1,0:T(8,128)(2,1)}, f16[400,768]{1,0:T(8,128)(2,1)S(1)}, u32[]{:S(2)}, u32[]{:S(2)}) collective-permute-start(f16[400,768]{1,0:T(8,128)(2,1)} %fusion.22), channel_id=1, source_target_pairs={{0,8},{4,12},{8,0},{12,4},{16,24},{20,28},{24,16},{28,20},{1,9},{5... | collective-permute-start | bytes 1843208 | tf_op jit(solution)/shard_map/ppermute | solution.py:774
  437.0 56.6 %collective-permute-start.27 = (f16[400,768]{1,0:T(8,128)(2,1)}, f16[400,768]{1,0:T(8,128)(2,1)}, u32[]{:S(2)}, u32[]{:S(2)}) collective-permute-start(f16[400,768]{1,0:T(8,128)(2,1)} %fusion.21), channel_id=1, source_target_pairs={{0,16},{4,20},{8,24},{12,28},{16,0},{20,4},{24,8},{28,12},{1,17},{... | collective-permute-start | bytes 1843208 | tf_op jit(solution)/shard_map/ppermute | solution.py:774
  462.9 161.6 %collective-permute-start.50 = (f16[96,1536]{1,0:T(8,128)(2,1)}, f16[96,1536]{1,0:T(8,128)(2,1)}, u32[]{:S(2)}, u32[]{:S(2)}) collective-permute-start(f16[96,1536]{1,0:T(8,128)(2,1)} %get-tuple-element.295), channel_id=1, source_target_pairs={{0,1},{1,0},{2,3},{3,2},{4,5},{5,4},{6,7},{7,6},{8,9},{9,8},{10,11... | collective-permute-start | bytes 884744 | tf_op jit(solution)/shard_map/ppermute | solution.py:774
  464.9 161.3 %collective-permute-start.51 = (f16[96,1536]{1,0:T(8,128)(2,1)}, f16[96,1536]{1,0:T(8,128)(2,1)}, u32[]{:S(2)}, u32[]{:S(2)}) collective-permute-start(f16[96,1536]{1,0:T(8,128)(2,1)} %get-tuple-element.294), channel_id=1, source_target_pairs={{0,2},{1,3},{2,0},{3,1},{4,6},{5,7},{6,4},{7,5},{8,10},{9,11},{10,... | collective-permute-start | bytes 884744 | tf_op jit(solution)/shard_map/ppermute | solution.py:774
  524.9 102.4 %collective-permute-start.52 = (f16[96,1536]{1,0:T(8,128)(2,1)}, f16[96,1536]{1,0:T(8,128)(2,1)}, u32[]{:S(2)}, u32[]{:S(2)}) collective-permute-start(f16[96,1536]{1,0:T(8,128)(2,1)} %get-tuple-element.293), channel_id=1, source_target_pairs={{0,3},{1,2},{2,1},{3,0},{4,7},{5,6},{6,5},{7,4},{8,11},{9,10},{10,... | collective-permute-start | bytes 884744 | tf_op jit(solution)/shard_map/ppermute | solution.py:774
  587.2 28.0 %collective-permute-start.42 = (f16[64,3072]{1,0:T(8,128)(2,1)S(1)}, f16[64,3072]{1,0:T(8,128)(2,1)S(1)}, u32[]{:S(2)}, u32[]{:S(2)}) collective-permute-start(f16[64,3072]{1,0:T(8,128)(2,1)S(1)} %copy-done.52), channel_id=1, source_target_pairs={{0,2},{1,3},{2,0},{3,1},{4,6},{5,7},{6,4},{7,5},{8,10},{9,11},{10,... | collective-permute-start | bytes 1179656 | tf_op jit(solution)/shard_map/ppermute | solution.py:774
  615.3 33.9 %collective-permute-start.45 = (f16[64,1536]{1,0:T(8,128)(2,1)S(1)}, f16[64,1536]{1,0:T(8,128)(2,1)S(1)}, u32[]{:S(2)}, u32[]{:S(2)}) collective-permute-start(f16[64,1536]{1,0:T(8,128)(2,1)S(1)} %copy-done.59), channel_id=1, source_target_pairs={{0,2},{1,3},{2,0},{3,1},{4,6},{5,7},{6,4},{7,5},{8,10},{9,11},{10,... | collective-permute-start | bytes 589832 | tf_op jit(solution)/shard_map/ppermute | solution.py:774
  627.2 37.4 %collective-permute-start.49 = (f16[64,1920]{1,0:T(8,128)(2,1)S(1)}, f16[64,1920]{1,0:T(8,128)(2,1)S(1)}, u32[]{:S(2)}, u32[]{:S(2)}) collective-permute-start(f16[64,1920]{1,0:T(8,128)(2,1)S(1)} %get-tuple-element.296), channel_id=1, source_target_pairs={{0,3},{1,2},{2,1},{3,0},{4,7},{5,6},{6,5},{7,4},{8,11},{9,10},{10,... | collective-permute-start | bytes 737288 | tf_op jit(solution)/shard_map/ppermute | solution.py:774
  629.0 35.6 %collective-permute-start.48 = (f16[64,1920]{1,0:T(8,128)(2,1)S(1)}, f16[64,1920]{1,0:T(8,128)(2,1)S(1)}, u32[]{:S(2)}, u32[]{:S(2)}) collective-permute-start(f16[64,1920]{1,0:T(8,128)(2,1)S(1)} %get-tuple-element.298), channel_id=1, source_target_pairs={{0,2},{1,3},{2,0},{3,1},{4,6},{5,7},{6,4},{7,5},{8,10},{9,11},{10,... | collective-permute-start | bytes 737288 | tf_op jit(solution)/shard_map/ppermute | solution.py:774
  (136 other events, 1690.3 us)
Sparse Core Ops, SparseCore 0:
  46.7 66.8 all-gather.3
  116.1 58.6 all-gather.5
  177.3 58.6 all-gather.7
